TPU v7x, 128 devices: a whole 4x4x4 slice. The times are simulated.
128 devices in a mesh: rep: 32 (over y, z, x_lo), grp: 4 (over x_hi, core).
Axes of the slice: x: 4 (x_hi: 2, x_lo: 2; x = x_hi * 2 + x_lo), y: 4, z: 4, core: 2. Of those that a mesh axis runs over, the one named last changes fastest.
Arguments:
- tokens: bfloat16 [64, 1024, 768], P('rep', 'grp'), may hold values from -6 to 6
- segment: int32 [64, 1024], P('rep'), may hold values from 0 to 1, as said below
- piece_start: int32 [64, 1024], P('rep'), may hold values from 0 to 1023, as said below
- w_query: bfloat16 [768, 768], P('grp'), may hold values from -0.21875 to 0.21875
- w_key: bfloat16 [768, 768], P('grp'), may hold values from -0.21875 to 0.21875
- w_value: bfloat16 [768, 768], P('grp'), may hold values from -0.21875 to 0.21875
- w_out: bfloat16 [768, 768], P('grp'), may hold values from -3.5 to 3.5
- w_gate: bfloat16 [768, 3072], P('grp'), may hold values from -0.21875 to 0.21875
- w_up: bfloat16 [768, 3072], P('grp'), may hold values from -0.21875 to 0.21875
- w_down: bfloat16 [3072, 768], P('grp'), may hold values from -0.109375 to 0.109375
- cotangent: bfloat16 [64, 1024, 768], P('rep', 'grp'), may hold values from -6 to 6
Outputs:
- output: bfloat16 [64, 1024, 768], P('rep', 'grp')
- grad_tokens: bfloat16 [64, 1024, 768], P('rep', 'grp')
- grad_query: float32 [768, 768], P('grp')
- grad_key: float32 [768, 768], P('grp')
- grad_value: float32 [768, 768], P('grp')
- grad_out: float32 [768, 768], P('grp')
- grad_gate: float32 [768, 3072], P('grp')
- grad_up: float32 [768, 3072], P('grp')
- grad_down: float32 [3072, 768], P('grp')
Inputs may be any that keep to these rules, and one draw needn't show every extreme that they name: `segment`: along a sequence the numbers start at 0, never fall, rise by one at a time, and rise only at the first position of a picture piece. `piece_start`: each sequence holds 2 picture pieces of 256 positions, the k-th lying within positions k * (512) to (k + 1) * 512 - 1; a piece's positions hold its first position, all other positions their own.
All inputs are finite; a program needn't handle non-finite values.
Results may differ from a plain program's by a relative error of at most 0.029.
Values may be sent and summed in bfloat16 or wider, within the bound.
No kernel may reach another device: no remote copies, remote signals or barrier semaphores. Data moves between devices by JAX's collectives and lax.ppermute only.
A program may use at most 256 MiB of HBM per device.

v0:
```python
import jax
import jax.numpy as jnp
from jax import lax
from jax.sharding import Mesh
from jax.sharding import PartitionSpec as P
from jax.experimental import pallas as pl
from jax.experimental.pallas import tpu as pltpu

HEADS = 12
HDIM = 64
REP = ("y", "z", "xl")
GRP = ("xh", "c")


def layer_norm(hidden):
    centred = hidden - jnp.mean(hidden, axis=-1, keepdims=True)
    spread = jnp.mean(centred * centred, axis=-1, keepdims=True)
    return centred * lax.rsqrt(spread + 1e-05)


def rotate(heads, cosine, sine):
    half = heads.shape[-1] // 2
    first = heads[..., :half]
    second = heads[..., half:]
    return jnp.concatenate(
        [first * cosine - second * sine, second * cosine + first * sine], axis=-1
    )


def gated(gate, upper):
    return gate / (1.0 + jnp.exp(-gate)) * upper


def matmul(left, right):
    return jnp.dot(left, right, preferred_element_type=jnp.float32)


def contract_rows(left, right):
    return lax.dot_general(
        left, right, (((0,), (0,)), ((), ())), preferred_element_type=jnp.float32
    )


def contract_cols(left, right):
    return lax.dot_general(
        left, right, (((1,), (1,)), ((), ())), preferred_element_type=jnp.float32
    )


def allowed_mask(rq_ref, sq_ref, pq_ref, sk_ref, pk_ref, shape):
    cols = lax.broadcasted_iota(jnp.int32, shape, 1)
    return (sq_ref[...] == sk_ref[...]) & ((cols <= rq_ref[...]) | (pq_ref[...] == pk_ref[...]))


def attention_forward_kernel(q_ref, k_ref, v_ref, rq_ref, sq_ref, pq_ref, sk_ref, pk_ref, o_ref, lse_ref):
    queries = q_ref.shape[0]
    keys = k_ref.shape[0]
    allowed = allowed_mask(rq_ref, sq_ref, pq_ref, sk_ref, pk_ref, (queries, keys))
    scale = HDIM ** (-0.5)
    for h in range(q_ref.shape[1] // HDIM):
        cols = slice(h * HDIM, (h + 1) * HDIM)
        raw = lax.dot_general(
            q_ref[:, cols], k_ref[:, cols], (((1,), (1,)), ((), ())),
            preferred_element_type=jnp.float32,
        )
        scores = jnp.where(allowed, raw * scale, -1e30)
        highest = jnp.max(scores, axis=1, keepdims=True)
        expd = jnp.exp(scores - highest)
        total = jnp.sum(expd, axis=1, keepdims=True)
        probs_low = (expd / total).astype(jnp.bfloat16)
        o_ref[:, cols] = jnp.dot(probs_low, v_ref[:, cols], preferred_element_type=jnp.float32)
        lse_ref[:, h:h + 1] = highest + jnp.log(total)


def attention_backward_kernel(
    q_ref, k_ref, v_ref, do_ref, lse_ref, rq_ref, sq_ref, pq_ref, sk_ref, pk_ref, dq_ref, dk_ref, dv_ref
):
    queries = q_ref.shape[0]
    keys = k_ref.shape[0]
    allowed = allowed_mask(rq_ref, sq_ref, pq_ref, sk_ref, pk_ref, (queries, keys))
    scale = HDIM ** (-0.5)
    for h in range(q_ref.shape[1] // HDIM):
        cols = slice(h * HDIM, (h + 1) * HDIM)
        q = q_ref[:, cols]
        k = k_ref[:, cols]
        v = v_ref[:, cols]
        do = do_ref[:, cols]
        raw = lax.dot_general(q, k, (((1,), (1,)), ((), ())), preferred_element_type=jnp.float32)
        scores = jnp.where(allowed, raw * scale, -1e30)
        probs = jnp.exp(scores - lse_ref[:, h:h + 1])
        grad_probs = lax.dot_general(do, v, (((1,), (1,)), ((), ())), preferred_element_type=jnp.float32)
        inner = jnp.sum(probs * grad_probs, axis=1, keepdims=True)
        grad_raw = (probs * (grad_probs - inner) * scale).astype(jnp.bfloat16)
        dq_ref[:, cols] = jnp.dot(grad_raw, k, preferred_element_type=jnp.float32)
        dk_ref[:, cols] = lax.dot_general(
            grad_raw, q, (((0,), (0,)), ((), ())), preferred_element_type=jnp.float32
        )
        dv_ref[:, cols] = lax.dot_general(
            probs.astype(jnp.bfloat16), do, (((0,), (0,)), ((), ())), preferred_element_type=jnp.float32
        )


def mask_specs(queries, keys):
    column = pl.BlockSpec((queries, 1), lambda i: (0, 0))
    row = pl.BlockSpec((1, keys), lambda i: (0, 0))
    return [column, column, column, row, row]


def attention_forward(q, kv, masks):
    queries, width = q.shape
    keys = kv.shape[0]
    block = 2 * HDIM
    pairs = width // block
    return pl.pallas_call(
        attention_forward_kernel,
        grid=(pairs,),
        in_specs=[
            pl.BlockSpec((queries, block), lambda i: (0, i)),
            pl.BlockSpec((keys, block), lambda i: (0, i)),
            pl.BlockSpec((keys, block), lambda i, p=pairs: (0, i + p)),
        ] + mask_specs(queries, keys),
        out_specs=[
            pl.BlockSpec((queries, block), lambda i: (0, i)),
            pl.BlockSpec((None, queries, 2), lambda i: (i, 0, 0)),
        ],
        out_shape=[
            jax.ShapeDtypeStruct((queries, width), jnp.float32),
            jax.ShapeDtypeStruct((pairs, queries, 2), jnp.float32),
        ],
        compiler_params=pltpu.CompilerParams(dimension_semantics=("arbitrary",)),
        cost_estimate=pl.CostEstimate(
            flops=4 * queries * keys * width, transcendentals=queries * keys * HEADS,
            bytes_accessed=2 * (queries + 2 * keys) * width + 4 * queries * width,
        ),
    )(q, kv, kv, *masks)


def attention_backward(q, kv, do, lse, masks):
    queries, width = q.shape
    keys = kv.shape[0]
    block = 2 * HDIM
    pairs = width // block
    return pl.pallas_call(
        attention_backward_kernel,
        grid=(pairs,),
        in_specs=[
            pl.BlockSpec((queries, block), lambda i: (0, i)),
            pl.BlockSpec((keys, block), lambda i: (0, i)),
            pl.BlockSpec((keys, block), lambda i, p=pairs: (0, i + p)),
            pl.BlockSpec((queries, block), lambda i: (0, i)),
            pl.BlockSpec((None, queries, 2), lambda i: (i, 0, 0)),
        ] + mask_specs(queries, keys),
        out_specs=[
            pl.BlockSpec((queries, block), lambda i: (0, i)),
            pl.BlockSpec((keys, block), lambda i: (0, i)),
            pl.BlockSpec((keys, block), lambda i: (0, i)),
        ],
        out_shape=[
            jax.ShapeDtypeStruct((queries, width), jnp.float32),
            jax.ShapeDtypeStruct((keys, width), jnp.float32),
            jax.ShapeDtypeStruct((keys, width), jnp.float32),
        ],
        compiler_params=pltpu.CompilerParams(dimension_semantics=("arbitrary",)),
        cost_estimate=pl.CostEstimate(
            flops=10 * queries * keys * width, transcendentals=queries * keys * HEADS,
            bytes_accessed=2 * (2 * queries + 2 * keys) * width + 4 * (queries + 2 * keys) * width,
        ),
    )(q, kv, kv, do, lse, *masks)


def shift(x, axis, n, step):
    return lax.ppermute(x, axis, [(i, (i + step) % n) for i in range(n)])


def place(buf, piece, index, dim):
    start = [0] * buf.ndim
    start[dim] = index * piece.shape[dim]
    return lax.dynamic_update_slice(buf, piece, start)


def ring_gather(piece, axis, n, dim, direct=False):
    if n == 1:
        return piece
    me = lax.axis_index(axis)
    shape = list(piece.shape)
    shape[dim] *= n
    buf = place(jnp.zeros(shape, piece.dtype), piece, me, dim)
    if n == 2 or direct:
        for k in range(1, n):
            buf = place(buf, shift(piece, axis, n, k), (me - k) % n, dim)
        return buf
    back = piece
    ahead = piece
    for step in range(1, n // 2 + 1):
        if step < n - step:
            back = shift(back, axis, n, 1)
            ahead = shift(ahead, axis, n, -1)
            buf = place(buf, back, (me - step) % n, dim)
            buf = place(buf, ahead, (me + step) % n, dim)
        else:
            half = piece.shape[dim] // 2
            first = shift(lax.slice_in_dim(back, 0, half, axis=dim), axis, n, 1)
            second = shift(lax.slice_in_dim(ahead, half, piece.shape[dim], axis=dim), axis, n, -1)
            buf = place(buf, jnp.concatenate([first, second], axis=dim), (me + step) % n, dim)
    return buf


def ring_reduce(x, axis, n, dim, hdim, direct=False):
    if n == 1:
        return x
    me = lax.axis_index(axis)
    size = x.shape[dim] // n

    def chunk(k):
        return lax.dynamic_slice_in_dim(x, (k % n) * size, size, axis=dim)

    def low(v):
        return v.astype(jnp.bfloat16)

    if n == 2 or direct:
        acc = chunk(me)
        for k in range(1, n):
            acc = acc + shift(low(chunk(me + k)), axis, n, k).astype(jnp.float32)
        return acc
    assert n == 4
    half = x.shape[hdim] // 2

    def part(k, which):
        c = chunk(k)
        return lax.slice_in_dim(c, 0, half, axis=hdim) if which == 0 else lax.slice_in_dim(
            c, half, c.shape[hdim], axis=hdim
        )

    from_ahead = shift(low(jnp.stack([part(me - 2, 0), part(me - 1, 1)])), axis, n, -1)
    from_back = shift(low(jnp.stack([part(me + 2, 1), part(me + 1, 0)])), axis, n, 1)
    relay_ahead = shift(low(from_ahead[0].astype(jnp.float32) + part(me - 1, 0)), axis, n, -1)
    relay_back = shift(low(from_back[0].astype(jnp.float32) + part(me + 1, 1)), axis, n, 1)
    first = part(me, 0) + from_back[1].astype(jnp.float32) + relay_ahead.astype(jnp.float32)
    second = part(me, 1) + from_ahead[1].astype(jnp.float32) + relay_back.astype(jnp.float32)
    return jnp.concatenate([first, second], axis=hdim)


def cross(x):
    return lax.ppermute(x, ("xl", "xh"), [(i, 3 - i) for i in range(4)])


def swap_core(x):
    return lax.ppermute(x, "c", [(0, 1), (1, 0)])


def absolute(parts, rows):
    g = lax.axis_index("xh") * 2 + lax.axis_index("c")
    buf = jnp.zeros((4 * rows,) + parts[0].shape[1:], parts[0].dtype)
    for j, part in enumerate(parts):
        buf = place(buf, part, jnp.bitwise_xor(g, j), 0)
    return buf


def gather_group(own, axis, n, direct):
    size = own.shape[0] // n
    me = lax.axis_index(axis)
    mine = lax.dynamic_slice_in_dim(own, me * size, size, axis=0)
    other = ring_gather(cross(mine), axis, n, 0, direct)
    partner = swap_core(jnp.concatenate([own, other]))
    rows = own.shape[0]
    return [own, partner[:rows], other, partner[rows:]]


def gather_weights(group, axis, sizes, direct):
    parts = gather_group(jnp.concatenate(group), axis, sizes[axis], direct)
    out = []
    start = 0
    for s in group:
        rows = s.shape[0]
        out.append(absolute([p[start:start + rows] for p in parts], rows))
        start += rows
    return out


def reduce_group(grads, sizes, direct):
    g = lax.axis_index("xh") * 2 + lax.axis_index("c")

    def shard(w, j):
        rows = w.shape[0] // 4
        return lax.dynamic_slice_in_dim(w, jnp.bitwise_xor(g, j) * rows, rows, axis=0)

    send = jnp.concatenate([shard(w, 1) for w in grads] + [shard(w, 3) for w in grads])
    got = swap_core(send.astype(jnp.bfloat16)).astype(jnp.float32)
    total = got.shape[0] // 2
    own = jnp.concatenate([shard(w, 0) for w in grads]) + got[:total]
    oth = jnp.concatenate([shard(w, 2) for w in grads]) + got[total:]
    pair = jnp.stack([own, oth])
    pair = ring_reduce(pair, "y", sizes["y"], 1, 2, direct)
    pair = ring_reduce(pair, "z", sizes["z"], 1, 2, direct)
    low = pair.astype(jnp.bfloat16)
    mine = (
        pair[0]
        + lax.ppermute(low[0], "xl", [(0, 1), (1, 0)]).astype(jnp.float32)
        + cross(low[1]).astype(jnp.float32)
        + lax.ppermute(low[1], "xh", [(0, 1), (1, 0)]).astype(jnp.float32)
    )
    full = ring_gather(mine.astype(jnp.bfloat16), "z", sizes["z"], 0, direct)
    full = ring_gather(full, "y", sizes["y"], 0, direct)
    out = []
    start = 0
    for w in grads:
        rows = w.shape[0] // 4
        out.append(full[start:start + rows].astype(jnp.float32))
        start += rows
    return out


def to_sequence(x):
    xh = lax.axis_index("xh")
    c = lax.axis_index("c")
    first = lax.ppermute(lax.dynamic_index_in_dim(x, c, 0, False), GRP, [(0, 0), (1, 2), (2, 1), (3, 3)])
    second = lax.ppermute(lax.dynamic_index_in_dim(x, 1 - c, 0, False), GRP, [(0, 2), (1, 0), (2, 3), (3, 1)])
    return jnp.where(xh == 0, jnp.concatenate([first, second]), jnp.concatenate([second, first]))


def from_sequence(x):
    xh = lax.axis_index("xh")
    c = lax.axis_index("c")
    length = x.shape[0] // 2
    first = jnp.where(xh == 0, x[:length], x[length:])
    second = jnp.where(xh == 0, x[length:], x[:length])
    first = lax.ppermute(first, GRP, [(0, 0), (1, 2), (2, 1), (3, 3)])
    second = lax.ppermute(second, GRP, [(2, 0), (0, 1), (3, 2), (1, 3)])
    return jnp.where(c == 0, jnp.stack([first, second]), jnp.stack([second, first]))


def body(
    tokens, segment, piece_start, w_query, w_key, w_value, w_out, w_gate, w_up, w_down, cotangent
):
    sizes = {"y": lax.axis_size("y"), "z": lax.axis_size("z"), "xl": lax.axis_size("xl")}
    width = tokens.shape[2]
    local_length = tokens.shape[1] * 2
    full_length = segment.shape[1]
    head_count = HEADS
    head_size = HDIM
    scale = head_size ** (-0.5)
    xh = lax.axis_index("xh")
    c = lax.axis_index("c")
    first_row = c * local_length
    rows = first_row + jnp.arange(local_length, dtype=jnp.int32)
    columns = jnp.arange(full_length, dtype=jnp.int32)
    inverse = 10000.0 ** (-jnp.arange(0, head_size, 2).astype(jnp.float32) / head_size)
    angles = rows.astype(jnp.float32)[:, None] * inverse[None, :]
    cosine = jnp.cos(angles)[:, None, :]
    sine = jnp.sin(angles)[:, None, :]

    query_weight, key_weight, value_weight = gather_weights(
        (w_query, w_key, w_value), "y", sizes, True
    )

    both_in = to_sequence(jnp.concatenate([tokens, cotangent], axis=2))
    hidden = both_in[:, :width].astype(jnp.float32)
    grad_result = both_in[:, width:]
    seg_row = lax.dynamic_index_in_dim(segment, xh, 0, False)
    start_row = lax.dynamic_index_in_dim(piece_start, xh, 0, False)

    def swap_halves(mine):
        other = lax.ppermute(mine, "c", [(0, 1), (1, 0)])
        return jnp.where(c == 0, jnp.concatenate([mine, other]), jnp.concatenate([other, mine]))

    normed, norm_one_back = jax.vjp(layer_norm, hidden)
    normed_low = normed.astype(jnp.bfloat16)
    query_heads = rotate(
        matmul(normed_low, query_weight).reshape(local_length, head_count, head_size),
        cosine,
        sine,
    ).astype(jnp.bfloat16)
    keys = (
        rotate(
            matmul(normed_low, key_weight).reshape(local_length, head_count, head_size),
            cosine,
            sine,
        )
        .reshape(local_length, width)
        .astype(jnp.bfloat16)
    )
    values = matmul(normed_low, value_weight).astype(jnp.bfloat16)
    w_out, w_down, w_gate, w_up, values = lax.optimization_barrier((w_out, w_down, w_gate, w_up, values))
    out_weight, down_weight = gather_weights((w_out, w_down), "z", sizes, False)
    gate_weight, up_weight = gather_weights((w_gate, w_up), "y", sizes, False)
    both = swap_halves(jnp.concatenate([keys, values], axis=1))
    seg_local = lax.dynamic_slice_in_dim(seg_row, first_row, local_length)
    start_local = lax.dynamic_slice_in_dim(start_row, first_row, local_length)
    masks = (
        rows[:, None],
        seg_local[:, None],
        start_local[:, None],
        seg_row[None, :],
        start_row[None, :],
    )
    query_flat = query_heads.reshape(local_length, width)
    mixed, log_total = attention_forward(query_flat, both, masks)
    mixed_low = mixed.reshape(local_length, width).astype(jnp.bfloat16)
    after = hidden + matmul(mixed_low, out_weight)
    normed_two, norm_two_back = jax.vjp(layer_norm, after)
    normed_two_low = normed_two.astype(jnp.bfloat16)
    gate = matmul(normed_two_low, gate_weight)
    upper = matmul(normed_two_low, up_weight)
    active, gate_back = jax.vjp(gated, gate, upper)
    active_low = active.astype(jnp.bfloat16)
    result = after + matmul(active_low, down_weight)
    result_low = result.astype(jnp.bfloat16)

    grads = [None] * 7
    grads[6] = contract_rows(active_low, grad_result)
    grad_active = contract_cols(grad_result, down_weight)
    grad_gate, grad_upper = gate_back(grad_active)
    gate_low = grad_gate.astype(jnp.bfloat16)
    upper_low = grad_upper.astype(jnp.bfloat16)
    grads[4] = contract_rows(normed_two_low, gate_low)
    grads[5] = contract_rows(normed_two_low, upper_low)
    grad_normed_two = contract_cols(gate_low, gate_weight) + contract_cols(upper_low, up_weight)
    grad_after = grad_result.astype(jnp.float32) + norm_two_back(grad_normed_two)[0]
    after_low = grad_after.astype(jnp.bfloat16)
    grads[3] = contract_rows(mixed_low, after_low)
    grad_mixed = (
        contract_cols(after_low, out_weight)
        .astype(jnp.bfloat16)
        .reshape(local_length, head_count, head_size)
    )
    grad_query, grad_keys, grad_values = attention_backward(
        query_flat, both, grad_mixed.reshape(local_length, width), log_total, masks
    )
    grad_query = grad_query.reshape(local_length, head_count, head_size)
    grad_kv = jnp.concatenate([grad_keys, grad_values], axis=1)
    early = reduce_group(
        [grads[6], grads[4].reshape(-1, width), grads[5].reshape(-1, width), grads[3]], sizes, False
    )
    early, grad_kv = lax.optimization_barrier((early, grad_kv))
    mine_kv = jnp.where(c == 0, grad_kv[:local_length], grad_kv[local_length:])
    theirs_kv = jnp.where(c == 0, grad_kv[local_length:], grad_kv[:local_length])
    own_kv = mine_kv + lax.ppermute(theirs_kv, "c", [(0, 1), (1, 0)])
    own_keys = own_kv[:, :width]
    own_values = own_kv[:, width:]
    query_low = (
        rotate(grad_query, cosine, -sine).reshape(local_length, width).astype(jnp.bfloat16)
    )
    keys_low = (
        rotate(own_keys.reshape(local_length, head_count, head_size), cosine, -sine)
        .reshape(local_length, width)
        .astype(jnp.bfloat16)
    )
    values_low = own_values.astype(jnp.bfloat16)
    grads[0] = contract_rows(normed_low, query_low)
    grads[1] = contract_rows(normed_low, keys_low)
    grads[2] = contract_rows(normed_low, values_low)
    grad_normed = (
        contract_cols(query_low, query_weight)
        + contract_cols(keys_low, key_weight)
        + contract_cols(values_low, value_weight)
    )
    grad_hidden = grad_after + norm_one_back(grad_normed)[0]
    both_out = from_sequence(jnp.concatenate([result_low, grad_hidden.astype(jnp.bfloat16)], axis=1))
    output = both_out[..., :width]
    input_grads = both_out[..., width:]
    late = reduce_group([grads[0], grads[1], grads[2]], sizes, True)
    gate_rows = grads[4].shape[0]
    gate_grad = early[1].reshape(gate_rows // 4, -1)
    up_grad = early[2].reshape(gate_rows // 4, -1)
    owned = [late[0], late[1], late[2], early[3], gate_grad, up_grad, early[0]]

    return (output, input_grads, *owned)


def solution(mesh):
    rep, grp = mesh.devices.shape
    side = int(round((rep // 2) ** 0.5))
    devices = mesh.devices.reshape(side, rep // (2 * side), 2, grp // 2, 2)
    fine = Mesh(devices, ("y", "z", "xl", "xh", "c"))
    seqs = P(REP, GRP, None)
    rows = P(GRP, None)
    placed = (seqs, P(REP, None), P(REP, None), rows, rows, rows, rows, rows, rows, rows, seqs)
    return jax.shard_map(
        body,
        mesh=fine,
        in_specs=placed,
        out_specs=(seqs, seqs, rows, rows, rows, rows, rows, rows, rows),
        check_vma=False,
    )
```

profile of v0, /device:TPU:0, one launch (start us, length us, event | category | flops | bytes accessed | tf_op | source)
XLA Modules:
  0.0 607.4 jit_solution(17988151945343200479)
XLA Ops:
  37.0 13.8 %collective-permute-start.8 = (bf16[240,768]{1,0:T(8,128)(2,1)}, bf16[240,768]{1,0:T(8,128)(2,1)}, u32[]{:S(2)}, u32[]{:S(2)}) collective-permute-start(bf16[240,768]{1,0:T(8,128)(2,1)} %fusion.70), channel_id=1, source_target_pairs={{0,6},{2,4},{4,2},{6,0},{1,7},{3,5},{5,3},{7,1},{8,14},{10,12},{12... | collective-permute-start | bytes 1105928 | tf_op jit(solution)/shard_map/ppermute | solution.py:244
  93.2 6.1 collective-permute-done.17
  108.9 14.7 %maximum_select_fusion.k_ref.v_ref = bf16[1024,1536]{1,0:T(8,128)(2,1)} fusion(bf16[512,1536]{1,0:T(8,128)(2,1)} %collective-permute-done.7, bf16[512,768]{1,0:T(8,128)(2,1)S(1)} %copy-done.29, bf16[512,768]{1,0:T(8,128)(2,1)S(1)} %copy-done.22, pred[]{:T(512)S(6)} %eq.57), kind=kLoop, calls=%fused_computation.42 | loop fusion | flops 20447232 | bytes 6291457 | tf_op jit(solution)/shard_map/jit(_where)/select_n | solution.py:364
  123.6 23.9 %shard_map.178 = (f32[512,768]{1,0:T(8,128)}, f32[6,512,2]{2,1,0:T(8,128)}) custom-call(bf16[512,768]{1,0:T(8,128)(2,1)} %copy.23.q_ref, bf16[1024,1536]{1,0:T(8,128)(2,1)} %maximum_select_fusion.k_ref.v_ref, bf16[1024,1536]{1,0:T(8,128)(2,1)} %maximum_select_fusion.k_ref.v_ref, s32[512,1]{1,0:T(8,128)} %iota_add_fusion.rq_ref, s32[512,1]{1,0:T(8,128)} %copy.24.sq_ref, ...), custom_call_target="tpu_custom_call" | custom-call | flops 1610612736 | bytes 5505024 | tf_op jit(solution)/shard_map/pallas_call | solution.py:114
  160.5 7.2 %fusion.51 = f32[512,3072]{1,0:T(8,128)} fusion(bf16[3072,768]{1,0:T(8,128)(2,1)} %slice_dynamic-update-slice_fusion, bf16[512,1536]{1,0:T(8,128)(2,1)S(1)} %maximum_select_fusion.1), kind=kOutput, calls=%fused_computation.183 | convolution fusion | flops 2415919104 | bytes 11796480 | tf_op jit(solution)/shard_map/dot_general | solution.py:45
  180.8 9.1 %multiply_convert_fusion.1 = (bf16[512,3072]{1,0:T(8,128)(2,1)}, bf16[512,3072]{1,0:T(8,128)(2,1)S(1)}, bf16[512,3072]{1,0:T(8,128)(2,1)S(1)}) fusion(f32[512,3072]{1,0:T(8,128)S(1)} %fusion.109, f32[512,3072]{1,0:T(8,128)} %fusion.51, bf16[512,768]{1,0:T(8,128)(2,1)S(1)} %multiply_convert_fusion.2, bf16[768,3072]{1,0:T(8,128)(2,1)S(1)} %get-tuple-element.59), kind=kOutput, calls=%fused_computation.28 | convolution fusion | flops 2444230656 | bytes 27525120 | tf_op jit(solution)/shard_map/dot_general | solution.py:35
  192.6 5.2 fusion.113
  197.8 5.3 fusion.112
  203.1 5.2 multiply_reduce_fusion
  212.5 11.6 %reshape.212 = f32[3072,768]{1,0:T(8,128)} reshape(f32[768,3072]{1,0:T(8,128)} %fusion.113) | data formatting | bytes 18874368 | tf_op jit(solution)/shard_map/reshape | solution.py:432
  224.1 11.6 %reshape.211 = f32[3072,768]{1,0:T(8,128)} reshape(f32[768,3072]{1,0:T(8,128)} %fusion.112) | data formatting | bytes 18874368 | tf_op jit(solution)/shard_map/reshape | solution.py:432
  262.0 5.6 constant_dynamic-slice_fusion.8
  270.2 9.8 %convert_element_type.259 = f32[4992,768]{1,0:T(8,128)} convert(bf16[4992,768]{1,0:T(8,128)(2,1)} %collective-permute-done.20) | non-fusion elementwise | flops 3833856 | bytes 23003136 | tf_op jit(solution)/shard_map/convert_element_type | solution.py:288
  280.0 15.6 %fusion = (f32[1,2496,768]{2,1,0:T(8,128)}, f32[1,2496,768]{2,1,0:T(8,128)}) fusion(f32[4992,768]{1,0:T(8,128)} %convert_element_type.259, f32[192,768]{1,0:T(8,128)S(1)} %copy-done.35, f32[768,768]{1,0:T(8,128)S(1)} %get-tuple-element.57, f32[768,768]{1,0:T(8,128)} %get-tuple-element.55, f32[768,768]{1,0:T(8,128)} %get-tuple-element.53, ...), kind=kLoop, calls=%fused_computation.11 | loop fusion | flops 15335424 | bytes 46006272 | tf_op jit(solution)/shard_map/stack | solution.py:292
  295.6 6.3 %fusion.4 = (f32[2,624,768]{2,1,0:T(8,128)S(1)}, f32[2,624,768]{2,1,0:T(8,128)}, f32[2,624,768]{2,1,0:T(8,128)S(1)}) fusion(s32[]{:T(128)S(6)} %select_n.432, f32[1,2496,768]{2,1,0:T(8,128)} %get-tuple-element.49, f32[1,2496,768]{2,1,0:T(8,128)} %get-tuple-element.48, s32[]{:T(128)S(6)} %select_n.430, s32[]{:T(128)S(6)} %select_n.434), kind=kLoop, calls=%fused_computation.41 | loop fusion | flops 2875392 | bytes 26837004 | tf_op jit(solution)/shard_map/stack | solution.py:292
  309.5 41.0 %collective-permute-done.22 = bf16[2,2,624,384]{3,2,1,0:T(8,128)(2,1)S(1)} collective-permute-done((bf16[2,2,624,384]{3,2,1,0:T(8,128)(2,1)S(1)}, bf16[2,2,624,384]{3,2,1,0:T(8,128)(2,1)S(1)}, u32[]{:S(2)}, u32[]{:S(2)}) %collective-permute-start.22) | collective-permute-done | bytes 1916960 | tf_op jit(solution)/shard_map/ppermute | solution.py:172
  357.1 18.8 %collective-permute-done.23 = bf16[2,624,384]{2,1,0:T(8,128)(2,1)} collective-permute-done((bf16[2,624,384]{2,1,0:T(8,128)(2,1)}, bf16[2,624,384]{2,1,0:T(8,128)(2,1)}, u32[]{:S(2)}, u32[]{:S(2)}) %collective-permute-start.23) | collective-permute-done | bytes 958496 | tf_op jit(solution)/shard_map/ppermute | solution.py:172
  389.1 8.7 %collective-permute-done.26 = bf16[2,2,156,384]{3,2,1,0:T(8,128)(2,1)S(1)} collective-permute-done((bf16[2,2,156,384]{3,2,1,0:T(8,128)(2,1)S(1)}, bf16[2,2,156,384]{3,2,1,0:T(8,128)(2,1)S(1)}, u32[]{:S(2)}, u32[]{:S(2)}) %collective-permute-start.26) | collective-permute-done | bytes 479264 | tf_op jit(solution)/shard_map/ppermute | solution.py:172
  424.4 5.5 collective-permute-done.32
  445.0 31.0 %shard_map.179 = (f32[512,768]{1,0:T(8,128)}, f32[1024,768]{1,0:T(8,128)}, f32[1024,768]{1,0:T(8,128)}) custom-call(bf16[512,768]{1,0:T(8,128)(2,1)} %copy.23.q_ref, bf16[1024,1536]{1,0:T(8,128)(2,1)} %maximum_select_fusion.k_ref.v_ref, bf16[1024,1536]{1,0:T(8,128)(2,1)} %maximum_select_fusion.k_ref.v_ref, bf16[512,768]{1,0:T(8,128)(2,1)} %convolution_convert_fusion.do_ref, ...), custom_call_target="tpu_custom_call" | custom-call | flops 4026531840 | bytes 12582912 | tf_op jit(solution)/shard_map/pallas_call | solution.py:143
  496.6 6.5 %add_convert_fusion.2 = bf16[512,768]{1,0:T(8,128)(2,1)S(1)} fusion(f32[512,768]{1,0:T(8,128)} %copy-done.6, bf16[512,3072]{1,0:T(8,128)(2,1)} %get-tuple-element.50, bf16[3072,768]{1,0:T(8,128)(2,1)} %slice_dynamic-update-slice_fusion), kind=kOutput, calls=%fused_computation.97 | convolution fusion | flops 2416705536 | bytes 10223616 | tf_op jit(solution)/shard_map/dot_general | solution.py:35
  531.1 8.3 %collective-permute-done.44 = bf16[2,144,768]{2,1,0:T(8,128)(2,1)S(1)} collective-permute-done((bf16[2,144,768]{2,1,0:T(8,128)(2,1)S(1)}, bf16[2,144,768]{2,1,0:T(8,128)(2,1)S(1)}, u32[]{:S(2)}, u32[]{:S(2)}) %collective-permute-start.44) | collective-permute-done | bytes 442400 | tf_op jit(solution)/shard_map/ppermute | solution.py:172
  539.3 10.7 %collective-permute-done.45 = bf16[2,144,768]{2,1,0:T(8,128)(2,1)S(1)} collective-permute-done((bf16[2,144,768]{2,1,0:T(8,128)(2,1)S(1)}, bf16[2,144,768]{2,1,0:T(8,128)(2,1)S(1)}, u32[]{:S(2)}, u32[]{:S(2)}) %collective-permute-start.45) | collective-permute-done | bytes 442400 | tf_op jit(solution)/shard_map/ppermute | solution.py:172
  569.7 11.6 %collective-permute-done.51 = bf16[36,768]{1,0:T(8,128)(2,1)S(1)} collective-permute-done((bf16[36,768]{1,0:T(8,128)(2,1)}, bf16[36,768]{1,0:T(8,128)(2,1)S(1)}, u32[]{:S(2)}, u32[]{:S(2)}) %collective-permute-start.51) | collective-permute-done | bytes 55328 | tf_op jit(solution)/shard_map/ppermute | solution.py:244
  (439 shorter events, 311.7 us)
Async XLA Ops:
  6.8 23.3 %collective-permute-start = (bf16[256,1536]{1,0:T(8,128)(2,1)S(1)}, bf16[256,1536]{1,0:T(8,128)(2,1)}, u32[]{:S(2)}, u32[]{:S(2)}) collective-permute-start(bf16[256,1536]{1,0:T(8,128)(2,1)S(1)} %get-tuple-element.101), channel_id=1, source_target_pairs={{0,0},{1,2},{2,1},{3,3},{4,4},{5,6},{6,5},{7,7},{8,8},{9,10},{10,9... | collective-permute-start | bytes 2359304 | tf_op jit(solution)/shard_map/ppermute | solution.py:316
  8.5 21.6 %collective-permute-start.1 = (bf16[256,1536]{1,0:T(8,128)(2,1)S(1)}, bf16[256,1536]{1,0:T(8,128)(2,1)}, u32[]{:S(2)}, u32[]{:S(2)}) collective-permute-start(bf16[256,1536]{1,0:T(8,128)(2,1)S(1)} %get-tuple-element.102), channel_id=1, source_target_pairs={{0,2},{1,0},{2,3},{3,1},{4,6},{5,4},{6,7},{7,5},{8,10},{9,8},{10,1... | collective-permute-start | bytes 2359304 | tf_op jit(solution)/shard_map/ppermute | solution.py:317
  37.0 27.0 %collective-permute-start.8 = (bf16[240,768]{1,0:T(8,128)(2,1)}, bf16[240,768]{1,0:T(8,128)(2,1)}, u32[]{:S(2)}, u32[]{:S(2)}) collective-permute-start(bf16[240,768]{1,0:T(8,128)(2,1)} %fusion.70), channel_id=1, source_target_pairs={{0,6},{2,4},{4,2},{6,0},{1,7},{3,5},{5,3},{7,1},{8,14},{10,12},{12... | collective-permute-start | bytes 1105928 | tf_op jit(solution)/shard_map/ppermute | solution.py:244
  52.0 21.1 %collective-permute-start.14 = (bf16[96,3072]{1,0:T(8,128)(2,1)}, bf16[96,3072]{1,0:T(8,128)(2,1)}, u32[]{:S(2)}, u32[]{:S(2)}) collective-permute-start(bf16[96,3072]{1,0:T(8,128)(2,1)} %fusion.48), channel_id=1, source_target_pairs={{0,6},{2,4},{4,2},{6,0},{1,7},{3,5},{5,3},{7,1},{8,14},{10,12},{12... | collective-permute-start | bytes 1769480 | tf_op jit(solution)/shard_map/ppermute | solution.py:244
  60.9 47.4 %collective-permute-start.7 = (bf16[512,1536]{1,0:T(8,128)(2,1)}, bf16[512,1536]{1,0:T(8,128)(2,1)}, u32[]{:S(2)}, u32[]{:S(2)}) collective-permute-start(bf16[512,1536]{1,0:T(8,128)(2,1)} %pad_maximum_fusion.6), channel_id=1, source_target_pairs={{0,1},{1,0},{2,3},{3,2},{4,5},{5,4},{6,7},{7,6},{8,9},{9,8},{10,11... | collective-permute-start | bytes 4718600 | tf_op jit(solution)/shard_map/ppermute | solution.py:363
  64.0 13.3 %collective-permute-start.9 = (bf16[240,768]{1,0:T(8,128)(2,1)}, bf16[240,768]{1,0:T(8,128)(2,1)S(1)}, u32[]{:S(2)}, u32[]{:S(2)}) collective-permute-start(bf16[240,768]{1,0:T(8,128)(2,1)} %collective-permute-done.8), channel_id=1, source_target_pairs={{0,8},{8,16},{16,24},{24,0},{1,9},{9,17},{17,25},{25,1},{2,10},{10... | collective-permute-start | bytes 1105928 | tf_op jit(solution)/shard_map/ppermute | solution.py:172
  73.1 16.6 %collective-permute-start.15 = (bf16[96,3072]{1,0:T(8,128)(2,1)}, bf16[96,3072]{1,0:T(8,128)(2,1)S(1)}, u32[]{:S(2)}, u32[]{:S(2)}) collective-permute-start(bf16[96,3072]{1,0:T(8,128)(2,1)} %collective-permute-done.14), channel_id=1, source_target_pairs={{0,32},{32,64},{64,96},{96,0},{1,33},{33,65},{65,97},{97,1},{2,34}... | collective-permute-start | bytes 1769480 | tf_op jit(solution)/shard_map/ppermute | solution.py:172
  74.7 15.6 %collective-permute-start.16 = (bf16[96,3072]{1,0:T(8,128)(2,1)}, bf16[96,3072]{1,0:T(8,128)(2,1)S(1)}, u32[]{:S(2)}, u32[]{:S(2)}) collective-permute-start(bf16[96,3072]{1,0:T(8,128)(2,1)} %collective-permute-done.14), channel_id=1, source_target_pairs={{0,96},{32,0},{64,32},{96,64},{1,97},{33,1},{65,33},{97,65},{2,98}... | collective-permute-start | bytes 1769480 | tf_op jit(solution)/shard_map/ppermute | solution.py:172
  87.1 60.3 %collective-permute-start.13 = (bf16[1920,768]{1,0:T(8,128)(2,1)}, bf16[1920,768]{1,0:T(8,128)(2,1)}, u32[]{:S(2)}, u32[]{:S(2)}) collective-permute-start(bf16[1920,768]{1,0:T(8,128)(2,1)} %pad_maximum_fusion.2), channel_id=1, source_target_pairs={{0,1},{1,0},{2,3},{3,2},{4,5},{5,4},{6,7},{7,6},{8,9},{9,8},{10,11... | collective-permute-start | bytes 8847368 | tf_op jit(solution)/shard_map/ppermute | solution.py:248
  102.5 65.3 %collective-permute-start.19 = (bf16[768,3072]{1,0:T(8,128)(2,1)}, bf16[768,3072]{1,0:T(8,128)(2,1)}, u32[]{:S(2)}, u32[]{:S(2)}) collective-permute-start(bf16[768,3072]{1,0:T(8,128)(2,1)} %pad_maximum_fusion.1), channel_id=1, source_target_pairs={{0,1},{1,0},{2,3},{3,2},{4,5},{5,4},{6,7},{7,6},{8,9},{9,8},{10,11... | collective-permute-start | bytes 14155784 | tf_op jit(solution)/shard_map/ppermute | solution.py:248
  257.4 12.8 %collective-permute-start.20 = (bf16[4992,768]{1,0:T(8,128)(2,1)}, bf16[4992,768]{1,0:T(8,128)(2,1)}, u32[]{:S(2)}, u32[]{:S(2)}) collective-permute-start(bf16[4992,768]{1,0:T(8,128)(2,1)} %fusion.74), channel_id=1, source_target_pairs={{0,1},{1,0},{2,3},{3,2},{4,5},{5,4},{6,7},{7,6},{8,9},{9,8},{10,11... | collective-permute-start | bytes 23003144 | tf_op jit(solution)/shard_map/ppermute | solution.py:248
  306.2 44.4 %collective-permute-start.22 = (bf16[2,2,624,384]{3,2,1,0:T(8,128)(2,1)S(1)}, bf16[2,2,624,384]{3,2,1,0:T(8,128)(2,1)S(1)}, u32[]{:S(2)}, u32[]{:S(2)}) collective-permute-start(bf16[2,2,624,384]{3,2,1,0:T(8,128)(2,1)S(1)} %pad_maximum_fusion.4), channel_id=1, source_target_pairs={{0,96},{32,0},{64,32},{96,64},{1,97},{33,1},{65,33},{97,65},{2,98}... | collective-permute-start | bytes 5750792 | tf_op jit(solution)/shard_map/ppermute | solution.py:172
  309.5 46.0 %collective-permute-start.21 = (bf16[2,2,624,384]{3,2,1,0:T(8,128)(2,1)S(1)}, bf16[2,2,624,384]{3,2,1,0:T(8,128)(2,1)S(1)}, u32[]{:S(2)}, u32[]{:S(2)}) collective-permute-start(bf16[2,2,624,384]{3,2,1,0:T(8,128)(2,1)S(1)} %pad_maximum_fusion.3), channel_id=1, source_target_pairs={{0,32},{32,64},{64,96},{96,0},{1,33},{33,65},{65,97},{97,1},{2,34}... | collective-permute-start | bytes 5750792 | tf_op jit(solution)/shard_map/ppermute | solution.py:172
  351.8 24.1 %collective-permute-start.23 = (bf16[2,624,384]{2,1,0:T(8,128)(2,1)}, bf16[2,624,384]{2,1,0:T(8,128)(2,1)}, u32[]{:S(2)}, u32[]{:S(2)}) collective-permute-start(bf16[2,624,384]{2,1,0:T(8,128)(2,1)} %fusion.15), channel_id=1, source_target_pairs={{0,96},{32,0},{64,32},{96,64},{1,97},{33,1},{65,33},{97,65},{2,98}... | collective-permute-start | bytes 2875400 | tf_op jit(solution)/shard_map/ppermute | solution.py:172
  357.1 23.8 %collective-permute-start.24 = (bf16[2,624,384]{2,1,0:T(8,128)(2,1)}, bf16[2,624,384]{2,1,0:T(8,128)(2,1)}, u32[]{:S(2)}, u32[]{:S(2)}) collective-permute-start(bf16[2,624,384]{2,1,0:T(8,128)(2,1)} %fusion.13), channel_id=1, source_target_pairs={{0,32},{32,64},{64,96},{96,0},{1,33},{33,65},{65,97},{97,1},{2,34}... | collective-permute-start | bytes 2875400 | tf_op jit(solution)/shard_map/ppermute | solution.py:172
  438.6 37.4 %collective-permute-start.36 = (bf16[624,768]{1,0:T(8,128)(2,1)S(1)}, bf16[624,768]{1,0:T(8,128)(2,1)S(1)}, u32[]{:S(2)}, u32[]{:S(2)}) collective-permute-start(bf16[624,768]{1,0:T(8,128)(2,1)S(1)} %dynamic_update_slice.211), channel_id=1, source_target_pairs={{0,32},{32,64},{64,96},{96,0},{1,33},{33,65},{65,97},{97,1},{2,34}... | collective-permute-start | bytes 2875400 | tf_op jit(solution)/shard_map/ppermute | solution.py:172
  438.7 37.5 %collective-permute-start.37 = (bf16[624,768]{1,0:T(8,128)(2,1)S(1)}, bf16[624,768]{1,0:T(8,128)(2,1)}, u32[]{:S(2)}, u32[]{:S(2)}) collective-permute-start(bf16[624,768]{1,0:T(8,128)(2,1)S(1)} %dynamic_update_slice.211), channel_id=1, source_target_pairs={{0,96},{32,0},{64,32},{96,64},{1,97},{33,1},{65,33},{97,65},{2,98}... | collective-permute-start | bytes 2875400 | tf_op jit(solution)/shard_map/ppermute | solution.py:172
  524.9 14.5 %collective-permute-start.44 = (bf16[2,144,768]{2,1,0:T(8,128)(2,1)S(1)}, bf16[2,144,768]{2,1,0:T(8,128)(2,1)S(1)}, u32[]{:S(2)}, u32[]{:S(2)}) collective-permute-start(bf16[2,144,768]{2,1,0:T(8,128)(2,1)S(1)} %get-tuple-element.71), channel_id=1, source_target_pairs={{0,32},{32,64},{64,96},{96,0},{1,33},{33,65},{65,97},{97,1},{2,34}... | collective-permute-start | bytes 1327112 | tf_op jit(solution)/shard_map/ppermute | solution.py:172
  525.2 24.8 %collective-permute-start.45 = (bf16[2,144,768]{2,1,0:T(8,128)(2,1)S(1)}, bf16[2,144,768]{2,1,0:T(8,128)(2,1)S(1)}, u32[]{:S(2)}, u32[]{:S(2)}) collective-permute-start(bf16[2,144,768]{2,1,0:T(8,128)(2,1)S(1)} %get-tuple-element.72), channel_id=1, source_target_pairs={{0,64},{32,96},{64,0},{96,32},{1,65},{33,97},{65,1},{97,33},{2,66}... | collective-permute-start | bytes 1327112 | tf_op jit(solution)/shard_map/ppermute | solution.py:172
  530.4 19.6 %collective-permute-start.46 = (bf16[2,144,768]{2,1,0:T(8,128)(2,1)S(1)}, bf16[2,144,768]{2,1,0:T(8,128)(2,1)S(1)}, u32[]{:S(2)}, u32[]{:S(2)}) collective-permute-start(bf16[2,144,768]{2,1,0:T(8,128)(2,1)S(1)} %get-tuple-element.73), channel_id=1, source_target_pairs={{0,96},{32,0},{64,32},{96,64},{1,97},{33,1},{65,33},{97,65},{2,98}... | collective-permute-start | bytes 1327112 | tf_op jit(solution)/shard_map/ppermute | solution.py:172
  555.4 32.0 %collective-permute-start.41 = (bf16[256,1536]{1,0:T(8,128)(2,1)}, bf16[256,1536]{1,0:T(8,128)(2,1)S(1)}, u32[]{:S(2)}, u32[]{:S(2)}) collective-permute-start(bf16[256,1536]{1,0:T(8,128)(2,1)} %get-tuple-element.99), channel_id=1, source_target_pairs={{0,0},{1,2},{2,1},{3,3},{4,4},{5,6},{6,5},{7,7},{8,8},{9,10},{10,9... | collective-permute-start | bytes 2359304 | tf_op jit(solution)/shard_map/ppermute | solution.py:327
  557.2 30.2 %collective-permute-start.42 = (bf16[256,1536]{1,0:T(8,128)(2,1)}, bf16[256,1536]{1,0:T(8,128)(2,1)}, u32[]{:S(2)}, u32[]{:S(2)}) collective-permute-start(bf16[256,1536]{1,0:T(8,128)(2,1)} %get-tuple-element.100), channel_id=1, source_target_pairs={{2,0},{0,1},{3,2},{1,3},{6,4},{4,5},{7,6},{5,7},{10,8},{8,9},{11,1... | collective-permute-start | bytes 2359304 | tf_op jit(solution)/shard_map/ppermute | solution.py:328
  561.0 20.3 %collective-permute-start.51 = (bf16[36,768]{1,0:T(8,128)(2,1)}, bf16[36,768]{1,0:T(8,128)(2,1)S(1)}, u32[]{:S(2)}, u32[]{:S(2)}) collective-permute-start(bf16[36,768]{1,0:T(8,128)(2,1)} %get-tuple-element.120), channel_id=1, source_target_pairs={{0,6},{2,4},{4,2},{6,0},{1,7},{3,5},{5,3},{7,1},{8,14},{10,12},{12... | collective-permute-start | bytes 165896 | tf_op jit(solution)/shard_map/ppermute | solution.py:244
  562.7 18.6 %collective-permute-start.52 = (bf16[36,768]{1,0:T(8,128)(2,1)}, bf16[36,768]{1,0:T(8,128)(2,1)}, u32[]{:S(2)}, u32[]{:S(2)}) collective-permute-start(bf16[36,768]{1,0:T(8,128)(2,1)} %get-tuple-element.120), channel_id=1, source_target_pairs={{0,2},{2,0},{1,3},{3,1},{4,6},{6,4},{5,7},{7,5},{8,10},{10,8},{9,1... | collective-permute-start | bytes 165896 | tf_op jit(solution)/shard_map/ppermute | solution.py:300
  (100 other events, 1052.6 us)
where the time goes:
time: 617 us; the launch traced here: 607 us
  waiting for transfers between devices  152 us (25%)
  local copies, waits for them, and re-layouts  131 us (21%)
  starting transfers between devices  103 us (17%)
  other arithmetic  97 us (16%)
  matrix products  67 us (11%)
  Pallas kernels  54.9 us (9%)
    ppermute x39, waiting for transfers between devices, shift(): return lax.ppermute(x, axis, [(i, (i + step) % n) for i in range(n)])  133 us
    ppermute x39, starting transfers between devices, shift(): return lax.ppermute(x, axis, [(i, (i + step) % n) for i in range(n)])  66.4 us
    dynamic_update_slice x48, local copies, waits for them, and re-layouts, place(): return lax.dynamic_update_slice(buf, piece, start)  34.2 us
    unnamed x143, local copies, waits for them, and re-layouts  31.8 us
    pallas_call x1, Pallas kernels, attention_backward(): pl.pallas_call(attention_backward_kernel, grid=(pairs,), in_specs=[pl.Blo...  31 us
    dot_general x7, matrix products, matmul(): return jnp.dot(left, right, preferred_element_type=jnp.float32)  25.9 us
    pallas_call x1, Pallas kernels, attention_forward(): pl.pallas_call(attention_forward_kernel, grid=(pairs,), in_specs=[pl.Bloc...  23.9 us
    another operation x3, other arithmetic, reduce_group(): pair = jnp.stack([own, oth])  22.4 us
  transfers between devices with their start and end apart: 59, of which 26 were waited for; matrix products, arithmetic and copies ran while one was open for 21% of the time, Pallas kernels for 9%

commit v1 on v0

--- a/solution.py
+++ b/solution.py
@@ -47,15 +47,18 @@
     )
 
 
-def allowed_mask(rq_ref, sq_ref, pq_ref, sk_ref, pk_ref, shape):
-    cols = lax.broadcasted_iota(jnp.int32, shape, 1)
-    return (sq_ref[...] == sk_ref[...]) & ((cols <= rq_ref[...]) | (pq_ref[...] == pk_ref[...]))
-
-
-def attention_forward_kernel(q_ref, k_ref, v_ref, rq_ref, sq_ref, pq_ref, sk_ref, pk_ref, o_ref, lse_ref):
+def allowed_mask(rq_ref, sq_ref, pq_ref, sk_ref, pk_ref, rk_ref):
+    return (sq_ref[...] == sk_ref[...]) & (
+        (rk_ref[...] <= rq_ref[...]) | (pq_ref[...] == pk_ref[...])
+    )
+
+
+def attention_forward_kernel(
+    q_ref, k_ref, v_ref, rq_ref, sq_ref, pq_ref, sk_ref, pk_ref, rk_ref, o_ref, lse_ref
+):
     queries = q_ref.shape[0]
     keys = k_ref.shape[0]
-    allowed = allowed_mask(rq_ref, sq_ref, pq_ref, sk_ref, pk_ref, (queries, keys))
+    allowed = allowed_mask(rq_ref, sq_ref, pq_ref, sk_ref, pk_ref, rk_ref)
     scale = HDIM ** (-0.5)
     for h in range(q_ref.shape[1] // HDIM):
         cols = slice(h * HDIM, (h + 1) * HDIM)
@@ -73,11 +76,12 @@
 
 
 def attention_backward_kernel(
-    q_ref, k_ref, v_ref, do_ref, lse_ref, rq_ref, sq_ref, pq_ref, sk_ref, pk_ref, dq_ref, dk_ref, dv_ref
+    q_ref, k_ref, v_ref, do_ref, lse_ref, rq_ref, sq_ref, pq_ref, sk_ref, pk_ref, rk_ref,
+    dq_ref, dk_ref, dv_ref,
 ):
     queries = q_ref.shape[0]
     keys = k_ref.shape[0]
-    allowed = allowed_mask(rq_ref, sq_ref, pq_ref, sk_ref, pk_ref, (queries, keys))
+    allowed = allowed_mask(rq_ref, sq_ref, pq_ref, sk_ref, pk_ref, rk_ref)
     scale = HDIM ** (-0.5)
     for h in range(q_ref.shape[1] // HDIM):
         cols = slice(h * HDIM, (h + 1) * HDIM)
@@ -103,7 +107,7 @@
 def mask_specs(queries, keys):
     column = pl.BlockSpec((queries, 1), lambda i: (0, 0))
     row = pl.BlockSpec((1, keys), lambda i: (0, 0))
-    return [column, column, column, row, row]
+    return [column, column, column, row, row, row]
 
 
 def attention_forward(q, kv, masks):
@@ -285,11 +289,12 @@
         return lax.dynamic_slice_in_dim(w, jnp.bitwise_xor(g, j) * rows, rows, axis=0)
 
     send = jnp.concatenate([shard(w, 1) for w in grads] + [shard(w, 3) for w in grads])
-    got = swap_core(send.astype(jnp.bfloat16)).astype(jnp.float32)
+    got = swap_core(send.astype(jnp.bfloat16))
     total = got.shape[0] // 2
-    own = jnp.concatenate([shard(w, 0) for w in grads]) + got[:total]
-    oth = jnp.concatenate([shard(w, 2) for w in grads]) + got[total:]
-    pair = jnp.stack([own, oth])
+    kept = jnp.stack(
+        [jnp.concatenate([shard(w, 0) for w in grads]), jnp.concatenate([shard(w, 2) for w in grads])]
+    )
+    pair = kept.astype(jnp.float32) + got.reshape(2, total, -1).astype(jnp.float32)
     pair = ring_reduce(pair, "y", sizes["y"], 1, 2, direct)
     pair = ring_reduce(pair, "z", sizes["z"], 1, 2, direct)
     low = pair.astype(jnp.bfloat16)
@@ -359,10 +364,6 @@
     seg_row = lax.dynamic_index_in_dim(segment, xh, 0, False)
     start_row = lax.dynamic_index_in_dim(piece_start, xh, 0, False)
 
-    def swap_halves(mine):
-        other = lax.ppermute(mine, "c", [(0, 1), (1, 0)])
-        return jnp.where(c == 0, jnp.concatenate([mine, other]), jnp.concatenate([other, mine]))
-
     normed, norm_one_back = jax.vjp(layer_norm, hidden)
     normed_low = normed.astype(jnp.bfloat16)
     query_heads = rotate(
@@ -383,15 +384,23 @@
     w_out, w_down, w_gate, w_up, values = lax.optimization_barrier((w_out, w_down, w_gate, w_up, values))
     out_weight, down_weight = gather_weights((w_out, w_down), "z", sizes, False)
     gate_weight, up_weight = gather_weights((w_gate, w_up), "y", sizes, False)
-    both = swap_halves(jnp.concatenate([keys, values], axis=1))
+    mine_kv = jnp.concatenate([keys, values], axis=1)
+    both = jnp.concatenate([mine_kv, swap_core(mine_kv)])
+    other_row = (1 - c) * local_length
     seg_local = lax.dynamic_slice_in_dim(seg_row, first_row, local_length)
     start_local = lax.dynamic_slice_in_dim(start_row, first_row, local_length)
+    key_rows = jnp.concatenate([rows, other_row + jnp.arange(local_length, dtype=jnp.int32)])
+    seg_keys = jnp.concatenate([seg_local, lax.dynamic_slice_in_dim(seg_row, other_row, local_length)])
+    start_keys = jnp.concatenate(
+        [start_local, lax.dynamic_slice_in_dim(start_row, other_row, local_length)]
+    )
     masks = (
         rows[:, None],
         seg_local[:, None],
         start_local[:, None],
-        seg_row[None, :],
-        start_row[None, :],
+        seg_keys[None, :],
+        start_keys[None, :],
+        key_rows[None, :],
     )
     query_flat = query_heads.reshape(local_length, width)
     mixed, log_total = attention_forward(query_flat, both, masks)
@@ -428,13 +437,7 @@
     )
     grad_query = grad_query.reshape(local_length, head_count, head_size)
     grad_kv = jnp.concatenate([grad_keys, grad_values], axis=1)
-    early = reduce_group(
-        [grads[6], grads[4].reshape(-1, width), grads[5].reshape(-1, width), grads[3]], sizes, False
-    )
-    early, grad_kv = lax.optimization_barrier((early, grad_kv))
-    mine_kv = jnp.where(c == 0, grad_kv[:local_length], grad_kv[local_length:])
-    theirs_kv = jnp.where(c == 0, grad_kv[local_length:], grad_kv[:local_length])
-    own_kv = mine_kv + lax.ppermute(theirs_kv, "c", [(0, 1), (1, 0)])
+    own_kv = grad_kv[:local_length] + swap_core(grad_kv[local_length:])
     own_keys = own_kv[:, :width]
     own_values = own_kv[:, width:]
     query_low = (
@@ -458,11 +461,15 @@
     both_out = from_sequence(jnp.concatenate([result_low, grad_hidden.astype(jnp.bfloat16)], axis=1))
     output = both_out[..., :width]
     input_grads = both_out[..., width:]
-    late = reduce_group([grads[0], grads[1], grads[2]], sizes, True)
     gate_rows = grads[4].shape[0]
-    gate_grad = early[1].reshape(gate_rows // 4, -1)
-    up_grad = early[2].reshape(gate_rows // 4, -1)
-    owned = [late[0], late[1], late[2], early[3], gate_grad, up_grad, early[0]]
+    low = [w.astype(jnp.bfloat16) for w in grads]
+    owned = reduce_group(
+        [low[0], low[1], low[2], low[3], low[4].reshape(-1, width), low[5].reshape(-1, width), low[6]],
+        sizes,
+        False,
+    )
+    owned[4] = owned[4].reshape(gate_rows // 4, -1)
+    owned[5] = owned[5].reshape(gate_rows // 4, -1)
 
     return (output, input_grads, *owned)
 

time: 617 us -> 592 us (0.959)
  waiting for transfers between devices: 152 us -> 218 us
  starting transfers between devices: 103 us -> 59.3 us
  other arithmetic: 97 us -> 62.9 us
  local copies, waits for them, and re-layouts: 131 us -> 106 us
  matrix products: 67 us -> 82.5 us
    ppermute x39 -> x27, waiting for transfers between devices: 133 us -> 161 us  [shift(): return lax.ppermute(x, axis, [(i, (i + step) % n) for i in range(n)])]
    another operation x5 -> x2, other arithmetic: 26.3 us -> 3.96 us  [the longest x3 22.4 us: reduce_group(): pair = jnp.stack([own, oth])]
    ppermute x39 -> x27, starting transfers between devices: 66.4 us -> 44.6 us  [shift(): return lax.ppermute(x, axis, [(i, (i + step) % n) for i in range(n)])]
    select_n x2 -> x0, other arithmetic: 16.9 us -> none  [the longest x1 14.7 us: swap_halves(): jnp.where(c == 0, jnp.concatenate([mine, other]), jnp.concatenate([other,...]
    ppermute x5 -> x4, starting transfers between devices: 21.9 us -> 6.79 us  [cross(): return lax.ppermute(x, ('xl', 'xh'), [(i, 3 - i) for i in range(4)])]
    ppermute x5 -> x6, waiting for transfers between devices: 0.01 us -> 15 us  [swap_core(): return lax.ppermute(x, 'c', [(0, 1), (1, 0)])]
    dynamic_slice x8 -> x2, local copies, waits for them, and re-layouts: 13.5 us -> 0.17 us  [the longest x1 0.09 us: body(): lax.dynamic_slice_in_dim(seg_row, other_row, local_length)]
    ppermute x1, waiting for transfers between devices: 0.01 us -> 12.3 us  [from_sequence(): second = lax.ppermute(second, GRP, [(2, 0), (0, 1), (3, 2), (1, 3)])]
  transfers between devices with their start and end apart: 59 -> 43, of which waited for: 26 -> 24; matrix products, arithmetic and copies ran while one was open for 21% -> 21% of each run, Pallas kernels for 9% -> 4%
where the time goes in v1:
time: 592 us; the launch traced here: 585 us
  waiting for transfers between devices  218 us (37%)
  local copies, waits for them, and re-layouts  106 us (18%)
  matrix products  82.5 us (14%)
  other arithmetic  62.9 us (11%)
  starting transfers between devices  59.3 us (10%)
  Pallas kernels  54.1 us (9%)
    ppermute x27, waiting for transfers between devices, shift(): return lax.ppermute(x, axis, [(i, (i + step) % n) for i in range(n)])  161 us
    ppermute x27, starting transfers between devices, shift(): return lax.ppermute(x, axis, [(i, (i + step) % n) for i in range(n)])  44.6 us
    dot_general x7, matrix products, matmul(): return jnp.dot(left, right, preferred_element_type=jnp.float32)  35.6 us
    unnamed x153, local copies, waits for them, and re-layouts  31.5 us
    pallas_call x1, Pallas kernels, attention_backward(): pl.pallas_call(attention_backward_kernel, grid=(pairs,), in_specs=[pl.Blo...  30.7 us
    dot_general x7, matrix products, contract_rows(): lax.dot_general(left, right, (((0,), (0,)), ((), ())), preferred_element_...  28.3 us
    ppermute x4, waiting for transfers between devices, cross(): return lax.ppermute(x, ('xl', 'xh'), [(i, 3 - i) for i in range(4)])  24.6 us
    dynamic_update_slice x38, local copies, waits for them, and re-layouts, place(): return lax.dynamic_update_slice(buf, piece, start)  23.8 us
  transfers between devices with their start and end apart: 43, of which 24 were waited for; matrix products, arithmetic and copies ran while one was open for 21% of the time, Pallas kernels for 4%

profile of v1, /device:TPU:0, one launch (start us, length us, event | category | flops | bytes accessed | tf_op | source)
XLA Modules:
  0.0 585.1 jit_solution(7871904751366867600)
XLA Ops:
  11.3 16.6 %collective-permute-done.2 = bf16[144,768]{1,0:T(8,128)(2,1)S(1)} collective-permute-done((bf16[144,768]{1,0:T(8,128)(2,1)}, bf16[144,768]{1,0:T(8,128)(2,1)S(1)}, u32[]{:S(2)}, u32[]{:S(2)}) %collective-permute-start.2) | collective-permute-done | bytes 221216 | tf_op jit(solution)/shard_map/ppermute | solution.py:248
  36.6 5.0 collective-permute-done.4
  73.0 5.1 collective-permute-done.14
  97.5 7.0 %collective-permute-done.18 = bf16[48,3072]{1,0:T(8,128)(2,1)S(1)} collective-permute-done((bf16[48,3072]{1,0:T(8,128)(2,1)S(1)}, bf16[48,3072]{1,0:T(8,128)(2,1)S(1)}, u32[]{:S(2)}, u32[]{:S(2)}) %collective-permute-start.18) | collective-permute-done | bytes 294944 | tf_op jit(solution)/shard_map/ppermute | solution.py:176
  125.4 23.4 %shard_map.178 = (f32[512,768]{1,0:T(8,128)}, f32[6,512,2]{2,1,0:T(8,128)}) custom-call(bf16[512,768]{1,0:T(8,128)(2,1)} %copy.23.q_ref, bf16[1024,1536]{1,0:T(8,128)(2,1)} %pad_maximum_fusion.1.k_ref.v_ref, bf16[1024,1536]{1,0:T(8,128)(2,1)} %pad_maximum_fusion.1.k_ref.v_ref, s32[512,1]{1,0:T(8,128)} %iota_add_fusion.rq_ref, s32[512,1]{1,0:T(8,128)} %copy.24.sq_ref, ...), custom_call_target="tpu_custom_call" | custom-call | flops 1610612736 | bytes 5505024 | tf_op jit(solution)/shard_map/pallas_call | solution.py:118
  161.8 5.0 fusion.37
  179.9 19.2 %multiply_convert_fusion.1 = (bf16[512,3072]{1,0:T(8,128)(2,1)}, bf16[512,3072]{1,0:T(8,128)(2,1)}, bf16[512,3072]{1,0:T(8,128)(2,1)S(1)}) fusion(f32[512,3072]{1,0:T(8,128)S(1)} %fusion.68, f32[512,3072]{1,0:T(8,128)S(1)} %fusion.37, bf16[512,768]{1,0:T(8,128)(2,1)S(1)} %multiply_convert_fusion.2, bf16[768,3072]{1,0:T(8,128)(2,1)S(1)} %get-tuple-element.63), kind=kOutput, calls=%fused_computation.14 | convolution fusion | flops 2444230656 | bytes 27525120 | tf_op jit(solution)/shard_map/dot_general | solution.py:35
  202.1 5.1 multiply_reduce_fusion
  212.2 30.7 %shard_map.179 = (f32[512,768]{1,0:T(8,128)}, f32[1024,768]{1,0:T(8,128)}, f32[1024,768]{1,0:T(8,128)}) custom-call(bf16[512,768]{1,0:T(8,128)(2,1)} %copy.23.q_ref, bf16[1024,1536]{1,0:T(8,128)(2,1)} %pad_maximum_fusion.1.k_ref.v_ref, bf16[1024,1536]{1,0:T(8,128)(2,1)} %pad_maximum_fusion.1.k_ref.v_ref, bf16[512,768]{1,0:T(8,128)(2,1)} %convolution_convert_fusion.7.do_ref, ...), custom_call_target="tpu_custom_call" | custom-call | flops 4026531840 | bytes 12582912 | tf_op jit(solution)/shard_map/pallas_call | solution.py:147
  253.4 6.9 %convolution_convert_fusion.2 = bf16[768,3072]{1,0:T(8,128)(2,1)} fusion(bf16[512,768]{1,0:T(8,128)(2,1)} %copy-done.30, bf16[512,3072]{1,0:T(8,128)(2,1)} %get-tuple-element.40), kind=kOutput, calls=%fused_computation.18 | convolution fusion | flops 2418278400 | bytes 8650752 | tf_op jit(solution)/shard_map/dot_general | solution.py:39
  260.3 8.5 %reshape.223 = bf16[3072,768]{1,0:T(8,128)(2,1)} reshape(bf16[768,3072]{1,0:T(8,128)(2,1)} %convolution_convert_fusion.2) | data formatting | bytes 9437184 | tf_op jit(solution)/shard_map/reshape | solution.py:467
  268.8 6.9 %convolution_convert_fusion.1 = bf16[768,3072]{1,0:T(8,128)(2,1)} fusion(bf16[512,768]{1,0:T(8,128)(2,1)} %copy-done.30, bf16[512,3072]{1,0:T(8,128)(2,1)} %copy-done.59), kind=kOutput, calls=%fused_computation.17 | convolution fusion | flops 2418278400 | bytes 8650752 | tf_op jit(solution)/shard_map/dot_general | solution.py:39
  275.7 8.8 %reshape.224 = bf16[3072,768]{1,0:T(8,128)(2,1)} reshape(bf16[768,3072]{1,0:T(8,128)(2,1)} %convolution_convert_fusion.1) | data formatting | bytes 9437184 | tf_op jit(solution)/shard_map/reshape | solution.py:467
  288.1 6.8 %convolution_convert_fusion = bf16[3072,768]{1,0:T(8,128)(2,1)} fusion(bf16[512,3072]{1,0:T(8,128)(2,1)} %get-tuple-element.39, bf16[512,1536]{1,0:T(8,128)(2,1)S(1)} %maximum_select_fusion), kind=kOutput, calls=%fused_computation.16 | convolution fusion | flops 2418278400 | bytes 8650752 | tf_op jit(solution)/shard_map/dot_general | solution.py:39
  327.0 15.0 %collective-permute-done.23 = bf16[6144,768]{1,0:T(8,128)(2,1)} collective-permute-done((bf16[6144,768]{1,0:T(8,128)(2,1)}, bf16[6144,768]{1,0:T(8,128)(2,1)}, u32[]{:S(2)}, u32[]{:S(2)}) %collective-permute-start.23) | collective-permute-done | bytes 9437216 | tf_op jit(solution)/shard_map/ppermute | solution.py:252
  342.0 7.3 %convert_add_fusion = f32[2,3072,768]{2,1,0:T(8,128)S(1)} fusion(bf16[2,3072,768]{2,1,0:T(8,128)(2,1)} %bitcast.43, bf16[1,3072,768]{2,1,0:T(8,128)(2,1)} %bitcast.22, bf16[1,3072,768]{2,1,0:T(8,128)(2,1)} %bitcast.21), kind=kLoop, calls=%fused_computation | loop fusion | flops 18874368 | bytes 37748736 | tf_op jit(solution)/shard_map/add | solution.py:297
  360.6 49.4 %collective-permute-done.24 = bf16[2,2,768,384]{3,2,1,0:T(8,128)(2,1)S(1)} collective-permute-done((bf16[2,2,768,384]{3,2,1,0:T(8,128)(2,1)S(1)}, bf16[2,2,768,384]{3,2,1,0:T(8,128)(2,1)S(1)}, u32[]{:S(2)}, u32[]{:S(2)}) %collective-permute-start.24) | collective-permute-done | bytes 2359328 | tf_op jit(solution)/shard_map/ppermute | solution.py:176
  411.8 28.7 %collective-permute-done.27 = bf16[2,768,384]{2,1,0:T(8,128)(2,1)} collective-permute-done((bf16[2,768,384]{2,1,0:T(8,128)(2,1)}, bf16[2,768,384]{2,1,0:T(8,128)(2,1)}, u32[]{:S(2)}, u32[]{:S(2)}) %collective-permute-start.27) | collective-permute-done | bytes 1179680 | tf_op jit(solution)/shard_map/ppermute | solution.py:176
  440.5 5.7 fusion.5
  446.2 6.0 %add_convert_fusion.2 = bf16[512,768]{1,0:T(8,128)(2,1)S(1)} fusion(f32[512,768]{1,0:T(8,128)S(1)} %get-tuple-element.114, bf16[512,3072]{1,0:T(8,128)(2,1)} %get-tuple-element.39, bf16[3072,768]{1,0:T(8,128)(2,1)} %slice_dynamic-update-slice_fusion), kind=kOutput, calls=%fused_computation.62 | convolution fusion | flops 2416705536 | bytes 10223616 | tf_op jit(solution)/shard_map/dot_general | solution.py:35
  452.3 20.5 %collective-permute-done.26 = bf16[2,768,384]{2,1,0:T(8,128)(2,1)} collective-permute-done((bf16[2,768,384]{2,1,0:T(8,128)(2,1)}, bf16[2,768,384]{2,1,0:T(8,128)(2,1)}, u32[]{:S(2)}, u32[]{:S(2)}) %collective-permute-start.26) | collective-permute-done | bytes 1179680 | tf_op jit(solution)/shard_map/ppermute | solution.py:176
  481.7 7.8 %collective-permute-done.29 = bf16[2,2,192,384]{3,2,1,0:T(8,128)(2,1)S(1)} collective-permute-done((bf16[2,2,192,384]{3,2,1,0:T(8,128)(2,1)S(1)}, bf16[2,2,192,384]{3,2,1,0:T(8,128)(2,1)S(1)}, u32[]{:S(2)}, u32[]{:S(2)}) %collective-permute-start.29) | collective-permute-done | bytes 589856 | tf_op jit(solution)/shard_map/ppermute | solution.py:176
  537.7 12.3 %collective-permute-done.22 = bf16[256,1536]{1,0:T(8,128)(2,1)} collective-permute-done((bf16[256,1536]{1,0:T(8,128)(2,1)}, bf16[256,1536]{1,0:T(8,128)(2,1)}, u32[]{:S(2)}, u32[]{:S(2)}) %collective-permute-start.22) | collective-permute-done | bytes 786464 | tf_op jit(solution)/shard_map/ppermute | solution.py:333
  562.8 8.5 %collective-permute-done.42 = bf16[384,768]{1,0:T(8,128)(2,1)S(1)} collective-permute-done((bf16[384,768]{1,0:T(8,128)(2,1)S(1)}, bf16[384,768]{1,0:T(8,128)(2,1)S(1)}, u32[]{:S(2)}, u32[]{:S(2)}) %collective-permute-start.42) | collective-permute-done | bytes 589856 | tf_op jit(solution)/shard_map/ppermute | solution.py:176
  (385 shorter events, 266.3 us)
Async XLA Ops:
  2.6 25.3 %collective-permute-start.2 = (bf16[144,768]{1,0:T(8,128)(2,1)}, bf16[144,768]{1,0:T(8,128)(2,1)S(1)}, u32[]{:S(2)}, u32[]{:S(2)}) collective-permute-start(bf16[144,768]{1,0:T(8,128)(2,1)} %fusion.48), channel_id=1, source_target_pairs={{0,6},{2,4},{4,2},{6,0},{1,7},{3,5},{5,3},{7,1},{8,14},{10,12},{12... | collective-permute-start | bytes 663560 | tf_op jit(solution)/shard_map/ppermute | solution.py:248
  5.7 38.2 %collective-permute-start.1 = (bf16[256,1536]{1,0:T(8,128)(2,1)S(1)}, bf16[256,1536]{1,0:T(8,128)(2,1)}, u32[]{:S(2)}, u32[]{:S(2)}) collective-permute-start(bf16[256,1536]{1,0:T(8,128)(2,1)S(1)} %get-tuple-element.83), channel_id=1, source_target_pairs={{0,2},{1,0},{2,3},{3,1},{4,6},{5,4},{6,7},{7,5},{8,10},{9,8},{10,1... | collective-permute-start | bytes 2359304 | tf_op jit(solution)/shard_map/ppermute | solution.py:322
  6.6 37.4 %collective-permute-start = (bf16[256,1536]{1,0:T(8,128)(2,1)S(1)}, bf16[256,1536]{1,0:T(8,128)(2,1)}, u32[]{:S(2)}, u32[]{:S(2)}) collective-permute-start(bf16[256,1536]{1,0:T(8,128)(2,1)S(1)} %get-tuple-element.82), channel_id=1, source_target_pairs={{0,0},{1,2},{2,1},{3,3},{4,4},{5,6},{6,5},{7,7},{8,8},{9,10},{10,9... | collective-permute-start | bytes 2359304 | tf_op jit(solution)/shard_map/ppermute | solution.py:321
  61.2 16.9 %collective-permute-start.14 = (bf16[96,3072]{1,0:T(8,128)(2,1)}, bf16[96,3072]{1,0:T(8,128)(2,1)S(1)}, u32[]{:S(2)}, u32[]{:S(2)}) collective-permute-start(bf16[96,3072]{1,0:T(8,128)(2,1)} %fusion.27), channel_id=1, source_target_pairs={{0,6},{2,4},{4,2},{6,0},{1,7},{3,5},{5,3},{7,1},{8,14},{10,12},{12... | collective-permute-start | bytes 1769480 | tf_op jit(solution)/shard_map/ppermute | solution.py:248
  64.2 57.2 %collective-permute-start.7 = (bf16[512,1536]{1,0:T(8,128)(2,1)}, bf16[512,1536]{1,0:T(8,128)(2,1)}, u32[]{:S(2)}, u32[]{:S(2)}) collective-permute-start(bf16[512,1536]{1,0:T(8,128)(2,1)} %pad_maximum_fusion.6), channel_id=1, source_target_pairs={{0,1},{1,0},{2,3},{3,2},{4,5},{5,4},{6,7},{7,6},{8,9},{9,8},{10,11... | collective-permute-start | bytes 4718600 | tf_op jit(solution)/shard_map/ppermute | solution.py:252
  64.3 21.5 %collective-permute-start.9 = (bf16[240,768]{1,0:T(8,128)(2,1)}, bf16[240,768]{1,0:T(8,128)(2,1)S(1)}, u32[]{:S(2)}, u32[]{:S(2)}) collective-permute-start(bf16[240,768]{1,0:T(8,128)(2,1)} %collective-permute-done.8), channel_id=1, source_target_pairs={{0,8},{8,16},{16,24},{24,0},{1,9},{9,17},{17,25},{25,1},{2,10},{10... | collective-permute-start | bytes 1105928 | tf_op jit(solution)/shard_map/ppermute | solution.py:176
  66.3 15.4 %collective-permute-start.10 = (bf16[240,768]{1,0:T(8,128)(2,1)}, bf16[240,768]{1,0:T(8,128)(2,1)S(1)}, u32[]{:S(2)}, u32[]{:S(2)}) collective-permute-start(bf16[240,768]{1,0:T(8,128)(2,1)} %collective-permute-done.8), channel_id=1, source_target_pairs={{0,24},{8,0},{16,8},{24,16},{1,25},{9,1},{17,9},{25,17},{2,26},{10... | collective-permute-start | bytes 1105928 | tf_op jit(solution)/shard_map/ppermute | solution.py:176
  78.2 19.1 %collective-permute-start.15 = (bf16[96,3072]{1,0:T(8,128)(2,1)S(1)}, bf16[96,3072]{1,0:T(8,128)(2,1)S(1)}, u32[]{:S(2)}, u32[]{:S(2)}) collective-permute-start(bf16[96,3072]{1,0:T(8,128)(2,1)S(1)} %collective-permute-done.14), channel_id=1, source_target_pairs={{0,32},{32,64},{64,96},{96,0},{1,33},{33,65},{65,97},{97,1},{2,34}... | collective-permute-start | bytes 1769480 | tf_op jit(solution)/shard_map/ppermute | solution.py:176
  79.6 15.5 %collective-permute-start.16 = (bf16[96,3072]{1,0:T(8,128)(2,1)S(1)}, bf16[96,3072]{1,0:T(8,128)(2,1)S(1)}, u32[]{:S(2)}, u32[]{:S(2)}) collective-permute-start(bf16[96,3072]{1,0:T(8,128)(2,1)S(1)} %collective-permute-done.14), channel_id=1, source_target_pairs={{0,96},{32,0},{64,32},{96,64},{1,97},{33,1},{65,33},{97,65},{2,98}... | collective-permute-start | bytes 1769480 | tf_op jit(solution)/shard_map/ppermute | solution.py:176
  94.7 54.1 %collective-permute-start.13 = (bf16[1920,768]{1,0:T(8,128)(2,1)}, bf16[1920,768]{1,0:T(8,128)(2,1)}, u32[]{:S(2)}, u32[]{:S(2)}) collective-permute-start(bf16[1920,768]{1,0:T(8,128)(2,1)} %pad_maximum_fusion.2), channel_id=1, source_target_pairs={{0,1},{1,0},{2,3},{3,2},{4,5},{5,4},{6,7},{7,6},{8,9},{9,8},{10,11... | collective-permute-start | bytes 8847368 | tf_op jit(solution)/shard_map/ppermute | solution.py:252
  109.5 57.3 %collective-permute-start.19 = (bf16[768,3072]{1,0:T(8,128)(2,1)}, bf16[768,3072]{1,0:T(8,128)(2,1)}, u32[]{:S(2)}, u32[]{:S(2)}) collective-permute-start(bf16[768,3072]{1,0:T(8,128)(2,1)} %pad_maximum_fusion), channel_id=1, source_target_pairs={{0,1},{1,0},{2,3},{3,2},{4,5},{5,4},{6,7},{7,6},{8,9},{9,8},{10,11... | collective-permute-start | bytes 14155784 | tf_op jit(solution)/shard_map/ppermute | solution.py:252
  249.8 45.1 %collective-permute-start.20 = (f32[512,1536]{1,0:T(8,128)}, f32[512,1536]{1,0:T(8,128)}, u32[]{:S(2)}, u32[]{:S(2)}) collective-permute-start(f32[512,1536]{1,0:T(8,128)} %slice.390), channel_id=1, source_target_pairs={{0,1},{1,0},{2,3},{3,2},{4,5},{5,4},{6,7},{7,6},{8,9},{9,8},{10,11... | collective-permute-start | bytes 9437192 | tf_op jit(solution)/shard_map/ppermute | solution.py:252
  327.0 15.0 %collective-permute-start.23 = (bf16[6144,768]{1,0:T(8,128)(2,1)}, bf16[6144,768]{1,0:T(8,128)(2,1)}, u32[]{:S(2)}, u32[]{:S(2)}) collective-permute-start(bf16[6144,768]{1,0:T(8,128)(2,1)} %get-tuple-element.55), channel_id=1, source_target_pairs={{0,1},{1,0},{2,3},{3,2},{4,5},{5,4},{6,7},{7,6},{8,9},{9,8},{10,11... | collective-permute-start | bytes 28311560 | tf_op jit(solution)/shard_map/ppermute | solution.py:252
  355.4 54.6 %collective-permute-start.24 = (bf16[2,2,768,384]{3,2,1,0:T(8,128)(2,1)S(1)}, bf16[2,2,768,384]{3,2,1,0:T(8,128)(2,1)S(1)}, u32[]{:S(2)}, u32[]{:S(2)}) collective-permute-start(bf16[2,2,768,384]{3,2,1,0:T(8,128)(2,1)S(1)} %pad_maximum_fusion.3), channel_id=1, source_target_pairs={{0,32},{32,64},{64,96},{96,0},{1,33},{33,65},{65,97},{97,1},{2,34}... | collective-permute-start | bytes 7077896 | tf_op jit(solution)/shard_map/ppermute | solution.py:176
  357.7 54.1 %collective-permute-start.25 = (bf16[2,2,768,384]{3,2,1,0:T(8,128)(2,1)}, bf16[2,2,768,384]{3,2,1,0:T(8,128)(2,1)}, u32[]{:S(2)}, u32[]{:S(2)}) collective-permute-start(bf16[2,2,768,384]{3,2,1,0:T(8,128)(2,1)} %pad_maximum_fusion.4), channel_id=1, source_target_pairs={{0,96},{32,0},{64,32},{96,64},{1,97},{33,1},{65,33},{97,65},{2,98}... | collective-permute-start | bytes 7077896 | tf_op jit(solution)/shard_map/ppermute | solution.py:176
  411.8 28.7 %collective-permute-start.27 = (bf16[2,768,384]{2,1,0:T(8,128)(2,1)}, bf16[2,768,384]{2,1,0:T(8,128)(2,1)}, u32[]{:S(2)}, u32[]{:S(2)}) collective-permute-start(bf16[2,768,384]{2,1,0:T(8,128)(2,1)} %fusion.4), channel_id=1, source_target_pairs={{0,32},{32,64},{64,96},{96,0},{1,33},{33,65},{65,97},{97,1},{2,34}... | collective-permute-start | bytes 3538952 | tf_op jit(solution)/shard_map/ppermute | solution.py:176
  446.2 26.6 %collective-permute-start.26 = (bf16[2,768,384]{2,1,0:T(8,128)(2,1)}, bf16[2,768,384]{2,1,0:T(8,128)(2,1)}, u32[]{:S(2)}, u32[]{:S(2)}) collective-permute-start(bf16[2,768,384]{2,1,0:T(8,128)(2,1)} %get-tuple-element.34), channel_id=1, source_target_pairs={{0,96},{32,0},{64,32},{96,64},{1,97},{33,1},{65,33},{97,65},{2,98}... | collective-permute-start | bytes 3538952 | tf_op jit(solution)/shard_map/ppermute | solution.py:176
  479.4 13.9 %collective-permute-start.28 = (bf16[2,2,192,384]{3,2,1,0:T(8,128)(2,1)S(1)}, bf16[2,2,192,384]{3,2,1,0:T(8,128)(2,1)S(1)}, u32[]{:S(2)}, u32[]{:S(2)}) collective-permute-start(bf16[2,2,192,384]{3,2,1,0:T(8,128)(2,1)S(1)} %pad_maximum_fusion.13), channel_id=1, source_target_pairs={{0,8},{8,16},{16,24},{24,0},{1,9},{9,17},{17,25},{25,1},{2,10},{10... | collective-permute-start | bytes 1769480 | tf_op jit(solution)/shard_map/ppermute | solution.py:176
  531.8 27.8 %collective-permute-start.39 = (bf16[768,768]{1,0:T(8,128)(2,1)S(1)}, bf16[768,768]{1,0:T(8,128)(2,1)S(1)}, u32[]{:S(2)}, u32[]{:S(2)}) collective-permute-start(bf16[768,768]{1,0:T(8,128)(2,1)S(1)} %maximum_dynamic-update-slice_fusion.3), channel_id=1, source_target_pairs={{0,32},{32,64},{64,96},{96,0},{1,33},{33,65},{65,97},{97,1},{2,34}... | collective-permute-start | bytes 3538952 | tf_op jit(solution)/shard_map/ppermute | solution.py:176
  531.8 22.7 %collective-permute-start.40 = (bf16[768,768]{1,0:T(8,128)(2,1)S(1)}, bf16[768,768]{1,0:T(8,128)(2,1)}, u32[]{:S(2)}, u32[]{:S(2)}) collective-permute-start(bf16[768,768]{1,0:T(8,128)(2,1)S(1)} %maximum_dynamic-update-slice_fusion.3), channel_id=1, source_target_pairs={{0,96},{32,0},{64,32},{96,64},{1,97},{33,1},{65,33},{97,65},{2,98}... | collective-permute-start | bytes 3538952 | tf_op jit(solution)/shard_map/ppermute | solution.py:176
  536.2 13.8 %collective-permute-start.22 = (bf16[256,1536]{1,0:T(8,128)(2,1)}, bf16[256,1536]{1,0:T(8,128)(2,1)}, u32[]{:S(2)}, u32[]{:S(2)}) collective-permute-start(bf16[256,1536]{1,0:T(8,128)(2,1)} %get-tuple-element.81), channel_id=1, source_target_pairs={{2,0},{0,1},{3,2},{1,3},{6,4},{4,5},{7,6},{5,7},{10,8},{8,9},{11,1... | collective-permute-start | bytes 2359304 | tf_op jit(solution)/shard_map/ppermute | solution.py:333
  536.2 13.8 %collective-permute-start.21 = (bf16[256,1536]{1,0:T(8,128)(2,1)S(1)}, bf16[256,1536]{1,0:T(8,128)(2,1)}, u32[]{:S(2)}, u32[]{:S(2)}) collective-permute-start(bf16[256,1536]{1,0:T(8,128)(2,1)S(1)} %get-tuple-element.80), channel_id=1, source_target_pairs={{0,0},{1,2},{2,1},{3,3},{4,4},{5,6},{6,5},{7,7},{8,8},{9,10},{10,9... | collective-permute-start | bytes 2359304 | tf_op jit(solution)/shard_map/ppermute | solution.py:332
  555.6 15.7 %collective-permute-start.42 = (bf16[384,768]{1,0:T(8,128)(2,1)S(1)}, bf16[384,768]{1,0:T(8,128)(2,1)S(1)}, u32[]{:S(2)}, u32[]{:S(2)}) collective-permute-start(bf16[384,768]{1,0:T(8,128)(2,1)S(1)} %slice.420), channel_id=1, source_target_pairs={{0,96},{32,0},{64,32},{96,64},{1,97},{33,1},{65,33},{97,65},{2,98}... | collective-permute-start | bytes 1769480 | tf_op jit(solution)/shard_map/ppermute | solution.py:176
  559.6 15.9 %collective-permute-start.41 = (bf16[384,768]{1,0:T(8,128)(2,1)S(1)}, bf16[384,768]{1,0:T(8,128)(2,1)S(1)}, u32[]{:S(2)}, u32[]{:S(2)}) collective-permute-start(bf16[384,768]{1,0:T(8,128)(2,1)S(1)} %slice.419), channel_id=1, source_target_pairs={{0,32},{32,64},{64,96},{96,0},{1,33},{33,65},{65,97},{97,1},{2,34}... | collective-permute-start | bytes 1769480 | tf_op jit(solution)/shard_map/ppermute | solution.py:176
  (88 other events, 717.7 us)

commit v2 on v1

--- a/solution.py
+++ b/solution.py
@@ -295,14 +295,19 @@
         [jnp.concatenate([shard(w, 0) for w in grads]), jnp.concatenate([shard(w, 2) for w in grads])]
     )
     pair = kept.astype(jnp.float32) + got.reshape(2, total, -1).astype(jnp.float32)
-    pair = ring_reduce(pair, "y", sizes["y"], 1, 2, direct)
-    pair = ring_reduce(pair, "z", sizes["z"], 1, 2, direct)
-    low = pair.astype(jnp.bfloat16)
+    ny, nz = sizes["y"], sizes["z"]
+    rows = pair.shape[1]
+    own = ring_reduce(pair[0], "y", ny, 0, 1, direct)
+    own = ring_reduce(own, "z", nz, 0, 1, direct)
+    oth = ring_reduce(pair[1].reshape(ny, rows // ny, -1), "z", nz, 1, 2, direct)
+    oth = ring_reduce(oth, "y", ny, 0, 2, direct).reshape(own.shape)
+    low_own = own.astype(jnp.bfloat16)
+    low_oth = oth.astype(jnp.bfloat16)
     mine = (
-        pair[0]
-        + lax.ppermute(low[0], "xl", [(0, 1), (1, 0)]).astype(jnp.float32)
-        + cross(low[1]).astype(jnp.float32)
-        + lax.ppermute(low[1], "xh", [(0, 1), (1, 0)]).astype(jnp.float32)
+        own
+        + lax.ppermute(low_own, "xl", [(0, 1), (1, 0)]).astype(jnp.float32)
+        + cross(low_oth).astype(jnp.float32)
+        + lax.ppermute(low_oth, "xh", [(0, 1), (1, 0)]).astype(jnp.float32)
     )
     full = ring_gather(mine.astype(jnp.bfloat16), "z", sizes["z"], 0, direct)
     full = ring_gather(full, "y", sizes["y"], 0, direct)

time: 592 us -> 532 us (0.90)
  the two profiles are of different devices: /device:TPU:0 before, /device:TPU:1 now
where the time goes in v2:
time: 532 us; the launch traced here: 522 us
  waiting for transfers between devices  149 us (28%)
  local copies, waits for them, and re-layouts  114 us (21%)
  starting transfers between devices  80.7 us (15%)
  matrix products  71.7 us (13%)
  Pallas kernels  54.1 us (10%)
  other arithmetic  49.4 us (9%)
    ppermute x35, waiting for transfers between devices, shift(): return lax.ppermute(x, axis, [(i, (i + step) % n) for i in range(n)])  96.6 us
    ppermute x35, starting transfers between devices, shift(): return lax.ppermute(x, axis, [(i, (i + step) % n) for i in range(n)])  45.9 us
    pallas_call x1, Pallas kernels, attention_backward(): pl.pallas_call(attention_backward_kernel, grid=(pairs,), in_specs=[pl.Blo...  30.6 us
    unnamed x147, local copies, waits for them, and re-layouts  29.4 us
    dot_general x7, matrix products, contract_rows(): lax.dot_general(left, right, (((0,), (0,)), ((), ())), preferred_element_...  28.6 us
    dot_general x7, matrix products, matmul(): return jnp.dot(left, right, preferred_element_type=jnp.float32)  24.5 us
    pallas_call x1, Pallas kernels, attention_forward(): pl.pallas_call(attention_forward_kernel, grid=(pairs,), in_specs=[pl.Bloc...  23.4 us
    dynamic_update_slice x38, local copies, waits for them, and re-layouts, place(): return lax.dynamic_update_slice(buf, piece, start)  22.4 us
  transfers between devices with their start and end apart: 51, of which 25 were waited for; matrix products, arithmetic and copies ran while one was open for 23% of the time, Pallas kernels for 4%

profile of v2, /device:TPU:1, one launch (start us, length us, event | category | flops | bytes accessed | tf_op | source)
XLA Modules:
  0.0 521.8 jit_solution(8518349622058472575)
XLA Ops:
  12.9 14.7 %collective-permute-done.2 = bf16[144,768]{1,0:T(8,128)(2,1)S(1)} collective-permute-done((bf16[144,768]{1,0:T(8,128)(2,1)}, bf16[144,768]{1,0:T(8,128)(2,1)S(1)}, u32[]{:S(2)}, u32[]{:S(2)}) %collective-permute-start.2) | collective-permute-done | bytes 221216 | tf_op jit(solution)/shard_map/ppermute | solution.py:248
  34.9 5.6 %collective-permute-done.4 = bf16[144,768]{1,0:T(8,128)(2,1)S(1)} collective-permute-done((bf16[144,768]{1,0:T(8,128)(2,1)S(1)}, bf16[144,768]{1,0:T(8,128)(2,1)S(1)}, u32[]{:S(2)}, u32[]{:S(2)}) %collective-permute-start.4) | collective-permute-done | bytes 221216 | tf_op jit(solution)/shard_map/ppermute | solution.py:176
  98.9 6.9 %collective-permute-done.18 = bf16[48,3072]{1,0:T(8,128)(2,1)S(1)} collective-permute-done((bf16[48,3072]{1,0:T(8,128)(2,1)S(1)}, bf16[48,3072]{1,0:T(8,128)(2,1)S(1)}, u32[]{:S(2)}, u32[]{:S(2)}) %collective-permute-start.18) | collective-permute-done | bytes 294944 | tf_op jit(solution)/shard_map/ppermute | solution.py:176
  127.0 23.4 %shard_map.178 = (f32[512,768]{1,0:T(8,128)}, f32[6,512,2]{2,1,0:T(8,128)}) custom-call(bf16[512,768]{1,0:T(8,128)(2,1)} %copy.23.q_ref, bf16[1024,1536]{1,0:T(8,128)(2,1)} %pad_maximum_fusion.1.k_ref.v_ref, bf16[1024,1536]{1,0:T(8,128)(2,1)} %pad_maximum_fusion.1.k_ref.v_ref, s32[512,1]{1,0:T(8,128)} %iota_add_fusion.rq_ref, s32[512,1]{1,0:T(8,128)} %copy.24.sq_ref, ...), custom_call_target="tpu_custom_call" | custom-call | flops 1610612736 | bytes 5505024 | tf_op jit(solution)/shard_map/pallas_call | solution.py:118
  163.4 4.9 fusion.33
  181.4 7.4 %multiply_convert_fusion.1 = (bf16[512,3072]{1,0:T(8,128)(2,1)}, bf16[512,3072]{1,0:T(8,128)(2,1)}, bf16[512,3072]{1,0:T(8,128)(2,1)S(1)}) fusion(f32[512,3072]{1,0:T(8,128)S(1)} %fusion.87, f32[512,3072]{1,0:T(8,128)S(1)} %fusion.33, bf16[512,768]{1,0:T(8,128)(2,1)S(1)} %multiply_convert_fusion.2, bf16[768,3072]{1,0:T(8,128)(2,1)S(1)} %get-tuple-element.65), kind=kOutput, calls=%fused_computation.4 | convolution fusion | flops 2444230656 | bytes 27525120 | tf_op jit(solution)/shard_map/dot_general | solution.py:35
  191.8 5.1 multiply_reduce_fusion
  201.9 30.6 %shard_map.179 = (f32[512,768]{1,0:T(8,128)}, f32[1024,768]{1,0:T(8,128)}, f32[1024,768]{1,0:T(8,128)}) custom-call(bf16[512,768]{1,0:T(8,128)(2,1)} %copy.23.q_ref, bf16[1024,1536]{1,0:T(8,128)(2,1)} %pad_maximum_fusion.1.k_ref.v_ref, bf16[1024,1536]{1,0:T(8,128)(2,1)} %pad_maximum_fusion.1.k_ref.v_ref, bf16[512,768]{1,0:T(8,128)(2,1)} %convolution_convert_fusion.7.do_ref, ...), custom_call_target="tpu_custom_call" | custom-call | flops 4026531840 | bytes 12582912 | tf_op jit(solution)/shard_map/pallas_call | solution.py:147
  242.7 7.0 %convolution_convert_fusion.2 = bf16[768,3072]{1,0:T(8,128)(2,1)} fusion(bf16[512,768]{1,0:T(8,128)(2,1)} %copy-done.29, bf16[512,3072]{1,0:T(8,128)(2,1)} %get-tuple-element.36), kind=kOutput, calls=%fused_computation.8 | convolution fusion | flops 2418278400 | bytes 8650752 | tf_op jit(solution)/shard_map/dot_general | solution.py:39
  249.7 8.5 %reshape.372 = bf16[3072,768]{1,0:T(8,128)(2,1)} reshape(bf16[768,3072]{1,0:T(8,128)(2,1)} %convolution_convert_fusion.2) | data formatting | bytes 9437184 | tf_op jit(solution)/shard_map/reshape | solution.py:472
  258.2 7.0 %convolution_convert_fusion.1 = bf16[768,3072]{1,0:T(8,128)(2,1)} fusion(bf16[512,768]{1,0:T(8,128)(2,1)} %copy-done.29, bf16[512,3072]{1,0:T(8,128)(2,1)} %copy-done.53), kind=kOutput, calls=%fused_computation.7 | convolution fusion | flops 2418278400 | bytes 8650752 | tf_op jit(solution)/shard_map/dot_general | solution.py:39
  265.2 8.9 %reshape.373 = bf16[3072,768]{1,0:T(8,128)(2,1)} reshape(bf16[768,3072]{1,0:T(8,128)(2,1)} %convolution_convert_fusion.1) | data formatting | bytes 9437184 | tf_op jit(solution)/shard_map/reshape | solution.py:472
  277.8 6.8 %convolution_convert_fusion = bf16[3072,768]{1,0:T(8,128)(2,1)} fusion(bf16[512,3072]{1,0:T(8,128)(2,1)} %get-tuple-element.35, bf16[512,1536]{1,0:T(8,128)(2,1)S(1)} %maximum_select_fusion), kind=kOutput, calls=%fused_computation.6 | convolution fusion | flops 2418278400 | bytes 8650752 | tf_op jit(solution)/shard_map/dot_general | solution.py:39
  316.5 6.8 %add_convert_fusion.2 = bf16[512,768]{1,0:T(8,128)(2,1)} fusion(f32[512,768]{1,0:T(8,128)S(1)} %get-tuple-element.128, bf16[512,3072]{1,0:T(8,128)(2,1)} %get-tuple-element.35, bf16[3072,768]{1,0:T(8,128)(2,1)} %slice_dynamic-update-slice_fusion), kind=kOutput, calls=%fused_computation.63 | convolution fusion | flops 2416705536 | bytes 10223616 | tf_op jit(solution)/shard_map/dot_general | solution.py:35
  323.2 7.9 %collective-permute-done.23 = bf16[6144,768]{1,0:T(8,128)(2,1)} collective-permute-done((bf16[6144,768]{1,0:T(8,128)(2,1)}, bf16[6144,768]{1,0:T(8,128)(2,1)}, u32[]{:S(2)}, u32[]{:S(2)}) %collective-permute-start.23) | collective-permute-done | bytes 9437216 | tf_op jit(solution)/shard_map/ppermute | solution.py:252
  331.1 7.3 %convert_add_fusion = f32[2,3072,768]{2,1,0:T(8,128)S(1)} fusion(bf16[2,3072,768]{2,1,0:T(8,128)(2,1)} %bitcast.63, bf16[1,3072,768]{2,1,0:T(8,128)(2,1)} %bitcast.22, bf16[1,3072,768]{2,1,0:T(8,128)(2,1)} %bitcast.21), kind=kLoop, calls=%fused_computation | loop fusion | flops 18874368 | bytes 37748736 | tf_op jit(solution)/shard_map/add | solution.py:297
  338.4 7.2 %fusion.82 = (f32[1,3072,768]{2,1,0:T(8,128)}, f32[1,3072,768]{2,1,0:T(8,128)}) fusion(f32[2,3072,768]{2,1,0:T(8,128)S(1)} %convert_add_fusion), kind=kLoop, calls=%fused_computation.323 | loop fusion | bytes 37748736 | tf_op jit(solution)/shard_map/slice | solution.py:300
  360.6 20.0 %collective-permute-done.24 = bf16[2,768,384]{2,1,0:T(8,128)(2,1)S(1)} collective-permute-done((bf16[2,768,384]{2,1,0:T(8,128)(2,1)S(1)}, bf16[2,768,384]{2,1,0:T(8,128)(2,1)S(1)}, u32[]{:S(2)}, u32[]{:S(2)}) %collective-permute-start.24) | collective-permute-done | bytes 1179680 | tf_op jit(solution)/shard_map/ppermute | solution.py:176
  385.8 9.9 %collective-permute-done.27 = bf16[768,384]{1,0:T(8,128)(2,1)S(1)} collective-permute-done((bf16[768,384]{1,0:T(8,128)(2,1)S(1)}, bf16[768,384]{1,0:T(8,128)(2,1)S(1)}, u32[]{:S(2)}, u32[]{:S(2)}) %collective-permute-start.27) | collective-permute-done | bytes 589856 | tf_op jit(solution)/shard_map/ppermute | solution.py:176
  403.3 16.0 %collective-permute-done.29 = bf16[2,192,384]{2,1,0:T(8,128)(2,1)S(1)} collective-permute-done((bf16[2,192,384]{2,1,0:T(8,128)(2,1)S(1)}, bf16[2,192,384]{2,1,0:T(8,128)(2,1)S(1)}, u32[]{:S(2)}, u32[]{:S(2)}) %collective-permute-start.29) | collective-permute-done | bytes 294944 | tf_op jit(solution)/shard_map/ppermute | solution.py:176
  436.9 8.7 %collective-permute-done.42 = bf16[192,768]{1,0:T(8,128)(2,1)S(1)} collective-permute-done((bf16[192,768]{1,0:T(8,128)(2,1)S(1)}, bf16[192,768]{1,0:T(8,128)(2,1)S(1)}, u32[]{:S(2)}, u32[]{:S(2)}) %collective-permute-start.42) | collective-permute-done | bytes 294944 | tf_op jit(solution)/shard_map/ppermute | solution.py:310
  469.7 12.6 %collective-permute-start.21 = (bf16[256,1536]{1,0:T(8,128)(2,1)}, bf16[256,1536]{1,0:T(8,128)(2,1)}, u32[]{:S(2)}, u32[]{:S(2)}) collective-permute-start(bf16[256,1536]{1,0:T(8,128)(2,1)} %get-tuple-element.94), channel_id=1, source_target_pairs={{0,0},{1,2},{2,1},{3,3},{4,4},{5,6},{6,5},{7,7},{8,8},{9,10},{10,9... | collective-permute-start | bytes 2359304 | tf_op jit(solution)/shard_map/ppermute | solution.py:337
  482.4 16.5 %collective-permute-done.21 = bf16[256,1536]{1,0:T(8,128)(2,1)} collective-permute-done((bf16[256,1536]{1,0:T(8,128)(2,1)}, bf16[256,1536]{1,0:T(8,128)(2,1)}, u32[]{:S(2)}, u32[]{:S(2)}) %collective-permute-start.21) | collective-permute-done | bytes 786464 | tf_op jit(solution)/shard_map/ppermute | solution.py:337
  504.6 5.2 %collective-permute-done.50 = bf16[384,768]{1,0:T(8,128)(2,1)S(1)} collective-permute-done((bf16[384,768]{1,0:T(8,128)(2,1)S(1)}, bf16[384,768]{1,0:T(8,128)(2,1)S(1)}, u32[]{:S(2)}, u32[]{:S(2)}) %collective-permute-start.50) | collective-permute-done | bytes 589856 | tf_op jit(solution)/shard_map/ppermute | solution.py:176
  (417 shorter events, 263.9 us)
Async XLA Ops:
  2.6 25.1 %collective-permute-start.2 = (bf16[144,768]{1,0:T(8,128)(2,1)}, bf16[144,768]{1,0:T(8,128)(2,1)S(1)}, u32[]{:S(2)}, u32[]{:S(2)}) collective-permute-start(bf16[144,768]{1,0:T(8,128)(2,1)} %fusion.59), channel_id=1, source_target_pairs={{0,6},{2,4},{4,2},{6,0},{1,7},{3,5},{5,3},{7,1},{8,14},{10,12},{12... | collective-permute-start | bytes 663560 | tf_op jit(solution)/shard_map/ppermute | solution.py:248
  6.2 39.2 %collective-permute-start.1 = (bf16[256,1536]{1,0:T(8,128)(2,1)S(1)}, bf16[256,1536]{1,0:T(8,128)(2,1)}, u32[]{:S(2)}, u32[]{:S(2)}) collective-permute-start(bf16[256,1536]{1,0:T(8,128)(2,1)S(1)} %get-tuple-element.97), channel_id=1, source_target_pairs={{0,2},{1,0},{2,3},{3,1},{4,6},{5,4},{6,7},{7,5},{8,10},{9,8},{10,1... | collective-permute-start | bytes 2359304 | tf_op jit(solution)/shard_map/ppermute | solution.py:327
  7.2 38.1 %collective-permute-start = (bf16[256,1536]{1,0:T(8,128)(2,1)S(1)}, bf16[256,1536]{1,0:T(8,128)(2,1)}, u32[]{:S(2)}, u32[]{:S(2)}) collective-permute-start(bf16[256,1536]{1,0:T(8,128)(2,1)S(1)} %get-tuple-element.96), channel_id=1, source_target_pairs={{0,0},{1,2},{2,1},{3,3},{4,4},{5,6},{6,5},{7,7},{8,8},{9,10},{10,9... | collective-permute-start | bytes 2359304 | tf_op jit(solution)/shard_map/ppermute | solution.py:326
  63.0 16.1 %collective-permute-start.14 = (bf16[96,3072]{1,0:T(8,128)(2,1)}, bf16[96,3072]{1,0:T(8,128)(2,1)S(1)}, u32[]{:S(2)}, u32[]{:S(2)}) collective-permute-start(bf16[96,3072]{1,0:T(8,128)(2,1)} %fusion.25), channel_id=1, source_target_pairs={{0,6},{2,4},{4,2},{6,0},{1,7},{3,5},{5,3},{7,1},{8,14},{10,12},{12... | collective-permute-start | bytes 1769480 | tf_op jit(solution)/shard_map/ppermute | solution.py:248
  65.8 57.2 %collective-permute-start.7 = (bf16[512,1536]{1,0:T(8,128)(2,1)}, bf16[512,1536]{1,0:T(8,128)(2,1)}, u32[]{:S(2)}, u32[]{:S(2)}) collective-permute-start(bf16[512,1536]{1,0:T(8,128)(2,1)} %pad_maximum_fusion.4), channel_id=1, source_target_pairs={{0,1},{1,0},{2,3},{3,2},{4,5},{5,4},{6,7},{7,6},{8,9},{9,8},{10,11... | collective-permute-start | bytes 4718600 | tf_op jit(solution)/shard_map/ppermute | solution.py:252
  66.4 19.6 %collective-permute-start.9 = (bf16[240,768]{1,0:T(8,128)(2,1)}, bf16[240,768]{1,0:T(8,128)(2,1)S(1)}, u32[]{:S(2)}, u32[]{:S(2)}) collective-permute-start(bf16[240,768]{1,0:T(8,128)(2,1)} %collective-permute-done.8), channel_id=1, source_target_pairs={{0,8},{8,16},{16,24},{24,0},{1,9},{9,17},{17,25},{25,1},{2,10},{10... | collective-permute-start | bytes 1105928 | tf_op jit(solution)/shard_map/ppermute | solution.py:176
  79.0 18.8 %collective-permute-start.15 = (bf16[96,3072]{1,0:T(8,128)(2,1)S(1)}, bf16[96,3072]{1,0:T(8,128)(2,1)S(1)}, u32[]{:S(2)}, u32[]{:S(2)}) collective-permute-start(bf16[96,3072]{1,0:T(8,128)(2,1)S(1)} %collective-permute-done.14), channel_id=1, source_target_pairs={{0,32},{32,64},{64,96},{96,0},{1,33},{33,65},{65,97},{97,1},{2,34}... | collective-permute-start | bytes 1769480 | tf_op jit(solution)/shard_map/ppermute | solution.py:176
  80.3 16.8 %collective-permute-start.16 = (bf16[96,3072]{1,0:T(8,128)(2,1)S(1)}, bf16[96,3072]{1,0:T(8,128)(2,1)S(1)}, u32[]{:S(2)}, u32[]{:S(2)}) collective-permute-start(bf16[96,3072]{1,0:T(8,128)(2,1)S(1)} %collective-permute-done.14), channel_id=1, source_target_pairs={{0,96},{32,0},{64,32},{96,64},{1,97},{33,1},{65,33},{97,65},{2,98}... | collective-permute-start | bytes 1769480 | tf_op jit(solution)/shard_map/ppermute | solution.py:176
  93.9 56.5 %collective-permute-start.13 = (bf16[1920,768]{1,0:T(8,128)(2,1)}, bf16[1920,768]{1,0:T(8,128)(2,1)}, u32[]{:S(2)}, u32[]{:S(2)}) collective-permute-start(bf16[1920,768]{1,0:T(8,128)(2,1)} %pad_maximum_fusion.2), channel_id=1, source_target_pairs={{0,1},{1,0},{2,3},{3,2},{4,5},{5,4},{6,7},{7,6},{8,9},{9,8},{10,11... | collective-permute-start | bytes 8847368 | tf_op jit(solution)/shard_map/ppermute | solution.py:252
  109.1 59.3 %collective-permute-start.19 = (bf16[768,3072]{1,0:T(8,128)(2,1)}, bf16[768,3072]{1,0:T(8,128)(2,1)}, u32[]{:S(2)}, u32[]{:S(2)}) collective-permute-start(bf16[768,3072]{1,0:T(8,128)(2,1)} %pad_maximum_fusion), channel_id=1, source_target_pairs={{0,1},{1,0},{2,3},{3,2},{4,5},{5,4},{6,7},{7,6},{8,9},{9,8},{10,11... | collective-permute-start | bytes 14155784 | tf_op jit(solution)/shard_map/ppermute | solution.py:252
  239.4 45.2 %collective-permute-start.20 = (f32[512,1536]{1,0:T(8,128)}, f32[512,1536]{1,0:T(8,128)}, u32[]{:S(2)}, u32[]{:S(2)}) collective-permute-start(f32[512,1536]{1,0:T(8,128)} %slice.489), channel_id=1, source_target_pairs={{0,1},{1,0},{2,3},{3,2},{4,5},{5,4},{6,7},{7,6},{8,9},{9,8},{10,11... | collective-permute-start | bytes 9437192 | tf_op jit(solution)/shard_map/ppermute | solution.py:252
  315.9 15.2 %collective-permute-start.23 = (bf16[6144,768]{1,0:T(8,128)(2,1)}, bf16[6144,768]{1,0:T(8,128)(2,1)}, u32[]{:S(2)}, u32[]{:S(2)}) collective-permute-start(bf16[6144,768]{1,0:T(8,128)(2,1)} %get-tuple-element.57), channel_id=1, source_target_pairs={{0,1},{1,0},{2,3},{3,2},{4,5},{5,4},{6,7},{7,6},{8,9},{9,8},{10,11... | collective-permute-start | bytes 28311560 | tf_op jit(solution)/shard_map/ppermute | solution.py:252
  352.2 28.5 %collective-permute-start.24 = (bf16[2,768,384]{2,1,0:T(8,128)(2,1)S(1)}, bf16[2,768,384]{2,1,0:T(8,128)(2,1)S(1)}, u32[]{:S(2)}, u32[]{:S(2)}) collective-permute-start(bf16[2,768,384]{2,1,0:T(8,128)(2,1)S(1)} %pad_maximum_fusion.5), channel_id=1, source_target_pairs={{0,32},{32,64},{64,96},{96,0},{1,33},{33,65},{65,97},{97,1},{2,34}... | collective-permute-start | bytes 3538952 | tf_op jit(solution)/shard_map/ppermute | solution.py:176
  352.6 28.3 %collective-permute-start.25 = (bf16[2,768,384]{2,1,0:T(8,128)(2,1)S(1)}, bf16[2,768,384]{2,1,0:T(8,128)(2,1)S(1)}, u32[]{:S(2)}, u32[]{:S(2)}) collective-permute-start(bf16[2,768,384]{2,1,0:T(8,128)(2,1)S(1)} %pad_maximum_fusion.6), channel_id=1, source_target_pairs={{0,96},{32,0},{64,32},{96,64},{1,97},{33,1},{65,33},{97,65},{2,98}... | collective-permute-start | bytes 3538952 | tf_op jit(solution)/shard_map/ppermute | solution.py:176
  357.5 28.0 %collective-permute-start.33 = (bf16[2,4,192,384]{3,2,1,0:T(8,128)(2,1)S(1)}, bf16[2,4,192,384]{3,2,1,0:T(8,128)(2,1)S(1)}, u32[]{:S(2)}, u32[]{:S(2)}) collective-permute-start(bf16[2,4,192,384]{3,2,1,0:T(8,128)(2,1)S(1)} %pad_maximum_fusion.7), channel_id=1, source_target_pairs={{0,8},{8,16},{16,24},{24,0},{1,9},{9,17},{17,25},{25,1},{2,10},{10... | collective-permute-start | bytes 3538952 | tf_op jit(solution)/shard_map/ppermute | solution.py:176
  358.4 37.9 %collective-permute-start.34 = (bf16[2,4,192,384]{3,2,1,0:T(8,128)(2,1)S(1)}, bf16[2,4,192,384]{3,2,1,0:T(8,128)(2,1)S(1)}, u32[]{:S(2)}, u32[]{:S(2)}) collective-permute-start(bf16[2,4,192,384]{3,2,1,0:T(8,128)(2,1)S(1)} %pad_maximum_fusion.8), channel_id=1, source_target_pairs={{0,24},{8,0},{16,8},{24,16},{1,25},{9,1},{17,9},{25,17},{2,26},{10... | collective-permute-start | bytes 3538952 | tf_op jit(solution)/shard_map/ppermute | solution.py:176
  380.8 14.9 %collective-permute-start.27 = (bf16[768,384]{1,0:T(8,128)(2,1)S(1)}, bf16[768,384]{1,0:T(8,128)(2,1)S(1)}, u32[]{:S(2)}, u32[]{:S(2)}) collective-permute-start(bf16[768,384]{1,0:T(8,128)(2,1)S(1)} %fusion.13), channel_id=1, source_target_pairs={{0,32},{32,64},{64,96},{96,0},{1,33},{33,65},{65,97},{97,1},{2,34}... | collective-permute-start | bytes 1769480 | tf_op jit(solution)/shard_map/ppermute | solution.py:176
  400.5 20.8 %collective-permute-start.35 = (bf16[4,192,384]{2,1,0:T(8,128)(2,1)S(1)}, bf16[4,192,384]{2,1,0:T(8,128)(2,1)S(1)}, u32[]{:S(2)}, u32[]{:S(2)}) collective-permute-start(bf16[4,192,384]{2,1,0:T(8,128)(2,1)S(1)} %get-tuple-element.39), channel_id=1, source_target_pairs={{0,24},{8,0},{16,8},{24,16},{1,25},{9,1},{17,9},{25,17},{2,26},{10... | collective-permute-start | bytes 1769480 | tf_op jit(solution)/shard_map/ppermute | solution.py:176
  401.6 17.6 %collective-permute-start.29 = (bf16[2,192,384]{2,1,0:T(8,128)(2,1)S(1)}, bf16[2,192,384]{2,1,0:T(8,128)(2,1)S(1)}, u32[]{:S(2)}, u32[]{:S(2)}) collective-permute-start(bf16[2,192,384]{2,1,0:T(8,128)(2,1)S(1)} %pad_maximum_fusion.16), channel_id=1, source_target_pairs={{0,24},{8,0},{16,8},{24,16},{1,25},{9,1},{17,9},{25,17},{2,26},{10... | collective-permute-start | bytes 884744 | tf_op jit(solution)/shard_map/ppermute | solution.py:176
  401.9 21.6 %collective-permute-start.28 = (bf16[2,192,384]{2,1,0:T(8,128)(2,1)S(1)}, bf16[2,192,384]{2,1,0:T(8,128)(2,1)S(1)}, u32[]{:S(2)}, u32[]{:S(2)}) collective-permute-start(bf16[2,192,384]{2,1,0:T(8,128)(2,1)S(1)} %pad_maximum_fusion.15), channel_id=1, source_target_pairs={{0,8},{8,16},{16,24},{24,0},{1,9},{9,17},{17,25},{25,1},{2,10},{10... | collective-permute-start | bytes 884744 | tf_op jit(solution)/shard_map/ppermute | solution.py:176
  462.4 38.7 %collective-permute-start.47 = (bf16[768,768]{1,0:T(8,128)(2,1)S(1)}, bf16[768,768]{1,0:T(8,128)(2,1)S(1)}, u32[]{:S(2)}, u32[]{:S(2)}) collective-permute-start(bf16[768,768]{1,0:T(8,128)(2,1)S(1)} %maximum_dynamic-update-slice_fusion.3), channel_id=1, source_target_pairs={{0,32},{32,64},{64,96},{96,0},{1,33},{33,65},{65,97},{97,1},{2,34}... | collective-permute-start | bytes 3538952 | tf_op jit(solution)/shard_map/ppermute | solution.py:176
  462.5 38.5 %collective-permute-start.48 = (bf16[768,768]{1,0:T(8,128)(2,1)S(1)}, bf16[768,768]{1,0:T(8,128)(2,1)S(1)}, u32[]{:S(2)}, u32[]{:S(2)}) collective-permute-start(bf16[768,768]{1,0:T(8,128)(2,1)S(1)} %maximum_dynamic-update-slice_fusion.3), channel_id=1, source_target_pairs={{0,96},{32,0},{64,32},{96,64},{1,97},{33,1},{65,33},{97,65},{2,98}... | collective-permute-start | bytes 3538952 | tf_op jit(solution)/shard_map/ppermute | solution.py:176
  466.6 15.7 %collective-permute-start.22 = (bf16[256,1536]{1,0:T(8,128)(2,1)}, bf16[256,1536]{1,0:T(8,128)(2,1)}, u32[]{:S(2)}, u32[]{:S(2)}) collective-permute-start(bf16[256,1536]{1,0:T(8,128)(2,1)} %get-tuple-element.95), channel_id=1, source_target_pairs={{2,0},{0,1},{3,2},{1,3},{6,4},{4,5},{7,6},{5,7},{10,8},{8,9},{11,1... | collective-permute-start | bytes 2359304 | tf_op jit(solution)/shard_map/ppermute | solution.py:338
  469.7 29.1 %collective-permute-start.21 = (bf16[256,1536]{1,0:T(8,128)(2,1)}, bf16[256,1536]{1,0:T(8,128)(2,1)}, u32[]{:S(2)}, u32[]{:S(2)}) collective-permute-start(bf16[256,1536]{1,0:T(8,128)(2,1)} %get-tuple-element.94), channel_id=1, source_target_pairs={{0,0},{1,2},{2,1},{3,3},{4,4},{5,6},{6,5},{7,7},{8,8},{9,10},{10,9... | collective-permute-start | bytes 2359304 | tf_op jit(solution)/shard_map/ppermute | solution.py:337
  (93 other events, 952.5 us)

commit v3 on v2

--- a/solution.py
+++ b/solution.py
@@ -298,9 +298,9 @@
     ny, nz = sizes["y"], sizes["z"]
     rows = pair.shape[1]
     own = ring_reduce(pair[0], "y", ny, 0, 1, direct)
-    own = ring_reduce(own, "z", nz, 0, 1, direct)
+    own = ring_reduce(own, "z", nz, 0, 1, True)
     oth = ring_reduce(pair[1].reshape(ny, rows // ny, -1), "z", nz, 1, 2, direct)
-    oth = ring_reduce(oth, "y", ny, 0, 2, direct).reshape(own.shape)
+    oth = ring_reduce(oth, "y", ny, 0, 2, True).reshape(own.shape)
     low_own = own.astype(jnp.bfloat16)
     low_oth = oth.astype(jnp.bfloat16)
     mine = (
@@ -309,7 +309,7 @@
         + cross(low_oth).astype(jnp.float32)
         + lax.ppermute(low_oth, "xh", [(0, 1), (1, 0)]).astype(jnp.float32)
     )
-    full = ring_gather(mine.astype(jnp.bfloat16), "z", sizes["z"], 0, direct)
+    full = ring_gather(mine.astype(jnp.bfloat16), "z", sizes["z"], 0, True)
     full = ring_gather(full, "y", sizes["y"], 0, direct)
     out = []
     start = 0

time: 532 us -> 520 us (0.977)
  the two profiles are of different devices: /device:TPU:1 before, /device:TPU:0 now
where the time goes in v3:
time: 520 us; the launch traced here: 510 us
  waiting for transfers between devices  150 us (29%)
  local copies, waits for them, and re-layouts  117 us (22%)
  matrix products  71.6 us (14%)
  starting transfers between devices  66.8 us (13%)
  Pallas kernels  54.1 us (10%)
  other arithmetic  48.8 us (9%)
    ppermute x32, waiting for transfers between devices, shift(): return lax.ppermute(x, axis, [(i, (i + step) % n) for i in range(n)])  101 us
    ppermute x32, starting transfers between devices, shift(): return lax.ppermute(x, axis, [(i, (i + step) % n) for i in range(n)])  49.3 us
    pallas_call x1, Pallas kernels, attention_backward(): pl.pallas_call(attention_backward_kernel, grid=(pairs,), in_specs=[pl.Blo...  30.7 us
    unnamed x147, local copies, waits for them, and re-layouts  29.5 us
    dot_general x7, matrix products, contract_rows(): lax.dot_general(left, right, (((0,), (0,)), ((), ())), preferred_element_...  28.5 us
    ppermute x4, waiting for transfers between devices, cross(): return lax.ppermute(x, ('xl', 'xh'), [(i, 3 - i) for i in range(4)])  27 us
    dot_general x7, matrix products, matmul(): return jnp.dot(left, right, preferred_element_type=jnp.float32)  24.5 us
    pallas_call x1, Pallas kernels, attention_forward(): pl.pallas_call(attention_forward_kernel, grid=(pairs,), in_specs=[pl.Bloc...  23.4 us
  transfers between devices with their start and end apart: 48, of which 27 were waited for; matrix products, arithmetic and copies ran while one was open for 25% of the time, Pallas kernels for 5%

profile of v3, /device:TPU:0, one launch (start us, length us, event | category | flops | bytes accessed | tf_op | source)
XLA Modules:
  0.0 509.9 jit_solution(13723919640630404146)
XLA Ops:
  11.3 16.6 %collective-permute-done.2 = bf16[144,768]{1,0:T(8,128)(2,1)S(1)} collective-permute-done((bf16[144,768]{1,0:T(8,128)(2,1)}, bf16[144,768]{1,0:T(8,128)(2,1)S(1)}, u32[]{:S(2)}, u32[]{:S(2)}) %collective-permute-start.2) | collective-permute-done | bytes 221216 | tf_op jit(solution)/shard_map/ppermute | solution.py:248
  98.2 7.0 %collective-permute-done.18 = bf16[48,3072]{1,0:T(8,128)(2,1)S(1)} collective-permute-done((bf16[48,3072]{1,0:T(8,128)(2,1)S(1)}, bf16[48,3072]{1,0:T(8,128)(2,1)S(1)}, u32[]{:S(2)}, u32[]{:S(2)}) %collective-permute-start.18) | collective-permute-done | bytes 294944 | tf_op jit(solution)/shard_map/ppermute | solution.py:176
  125.6 23.4 %shard_map.178 = (f32[512,768]{1,0:T(8,128)}, f32[6,512,2]{2,1,0:T(8,128)}) custom-call(bf16[512,768]{1,0:T(8,128)(2,1)} %copy.23.q_ref, bf16[1024,1536]{1,0:T(8,128)(2,1)} %pad_maximum_fusion.1.k_ref.v_ref, bf16[1024,1536]{1,0:T(8,128)(2,1)} %pad_maximum_fusion.1.k_ref.v_ref, s32[512,1]{1,0:T(8,128)} %iota_add_fusion.rq_ref, s32[512,1]{1,0:T(8,128)} %copy.24.sq_ref, ...), custom_call_target="tpu_custom_call" | custom-call | flops 1610612736 | bytes 5505024 | tf_op jit(solution)/shard_map/pallas_call | solution.py:118
  180.1 7.4 %multiply_convert_fusion.1 = (bf16[512,3072]{1,0:T(8,128)(2,1)}, bf16[512,3072]{1,0:T(8,128)(2,1)}, bf16[512,3072]{1,0:T(8,128)(2,1)S(1)}) fusion(f32[512,3072]{1,0:T(8,128)S(1)} %fusion.78, f32[512,3072]{1,0:T(8,128)S(1)} %fusion.48, bf16[512,768]{1,0:T(8,128)(2,1)S(1)} %multiply_convert_fusion.2, bf16[768,3072]{1,0:T(8,128)(2,1)S(1)} %get-tuple-element.67), kind=kOutput, calls=%fused_computation.4 | convolution fusion | flops 2444230656 | bytes 27525120 | tf_op jit(solution)/shard_map/dot_general | solution.py:35
  190.5 5.1 multiply_reduce_fusion
  200.6 30.7 %shard_map.179 = (f32[512,768]{1,0:T(8,128)}, f32[1024,768]{1,0:T(8,128)}, f32[1024,768]{1,0:T(8,128)}) custom-call(bf16[512,768]{1,0:T(8,128)(2,1)} %copy.23.q_ref, bf16[1024,1536]{1,0:T(8,128)(2,1)} %pad_maximum_fusion.1.k_ref.v_ref, bf16[1024,1536]{1,0:T(8,128)(2,1)} %pad_maximum_fusion.1.k_ref.v_ref, bf16[512,768]{1,0:T(8,128)(2,1)} %convolution_convert_fusion.7.do_ref, ...), custom_call_target="tpu_custom_call" | custom-call | flops 4026531840 | bytes 12582912 | tf_op jit(solution)/shard_map/pallas_call | solution.py:147
  241.8 7.0 %convolution_convert_fusion.2 = bf16[768,3072]{1,0:T(8,128)(2,1)} fusion(bf16[512,768]{1,0:T(8,128)(2,1)} %copy-done.29, bf16[512,3072]{1,0:T(8,128)(2,1)} %get-tuple-element.38), kind=kOutput, calls=%fused_computation.8 | convolution fusion | flops 2418278400 | bytes 8650752 | tf_op jit(solution)/shard_map/dot_general | solution.py:39
  248.8 8.5 %reshape.232 = bf16[3072,768]{1,0:T(8,128)(2,1)} reshape(bf16[768,3072]{1,0:T(8,128)(2,1)} %convolution_convert_fusion.2) | data formatting | bytes 9437184 | tf_op jit(solution)/shard_map/reshape | solution.py:472
  257.3 7.0 %convolution_convert_fusion.1 = bf16[768,3072]{1,0:T(8,128)(2,1)} fusion(bf16[512,768]{1,0:T(8,128)(2,1)} %copy-done.29, bf16[512,3072]{1,0:T(8,128)(2,1)} %copy-done.53), kind=kOutput, calls=%fused_computation.7 | convolution fusion | flops 2418278400 | bytes 8650752 | tf_op jit(solution)/shard_map/dot_general | solution.py:39
  264.2 8.8 %reshape.233 = bf16[3072,768]{1,0:T(8,128)(2,1)} reshape(bf16[768,3072]{1,0:T(8,128)(2,1)} %convolution_convert_fusion.1) | data formatting | bytes 9437184 | tf_op jit(solution)/shard_map/reshape | solution.py:472
  276.8 6.8 %convolution_convert_fusion = bf16[3072,768]{1,0:T(8,128)(2,1)} fusion(bf16[512,3072]{1,0:T(8,128)(2,1)} %get-tuple-element.37, bf16[512,1536]{1,0:T(8,128)(2,1)S(1)} %maximum_select_fusion), kind=kOutput, calls=%fused_computation.6 | convolution fusion | flops 2418278400 | bytes 8650752 | tf_op jit(solution)/shard_map/dot_general | solution.py:39
  315.3 6.8 %add_convert_fusion.2 = bf16[512,768]{1,0:T(8,128)(2,1)} fusion(f32[512,768]{1,0:T(8,128)S(1)} %get-tuple-element.122, bf16[512,3072]{1,0:T(8,128)(2,1)} %get-tuple-element.37, bf16[3072,768]{1,0:T(8,128)(2,1)} %slice_dynamic-update-slice_fusion), kind=kOutput, calls=%fused_computation.59 | convolution fusion | flops 2416705536 | bytes 10223616 | tf_op jit(solution)/shard_map/dot_general | solution.py:35
  322.0 8.0 %collective-permute-done.23 = bf16[6144,768]{1,0:T(8,128)(2,1)} collective-permute-done((bf16[6144,768]{1,0:T(8,128)(2,1)}, bf16[6144,768]{1,0:T(8,128)(2,1)}, u32[]{:S(2)}, u32[]{:S(2)}) %collective-permute-start.23) | collective-permute-done | bytes 9437216 | tf_op jit(solution)/shard_map/ppermute | solution.py:252
  330.0 7.3 %convert_add_fusion = f32[2,3072,768]{2,1,0:T(8,128)S(1)} fusion(bf16[2,3072,768]{2,1,0:T(8,128)(2,1)} %bitcast.47, bf16[1,3072,768]{2,1,0:T(8,128)(2,1)} %bitcast.22, bf16[1,3072,768]{2,1,0:T(8,128)(2,1)} %bitcast.21), kind=kLoop, calls=%fused_computation | loop fusion | flops 18874368 | bytes 37748736 | tf_op jit(solution)/shard_map/add | solution.py:297
  337.3 7.1 %fusion.73 = (f32[1,3072,768]{2,1,0:T(8,128)}, f32[1,3072,768]{2,1,0:T(8,128)}) fusion(f32[2,3072,768]{2,1,0:T(8,128)S(1)} %convert_add_fusion), kind=kLoop, calls=%fused_computation.283 | loop fusion | bytes 37748736 | tf_op jit(solution)/shard_map/slice | solution.py:300
  362.1 14.7 %collective-permute-done.32 = bf16[2,4,192,384]{3,2,1,0:T(8,128)(2,1)S(1)} collective-permute-done((bf16[2,4,192,384]{3,2,1,0:T(8,128)(2,1)S(1)}, bf16[2,4,192,384]{3,2,1,0:T(8,128)(2,1)S(1)}, u32[]{:S(2)}, u32[]{:S(2)}) %collective-permute-start.32) | collective-permute-done | bytes 1179680 | tf_op jit(solution)/shard_map/ppermute | solution.py:176
  377.9 6.1 %collective-permute-done.24 = bf16[2,768,384]{2,1,0:T(8,128)(2,1)S(1)} collective-permute-done((bf16[2,768,384]{2,1,0:T(8,128)(2,1)S(1)}, bf16[2,768,384]{2,1,0:T(8,128)(2,1)S(1)}, u32[]{:S(2)}, u32[]{:S(2)}) %collective-permute-start.24) | collective-permute-done | bytes 1179680 | tf_op jit(solution)/shard_map/ppermute | solution.py:176
  387.6 5.2 %collective-permute-done.35 = bf16[4,192,384]{2,1,0:T(8,128)(2,1)S(1)} collective-permute-done((bf16[4,192,384]{2,1,0:T(8,128)(2,1)S(1)}, bf16[4,192,384]{2,1,0:T(8,128)(2,1)S(1)}, u32[]{:S(2)}, u32[]{:S(2)}) %collective-permute-start.35) | collective-permute-done | bytes 589856 | tf_op jit(solution)/shard_map/ppermute | solution.py:176
  432.6 5.4 %collective-permute-done.39 = bf16[192,768]{1,0:T(8,128)(2,1)S(1)} collective-permute-done((bf16[192,768]{1,0:T(8,128)(2,1)S(1)}, bf16[192,768]{1,0:T(8,128)(2,1)S(1)}, u32[]{:S(2)}, u32[]{:S(2)}) %collective-permute-start.39) | collective-permute-done | bytes 294944 | tf_op jit(solution)/shard_map/ppermute | solution.py:248
  442.8 11.3 %collective-permute-done.41 = bf16[192,768]{1,0:T(8,128)(2,1)S(1)} collective-permute-done((bf16[192,768]{1,0:T(8,128)(2,1)S(1)}, bf16[192,768]{1,0:T(8,128)(2,1)S(1)}, u32[]{:S(2)}, u32[]{:S(2)}) %collective-permute-start.41) | collective-permute-done | bytes 294944 | tf_op jit(solution)/shard_map/ppermute | solution.py:176
  459.4 7.4 %collective-permute-start.21 = (bf16[256,1536]{1,0:T(8,128)(2,1)}, bf16[256,1536]{1,0:T(8,128)(2,1)}, u32[]{:S(2)}, u32[]{:S(2)}) collective-permute-start(bf16[256,1536]{1,0:T(8,128)(2,1)} %get-tuple-element.92), channel_id=1, source_target_pairs={{0,0},{1,2},{2,1},{3,3},{4,4},{5,6},{6,5},{7,7},{8,8},{9,10},{10,9... | collective-permute-start | bytes 2359304 | tf_op jit(solution)/shard_map/ppermute | solution.py:337
  466.8 6.4 %collective-permute-done.22 = bf16[256,1536]{1,0:T(8,128)(2,1)} collective-permute-done((bf16[256,1536]{1,0:T(8,128)(2,1)}, bf16[256,1536]{1,0:T(8,128)(2,1)}, u32[]{:S(2)}, u32[]{:S(2)}) %collective-permute-start.22) | collective-permute-done | bytes 786464 | tf_op jit(solution)/shard_map/ppermute | solution.py:338
  475.3 6.1 %collective-permute-done.45 = bf16[768,768]{1,0:T(8,128)(2,1)S(1)} collective-permute-done((bf16[768,768]{1,0:T(8,128)(2,1)S(1)}, bf16[768,768]{1,0:T(8,128)(2,1)S(1)}, u32[]{:S(2)}, u32[]{:S(2)}) %collective-permute-start.45) | collective-permute-done | bytes 1179680 | tf_op jit(solution)/shard_map/ppermute | solution.py:176
  487.3 9.5 %collective-permute-done.47 = bf16[384,768]{1,0:T(8,128)(2,1)S(1)} collective-permute-done((bf16[384,768]{1,0:T(8,128)(2,1)S(1)}, bf16[384,768]{1,0:T(8,128)(2,1)S(1)}, u32[]{:S(2)}, u32[]{:S(2)}) %collective-permute-start.47) | collective-permute-done | bytes 589856 | tf_op jit(solution)/shard_map/ppermute | solution.py:176
  (393 shorter events, 277.9 us)
Async XLA Ops:
  2.6 25.3 %collective-permute-start.2 = (bf16[144,768]{1,0:T(8,128)(2,1)}, bf16[144,768]{1,0:T(8,128)(2,1)S(1)}, u32[]{:S(2)}, u32[]{:S(2)}) collective-permute-start(bf16[144,768]{1,0:T(8,128)(2,1)} %fusion.56), channel_id=1, source_target_pairs={{0,6},{2,4},{4,2},{6,0},{1,7},{3,5},{5,3},{7,1},{8,14},{10,12},{12... | collective-permute-start | bytes 663560 | tf_op jit(solution)/shard_map/ppermute | solution.py:248
  5.7 38.2 %collective-permute-start.1 = (bf16[256,1536]{1,0:T(8,128)(2,1)S(1)}, bf16[256,1536]{1,0:T(8,128)(2,1)}, u32[]{:S(2)}, u32[]{:S(2)}) collective-permute-start(bf16[256,1536]{1,0:T(8,128)(2,1)S(1)} %get-tuple-element.95), channel_id=1, source_target_pairs={{0,2},{1,0},{2,3},{3,1},{4,6},{5,4},{6,7},{7,5},{8,10},{9,8},{10,1... | collective-permute-start | bytes 2359304 | tf_op jit(solution)/shard_map/ppermute | solution.py:327
  6.6 37.4 %collective-permute-start = (bf16[256,1536]{1,0:T(8,128)(2,1)S(1)}, bf16[256,1536]{1,0:T(8,128)(2,1)}, u32[]{:S(2)}, u32[]{:S(2)}) collective-permute-start(bf16[256,1536]{1,0:T(8,128)(2,1)S(1)} %get-tuple-element.94), channel_id=1, source_target_pairs={{0,0},{1,2},{2,1},{3,3},{4,4},{5,6},{6,5},{7,7},{8,8},{9,10},{10,9... | collective-permute-start | bytes 2359304 | tf_op jit(solution)/shard_map/ppermute | solution.py:326
  61.9 16.9 %collective-permute-start.14 = (bf16[96,3072]{1,0:T(8,128)(2,1)}, bf16[96,3072]{1,0:T(8,128)(2,1)S(1)}, u32[]{:S(2)}, u32[]{:S(2)}) collective-permute-start(bf16[96,3072]{1,0:T(8,128)(2,1)} %fusion.25), channel_id=1, source_target_pairs={{0,6},{2,4},{4,2},{6,0},{1,7},{3,5},{5,3},{7,1},{8,14},{10,12},{12... | collective-permute-start | bytes 1769480 | tf_op jit(solution)/shard_map/ppermute | solution.py:248
  65.0 56.6 %collective-permute-start.7 = (bf16[512,1536]{1,0:T(8,128)(2,1)}, bf16[512,1536]{1,0:T(8,128)(2,1)}, u32[]{:S(2)}, u32[]{:S(2)}) collective-permute-start(bf16[512,1536]{1,0:T(8,128)(2,1)} %pad_maximum_fusion.4), channel_id=1, source_target_pairs={{0,1},{1,0},{2,3},{3,2},{4,5},{5,4},{6,7},{7,6},{8,9},{9,8},{10,11... | collective-permute-start | bytes 4718600 | tf_op jit(solution)/shard_map/ppermute | solution.py:252
  65.0 21.5 %collective-permute-start.9 = (bf16[240,768]{1,0:T(8,128)(2,1)}, bf16[240,768]{1,0:T(8,128)(2,1)S(1)}, u32[]{:S(2)}, u32[]{:S(2)}) collective-permute-start(bf16[240,768]{1,0:T(8,128)(2,1)} %collective-permute-done.8), channel_id=1, source_target_pairs={{0,8},{8,16},{16,24},{24,0},{1,9},{9,17},{17,25},{25,1},{2,10},{10... | collective-permute-start | bytes 1105928 | tf_op jit(solution)/shard_map/ppermute | solution.py:176
  66.9 15.4 %collective-permute-start.10 = (bf16[240,768]{1,0:T(8,128)(2,1)}, bf16[240,768]{1,0:T(8,128)(2,1)S(1)}, u32[]{:S(2)}, u32[]{:S(2)}) collective-permute-start(bf16[240,768]{1,0:T(8,128)(2,1)} %collective-permute-done.8), channel_id=1, source_target_pairs={{0,24},{8,0},{16,8},{24,16},{1,25},{9,1},{17,9},{25,17},{2,26},{10... | collective-permute-start | bytes 1105928 | tf_op jit(solution)/shard_map/ppermute | solution.py:176
  78.8 19.2 %collective-permute-start.15 = (bf16[96,3072]{1,0:T(8,128)(2,1)S(1)}, bf16[96,3072]{1,0:T(8,128)(2,1)S(1)}, u32[]{:S(2)}, u32[]{:S(2)}) collective-permute-start(bf16[96,3072]{1,0:T(8,128)(2,1)S(1)} %collective-permute-done.14), channel_id=1, source_target_pairs={{0,32},{32,64},{64,96},{96,0},{1,33},{33,65},{65,97},{97,1},{2,34}... | collective-permute-start | bytes 1769480 | tf_op jit(solution)/shard_map/ppermute | solution.py:176
  80.3 15.4 %collective-permute-start.16 = (bf16[96,3072]{1,0:T(8,128)(2,1)S(1)}, bf16[96,3072]{1,0:T(8,128)(2,1)S(1)}, u32[]{:S(2)}, u32[]{:S(2)}) collective-permute-start(bf16[96,3072]{1,0:T(8,128)(2,1)S(1)} %collective-permute-done.14), channel_id=1, source_target_pairs={{0,96},{32,0},{64,32},{96,64},{1,97},{33,1},{65,33},{97,65},{2,98}... | collective-permute-start | bytes 1769480 | tf_op jit(solution)/shard_map/ppermute | solution.py:176
  95.3 53.7 %collective-permute-start.13 = (bf16[1920,768]{1,0:T(8,128)(2,1)}, bf16[1920,768]{1,0:T(8,128)(2,1)}, u32[]{:S(2)}, u32[]{:S(2)}) collective-permute-start(bf16[1920,768]{1,0:T(8,128)(2,1)} %pad_maximum_fusion.2), channel_id=1, source_target_pairs={{0,1},{1,0},{2,3},{3,2},{4,5},{5,4},{6,7},{7,6},{8,9},{9,8},{10,11... | collective-permute-start | bytes 8847368 | tf_op jit(solution)/shard_map/ppermute | solution.py:252
  110.1 56.9 %collective-permute-start.19 = (bf16[768,3072]{1,0:T(8,128)(2,1)}, bf16[768,3072]{1,0:T(8,128)(2,1)}, u32[]{:S(2)}, u32[]{:S(2)}) collective-permute-start(bf16[768,3072]{1,0:T(8,128)(2,1)} %pad_maximum_fusion), channel_id=1, source_target_pairs={{0,1},{1,0},{2,3},{3,2},{4,5},{5,4},{6,7},{7,6},{8,9},{9,8},{10,11... | collective-permute-start | bytes 14155784 | tf_op jit(solution)/shard_map/ppermute | solution.py:252
  238.1 45.5 %collective-permute-start.20 = (f32[512,1536]{1,0:T(8,128)}, f32[512,1536]{1,0:T(8,128)}, u32[]{:S(2)}, u32[]{:S(2)}) collective-permute-start(f32[512,1536]{1,0:T(8,128)} %slice.377), channel_id=1, source_target_pairs={{0,1},{1,0},{2,3},{3,2},{4,5},{5,4},{6,7},{7,6},{8,9},{9,8},{10,11... | collective-permute-start | bytes 9437192 | tf_op jit(solution)/shard_map/ppermute | solution.py:252
  347.4 29.3 %collective-permute-start.32 = (bf16[2,4,192,384]{3,2,1,0:T(8,128)(2,1)S(1)}, bf16[2,4,192,384]{3,2,1,0:T(8,128)(2,1)S(1)}, u32[]{:S(2)}, u32[]{:S(2)}) collective-permute-start(bf16[2,4,192,384]{3,2,1,0:T(8,128)(2,1)S(1)} %pad_maximum_fusion.7), channel_id=1, source_target_pairs={{0,8},{8,16},{16,24},{24,0},{1,9},{9,17},{17,25},{25,1},{2,10},{10... | collective-permute-start | bytes 3538952 | tf_op jit(solution)/shard_map/ppermute | solution.py:176
  354.9 29.0 %collective-permute-start.24 = (bf16[2,768,384]{2,1,0:T(8,128)(2,1)S(1)}, bf16[2,768,384]{2,1,0:T(8,128)(2,1)S(1)}, u32[]{:S(2)}, u32[]{:S(2)}) collective-permute-start(bf16[2,768,384]{2,1,0:T(8,128)(2,1)S(1)} %pad_maximum_fusion.5), channel_id=1, source_target_pairs={{0,32},{32,64},{64,96},{96,0},{1,33},{33,65},{65,97},{97,1},{2,34}... | collective-permute-start | bytes 3538952 | tf_op jit(solution)/shard_map/ppermute | solution.py:176
  355.3 28.8 %collective-permute-start.25 = (bf16[2,768,384]{2,1,0:T(8,128)(2,1)S(1)}, bf16[2,768,384]{2,1,0:T(8,128)(2,1)S(1)}, u32[]{:S(2)}, u32[]{:S(2)}) collective-permute-start(bf16[2,768,384]{2,1,0:T(8,128)(2,1)S(1)} %pad_maximum_fusion.6), channel_id=1, source_target_pairs={{0,96},{32,0},{64,32},{96,64},{1,97},{33,1},{65,33},{97,65},{2,98}... | collective-permute-start | bytes 3538952 | tf_op jit(solution)/shard_map/ppermute | solution.py:176
  358.8 28.9 %collective-permute-start.33 = (bf16[2,4,192,384]{3,2,1,0:T(8,128)(2,1)S(1)}, bf16[2,4,192,384]{3,2,1,0:T(8,128)(2,1)S(1)}, u32[]{:S(2)}, u32[]{:S(2)}) collective-permute-start(bf16[2,4,192,384]{3,2,1,0:T(8,128)(2,1)S(1)} %pad_maximum_fusion.8), channel_id=1, source_target_pairs={{0,24},{8,0},{16,8},{24,16},{1,25},{9,1},{17,9},{25,17},{2,26},{10... | collective-permute-start | bytes 3538952 | tf_op jit(solution)/shard_map/ppermute | solution.py:176
  376.9 15.9 %collective-permute-start.35 = (bf16[4,192,384]{2,1,0:T(8,128)(2,1)S(1)}, bf16[4,192,384]{2,1,0:T(8,128)(2,1)S(1)}, u32[]{:S(2)}, u32[]{:S(2)}) collective-permute-start(bf16[4,192,384]{2,1,0:T(8,128)(2,1)S(1)} %fusion.9), channel_id=1, source_target_pairs={{0,8},{8,16},{16,24},{24,0},{1,9},{9,17},{17,25},{25,1},{2,10},{10... | collective-permute-start | bytes 1769480 | tf_op jit(solution)/shard_map/ppermute | solution.py:176
  384.1 15.5 %collective-permute-start.27 = (bf16[768,384]{1,0:T(8,128)(2,1)S(1)}, bf16[768,384]{1,0:T(8,128)(2,1)S(1)}, u32[]{:S(2)}, u32[]{:S(2)}) collective-permute-start(bf16[768,384]{1,0:T(8,128)(2,1)S(1)} %fusion.13), channel_id=1, source_target_pairs={{0,32},{32,64},{64,96},{96,0},{1,33},{33,65},{65,97},{97,1},{2,34}... | collective-permute-start | bytes 1769480 | tf_op jit(solution)/shard_map/ppermute | solution.py:176
  393.2 16.3 %collective-permute-start.34 = (bf16[4,192,384]{2,1,0:T(8,128)(2,1)S(1)}, bf16[4,192,384]{2,1,0:T(8,128)(2,1)S(1)}, u32[]{:S(2)}, u32[]{:S(2)}) collective-permute-start(bf16[4,192,384]{2,1,0:T(8,128)(2,1)S(1)} %get-tuple-element.41), channel_id=1, source_target_pairs={{0,24},{8,0},{16,8},{24,16},{1,25},{9,1},{17,9},{25,17},{2,26},{10... | collective-permute-start | bytes 1769480 | tf_op jit(solution)/shard_map/ppermute | solution.py:176
  400.0 15.8 %collective-permute-start.30 = (bf16[192,768]{1,0:T(8,128)(2,1)S(1)}, bf16[192,768]{1,0:T(8,128)(2,1)S(1)}, u32[]{:S(2)}, u32[]{:S(2)}) collective-permute-start(bf16[192,768]{1,0:T(8,128)(2,1)S(1)} %get-tuple-element.71), channel_id=1, source_target_pairs={{0,24},{8,0},{16,8},{24,16},{1,25},{9,1},{17,9},{25,17},{2,26},{10... | collective-permute-start | bytes 884744 | tf_op jit(solution)/shard_map/ppermute | solution.py:176
  438.2 15.8 %collective-permute-start.41 = (bf16[192,768]{1,0:T(8,128)(2,1)S(1)}, bf16[192,768]{1,0:T(8,128)(2,1)S(1)}, u32[]{:S(2)}, u32[]{:S(2)}) collective-permute-start(bf16[192,768]{1,0:T(8,128)(2,1)S(1)} %get-tuple-element.30), channel_id=1, source_target_pairs={{0,8},{8,16},{16,24},{24,0},{1,9},{9,17},{17,25},{25,1},{2,10},{10... | collective-permute-start | bytes 884744 | tf_op jit(solution)/shard_map/ppermute | solution.py:176
  438.3 15.7 %collective-permute-start.42 = (bf16[192,768]{1,0:T(8,128)(2,1)S(1)}, bf16[192,768]{1,0:T(8,128)(2,1)S(1)}, u32[]{:S(2)}, u32[]{:S(2)}) collective-permute-start(bf16[192,768]{1,0:T(8,128)(2,1)S(1)} %get-tuple-element.30), channel_id=1, source_target_pairs={{0,16},{8,24},{16,0},{24,8},{1,17},{9,25},{17,1},{25,9},{2,18},{10... | collective-permute-start | bytes 884744 | tf_op jit(solution)/shard_map/ppermute | solution.py:176
  454.7 30.5 %collective-permute-start.44 = (bf16[768,768]{1,0:T(8,128)(2,1)S(1)}, bf16[768,768]{1,0:T(8,128)(2,1)S(1)}, u32[]{:S(2)}, u32[]{:S(2)}) collective-permute-start(bf16[768,768]{1,0:T(8,128)(2,1)S(1)} %constant_dynamic-update-slice_fusion.7), channel_id=1, source_target_pairs={{0,32},{32,64},{64,96},{96,0},{1,33},{33,65},{65,97},{97,1},{2,34}... | collective-permute-start | bytes 3538952 | tf_op jit(solution)/shard_map/ppermute | solution.py:176
  454.8 26.6 %collective-permute-start.45 = (bf16[768,768]{1,0:T(8,128)(2,1)S(1)}, bf16[768,768]{1,0:T(8,128)(2,1)S(1)}, u32[]{:S(2)}, u32[]{:S(2)}) collective-permute-start(bf16[768,768]{1,0:T(8,128)(2,1)S(1)} %constant_dynamic-update-slice_fusion.7), channel_id=1, source_target_pairs={{0,96},{32,0},{64,32},{96,64},{1,97},{33,1},{65,33},{97,65},{2,98}... | collective-permute-start | bytes 3538952 | tf_op jit(solution)/shard_map/ppermute | solution.py:176
  (90 other events, 1057.1 us)

commit v4 on v3

--- a/solution.py
+++ b/solution.py
@@ -309,8 +309,13 @@
         + cross(low_oth).astype(jnp.float32)
         + lax.ppermute(low_oth, "xh", [(0, 1), (1, 0)]).astype(jnp.float32)
     )
-    full = ring_gather(mine.astype(jnp.bfloat16), "z", sizes["z"], 0, True)
-    full = ring_gather(full, "y", sizes["y"], 0, direct)
+    low_mine = mine.astype(jnp.bfloat16)
+    half = low_mine.shape[1] // 2
+    first = ring_gather(low_mine[:, :half], "z", nz, 0, True)
+    first = ring_gather(first, "y", ny, 0, direct)
+    second = ring_gather(low_mine[None, :, half:], "y", ny, 0, True)
+    second = ring_gather(second, "z", nz, 1, direct).reshape(first.shape)
+    full = jnp.concatenate([first, second], axis=1)
     out = []
     start = 0
     for w in grads:

time: 520 us -> 523 us (level)
    ppermute x4, waiting for transfers between devices: 27 us -> 44 us  [cross(): return lax.ppermute(x, ('xl', 'xh'), [(i, 3 - i) for i in range(4)])]
    ppermute x32 -> x39, starting transfers between devices: 49.3 us -> 58 us  [shift(): return lax.ppermute(x, axis, [(i, (i + step) % n) for i in range(n)])]
    ppermute x1, starting transfers between devices: 7.41 us -> 0.71 us  [from_sequence(): first = lax.ppermute(first, GRP, [(0, 0), (1, 2), (2, 1), (3, 3)])]
    ppermute x1, waiting for transfers between devices: 6.4 us -> 0.01 us  [from_sequence(): second = lax.ppermute(second, GRP, [(2, 0), (0, 1), (3, 2), (1, 3)])]
    ppermute x32 -> x39, waiting for transfers between devices: 101 us -> 94.9 us  [shift(): return lax.ppermute(x, axis, [(i, (i + step) % n) for i in range(n)])]
    dynamic_update_slice x39 -> x46, local copies, waits for them, and re-layouts: 22.5 us -> 22.9 us  [place(): return lax.dynamic_update_slice(buf, piece, start)]
    unnamed x147 -> x149, local copies, waits for them, and re-layouts: 29.5 us -> 29.6 us
  transfers between devices with their start and end apart: 48 -> 55, of which waited for: 27 -> 27; matrix products, arithmetic and copies ran while one was open for 25% -> 24% of each run, Pallas kernels for 5% -> 5%
where the time goes in v4:
time: 523 us; the launch traced here: 513 us
  waiting for transfers between devices  151 us (29%)
  local copies, waits for them, and re-layouts  117 us (22%)
  matrix products  73 us (14%)
  starting transfers between devices  69.2 us (13%)
  Pallas kernels  54.1 us (10%)
  other arithmetic  45.9 us (9%)
    ppermute x39, waiting for transfers between devices, shift(): return lax.ppermute(x, axis, [(i, (i + step) % n) for i in range(n)])  94.9 us
    ppermute x39, starting transfers between devices, shift(): return lax.ppermute(x, axis, [(i, (i + step) % n) for i in range(n)])  58 us
    ppermute x4, waiting for transfers between devices, cross(): return lax.ppermute(x, ('xl', 'xh'), [(i, 3 - i) for i in range(4)])  44 us
    pallas_call x1, Pallas kernels, attention_backward(): pl.pallas_call(attention_backward_kernel, grid=(pairs,), in_specs=[pl.Blo...  30.7 us
    unnamed x149, local copies, waits for them, and re-layouts  29.6 us
    dot_general x7, matrix products, contract_rows(): lax.dot_general(left, right, (((0,), (0,)), ((), ())), preferred_element_...  28.6 us
    dot_general x7, matrix products, matmul(): return jnp.dot(left, right, preferred_element_type=jnp.float32)  24.7 us
    pallas_call x1, Pallas kernels, attention_forward(): pl.pallas_call(attention_forward_kernel, grid=(pairs,), in_specs=[pl.Bloc...  23.4 us
  transfers between devices with their start and end apart: 55, of which 27 were waited for; matrix products, arithmetic and copies ran while one was open for 24% of the time, Pallas kernels for 5%

profile of v4, /device:TPU:0, one launch (start us, length us, event | category | flops | bytes accessed | tf_op | source)
XLA Modules:
  0.0 513.0 jit_solution(2930840060142300865)
XLA Ops:
  11.2 16.7 %collective-permute-done.2 = bf16[144,768]{1,0:T(8,128)(2,1)S(1)} collective-permute-done((bf16[144,768]{1,0:T(8,128)(2,1)}, bf16[144,768]{1,0:T(8,128)(2,1)S(1)}, u32[]{:S(2)}, u32[]{:S(2)}) %collective-permute-start.2) | collective-permute-done | bytes 221216 | tf_op jit(solution)/shard_map/ppermute | solution.py:248
  36.6 5.0 collective-permute-done.4
  98.1 7.0 %collective-permute-done.18 = bf16[48,3072]{1,0:T(8,128)(2,1)S(1)} collective-permute-done((bf16[48,3072]{1,0:T(8,128)(2,1)S(1)}, bf16[48,3072]{1,0:T(8,128)(2,1)S(1)}, u32[]{:S(2)}, u32[]{:S(2)}) %collective-permute-start.18) | collective-permute-done | bytes 294944 | tf_op jit(solution)/shard_map/ppermute | solution.py:176
  125.9 23.4 %shard_map.178 = (f32[512,768]{1,0:T(8,128)}, f32[6,512,2]{2,1,0:T(8,128)}) custom-call(bf16[512,768]{1,0:T(8,128)(2,1)} %copy.23.q_ref, bf16[1024,1536]{1,0:T(8,128)(2,1)} %pad_maximum_fusion.1.k_ref.v_ref, bf16[1024,1536]{1,0:T(8,128)(2,1)} %pad_maximum_fusion.1.k_ref.v_ref, s32[512,1]{1,0:T(8,128)} %iota_add_fusion.rq_ref, s32[512,1]{1,0:T(8,128)} %copy.24.sq_ref, ...), custom_call_target="tpu_custom_call" | custom-call | flops 1610612736 | bytes 5505024 | tf_op jit(solution)/shard_map/pallas_call | solution.py:118
  180.3 7.5 %multiply_convert_fusion.1 = (bf16[512,3072]{1,0:T(8,128)(2,1)}, bf16[512,3072]{1,0:T(8,128)(2,1)}, bf16[512,3072]{1,0:T(8,128)(2,1)S(1)}) fusion(f32[512,3072]{1,0:T(8,128)S(1)} %fusion.80, f32[512,3072]{1,0:T(8,128)S(1)} %fusion.49, bf16[512,768]{1,0:T(8,128)(2,1)S(1)} %multiply_convert_fusion.2, bf16[768,3072]{1,0:T(8,128)(2,1)S(1)} %get-tuple-element.65), kind=kOutput, calls=%fused_computation.4 | convolution fusion | flops 2444230656 | bytes 27525120 | tf_op jit(solution)/shard_map/dot_general | solution.py:35
  190.9 5.1 multiply_reduce_fusion
  200.9 30.7 %shard_map.179 = (f32[512,768]{1,0:T(8,128)}, f32[1024,768]{1,0:T(8,128)}, f32[1024,768]{1,0:T(8,128)}) custom-call(bf16[512,768]{1,0:T(8,128)(2,1)} %copy.23.q_ref, bf16[1024,1536]{1,0:T(8,128)(2,1)} %pad_maximum_fusion.1.k_ref.v_ref, bf16[1024,1536]{1,0:T(8,128)(2,1)} %pad_maximum_fusion.1.k_ref.v_ref, bf16[512,768]{1,0:T(8,128)(2,1)} %convolution_convert_fusion.7.do_ref, ...), custom_call_target="tpu_custom_call" | custom-call | flops 4026531840 | bytes 12582912 | tf_op jit(solution)/shard_map/pallas_call | solution.py:147
  242.1 7.0 %convolution_convert_fusion.2 = bf16[768,3072]{1,0:T(8,128)(2,1)} fusion(bf16[512,768]{1,0:T(8,128)(2,1)} %copy-done.29, bf16[512,3072]{1,0:T(8,128)(2,1)} %get-tuple-element.36), kind=kOutput, calls=%fused_computation.8 | convolution fusion | flops 2418278400 | bytes 8650752 | tf_op jit(solution)/shard_map/dot_general | solution.py:39
  249.2 8.5 %reshape.235 = bf16[3072,768]{1,0:T(8,128)(2,1)} reshape(bf16[768,3072]{1,0:T(8,128)(2,1)} %convolution_convert_fusion.2) | data formatting | bytes 9437184 | tf_op jit(solution)/shard_map/reshape | solution.py:477
  257.7 7.0 %convolution_convert_fusion.1 = bf16[768,3072]{1,0:T(8,128)(2,1)} fusion(bf16[512,768]{1,0:T(8,128)(2,1)} %copy-done.29, bf16[512,3072]{1,0:T(8,128)(2,1)} %copy-done.54), kind=kOutput, calls=%fused_computation.7 | convolution fusion | flops 2418278400 | bytes 8650752 | tf_op jit(solution)/shard_map/dot_general | solution.py:39
  264.7 8.8 %reshape.236 = bf16[3072,768]{1,0:T(8,128)(2,1)} reshape(bf16[768,3072]{1,0:T(8,128)(2,1)} %convolution_convert_fusion.1) | data formatting | bytes 9437184 | tf_op jit(solution)/shard_map/reshape | solution.py:477
  277.2 6.8 %convolution_convert_fusion = bf16[3072,768]{1,0:T(8,128)(2,1)} fusion(bf16[512,3072]{1,0:T(8,128)(2,1)} %get-tuple-element.35, bf16[512,1536]{1,0:T(8,128)(2,1)S(1)} %maximum_select_fusion), kind=kOutput, calls=%fused_computation.6 | convolution fusion | flops 2418278400 | bytes 8650752 | tf_op jit(solution)/shard_map/dot_general | solution.py:39
  315.8 6.9 %add_convert_fusion.2 = bf16[512,768]{1,0:T(8,128)(2,1)} fusion(f32[512,768]{1,0:T(8,128)S(1)} %get-tuple-element.123, bf16[512,3072]{1,0:T(8,128)(2,1)} %get-tuple-element.35, bf16[3072,768]{1,0:T(8,128)(2,1)} %slice_dynamic-update-slice_fusion), kind=kOutput, calls=%fused_computation.59 | convolution fusion | flops 2416705536 | bytes 10223616 | tf_op jit(solution)/shard_map/dot_general | solution.py:35
  324.7 5.9 %collective-permute-done.23 = bf16[6144,768]{1,0:T(8,128)(2,1)} collective-permute-done((bf16[6144,768]{1,0:T(8,128)(2,1)}, bf16[6144,768]{1,0:T(8,128)(2,1)}, u32[]{:S(2)}, u32[]{:S(2)}) %collective-permute-start.23) | collective-permute-done | bytes 9437216 | tf_op jit(solution)/shard_map/ppermute | solution.py:252
  330.6 7.3 %convert_add_fusion = f32[2,3072,768]{2,1,0:T(8,128)S(1)} fusion(bf16[2,3072,768]{2,1,0:T(8,128)(2,1)} %bitcast.49, bf16[1,3072,768]{2,1,0:T(8,128)(2,1)} %bitcast.22, bf16[1,3072,768]{2,1,0:T(8,128)(2,1)} %bitcast.21), kind=kLoop, calls=%fused_computation | loop fusion | flops 18874368 | bytes 37748736 | tf_op jit(solution)/shard_map/add | solution.py:297
  337.9 7.1 %fusion.74 = (f32[1,3072,768]{2,1,0:T(8,128)}, f32[1,3072,768]{2,1,0:T(8,128)}) fusion(f32[2,3072,768]{2,1,0:T(8,128)S(1)} %convert_add_fusion), kind=kLoop, calls=%fused_computation.293 | loop fusion | bytes 37748736 | tf_op jit(solution)/shard_map/slice | solution.py:300
  363.5 13.7 %collective-permute-done.32 = bf16[2,4,192,384]{3,2,1,0:T(8,128)(2,1)S(1)} collective-permute-done((bf16[2,4,192,384]{3,2,1,0:T(8,128)(2,1)S(1)}, bf16[2,4,192,384]{3,2,1,0:T(8,128)(2,1)S(1)}, u32[]{:S(2)}, u32[]{:S(2)}) %collective-permute-start.32) | collective-permute-done | bytes 1179680 | tf_op jit(solution)/shard_map/ppermute | solution.py:176
  377.5 6.9 %collective-permute-done.24 = bf16[2,768,384]{2,1,0:T(8,128)(2,1)S(1)} collective-permute-done((bf16[2,768,384]{2,1,0:T(8,128)(2,1)S(1)}, bf16[2,768,384]{2,1,0:T(8,128)(2,1)S(1)}, u32[]{:S(2)}, u32[]{:S(2)}) %collective-permute-start.24) | collective-permute-done | bytes 1179680 | tf_op jit(solution)/shard_map/ppermute | solution.py:176
  388.1 5.3 %collective-permute-done.35 = bf16[4,192,384]{2,1,0:T(8,128)(2,1)S(1)} collective-permute-done((bf16[4,192,384]{2,1,0:T(8,128)(2,1)S(1)}, bf16[4,192,384]{2,1,0:T(8,128)(2,1)S(1)}, u32[]{:S(2)}, u32[]{:S(2)}) %collective-permute-start.35) | collective-permute-done | bytes 589856 | tf_op jit(solution)/shard_map/ppermute | solution.py:176
  395.0 5.1 collective-permute-done.27
  428.0 5.4 %collective-permute-done.40 = bf16[192,768]{1,0:T(8,128)(2,1)S(1)} collective-permute-done((bf16[192,768]{1,0:T(8,128)(2,1)S(1)}, bf16[192,768]{1,0:T(8,128)(2,1)S(1)}, u32[]{:S(2)}, u32[]{:S(2)}) %collective-permute-start.40) | collective-permute-done | bytes 294944 | tf_op jit(solution)/shard_map/ppermute | solution.py:310
  433.4 22.4 %collective-permute-done.39 = bf16[192,768]{1,0:T(8,128)(2,1)S(1)} collective-permute-done((bf16[192,768]{1,0:T(8,128)(2,1)S(1)}, bf16[192,768]{1,0:T(8,128)(2,1)S(1)}, u32[]{:S(2)}, u32[]{:S(2)}) %collective-permute-start.39) | collective-permute-done | bytes 294944 | tf_op jit(solution)/shard_map/ppermute | solution.py:248
  459.4 6.3 %collective-permute-done.48 = bf16[1,192,384]{2,1,0:T(8,128)(2,1)S(1)} collective-permute-done((bf16[1,192,384]{2,1,0:T(8,128)(2,1)S(1)}, bf16[1,192,384]{2,1,0:T(8,128)(2,1)S(1)}, u32[]{:S(2)}, u32[]{:S(2)}) %collective-permute-start.48) | collective-permute-done | bytes 147488 | tf_op jit(solution)/shard_map/ppermute | solution.py:176
  469.2 5.7 %collective-permute-done.41 = bf16[192,384]{1,0:T(8,128)(2,1)S(1)} collective-permute-done((bf16[192,384]{1,0:T(8,128)(2,1)S(1)}, bf16[192,384]{1,0:T(8,128)(2,1)S(1)}, u32[]{:S(2)}, u32[]{:S(2)}) %collective-permute-start.41) | collective-permute-done | bytes 147488 | tf_op jit(solution)/shard_map/ppermute | solution.py:176
  (422 shorter events, 278.7 us)
Async XLA Ops:
  2.6 25.3 %collective-permute-start.2 = (bf16[144,768]{1,0:T(8,128)(2,1)}, bf16[144,768]{1,0:T(8,128)(2,1)S(1)}, u32[]{:S(2)}, u32[]{:S(2)}) collective-permute-start(bf16[144,768]{1,0:T(8,128)(2,1)} %fusion.57), channel_id=1, source_target_pairs={{0,6},{2,4},{4,2},{6,0},{1,7},{3,5},{5,3},{7,1},{8,14},{10,12},{12... | collective-permute-start | bytes 663560 | tf_op jit(solution)/shard_map/ppermute | solution.py:248
  5.7 38.2 %collective-permute-start.1 = (bf16[256,1536]{1,0:T(8,128)(2,1)S(1)}, bf16[256,1536]{1,0:T(8,128)(2,1)}, u32[]{:S(2)}, u32[]{:S(2)}) collective-permute-start(bf16[256,1536]{1,0:T(8,128)(2,1)S(1)} %get-tuple-element.93), channel_id=1, source_target_pairs={{0,2},{1,0},{2,3},{3,1},{4,6},{5,4},{6,7},{7,5},{8,10},{9,8},{10,1... | collective-permute-start | bytes 2359304 | tf_op jit(solution)/shard_map/ppermute | solution.py:332
  6.6 37.4 %collective-permute-start = (bf16[256,1536]{1,0:T(8,128)(2,1)S(1)}, bf16[256,1536]{1,0:T(8,128)(2,1)}, u32[]{:S(2)}, u32[]{:S(2)}) collective-permute-start(bf16[256,1536]{1,0:T(8,128)(2,1)S(1)} %get-tuple-element.92), channel_id=1, source_target_pairs={{0,0},{1,2},{2,1},{3,3},{4,4},{5,6},{6,5},{7,7},{8,8},{9,10},{10,9... | collective-permute-start | bytes 2359304 | tf_op jit(solution)/shard_map/ppermute | solution.py:331
  61.9 16.9 %collective-permute-start.14 = (bf16[96,3072]{1,0:T(8,128)(2,1)}, bf16[96,3072]{1,0:T(8,128)(2,1)S(1)}, u32[]{:S(2)}, u32[]{:S(2)}) collective-permute-start(bf16[96,3072]{1,0:T(8,128)(2,1)} %fusion.26), channel_id=1, source_target_pairs={{0,6},{2,4},{4,2},{6,0},{1,7},{3,5},{5,3},{7,1},{8,14},{10,12},{12... | collective-permute-start | bytes 1769480 | tf_op jit(solution)/shard_map/ppermute | solution.py:248
  65.0 56.9 %collective-permute-start.7 = (bf16[512,1536]{1,0:T(8,128)(2,1)}, bf16[512,1536]{1,0:T(8,128)(2,1)}, u32[]{:S(2)}, u32[]{:S(2)}) collective-permute-start(bf16[512,1536]{1,0:T(8,128)(2,1)} %pad_maximum_fusion.4), channel_id=1, source_target_pairs={{0,1},{1,0},{2,3},{3,2},{4,5},{5,4},{6,7},{7,6},{8,9},{9,8},{10,11... | collective-permute-start | bytes 4718600 | tf_op jit(solution)/shard_map/ppermute | solution.py:252
  65.0 21.4 %collective-permute-start.9 = (bf16[240,768]{1,0:T(8,128)(2,1)}, bf16[240,768]{1,0:T(8,128)(2,1)S(1)}, u32[]{:S(2)}, u32[]{:S(2)}) collective-permute-start(bf16[240,768]{1,0:T(8,128)(2,1)} %collective-permute-done.8), channel_id=1, source_target_pairs={{0,8},{8,16},{16,24},{24,0},{1,9},{9,17},{17,25},{25,1},{2,10},{10... | collective-permute-start | bytes 1105928 | tf_op jit(solution)/shard_map/ppermute | solution.py:176
  78.8 19.1 %collective-permute-start.15 = (bf16[96,3072]{1,0:T(8,128)(2,1)S(1)}, bf16[96,3072]{1,0:T(8,128)(2,1)S(1)}, u32[]{:S(2)}, u32[]{:S(2)}) collective-permute-start(bf16[96,3072]{1,0:T(8,128)(2,1)S(1)} %collective-permute-done.14), channel_id=1, source_target_pairs={{0,32},{32,64},{64,96},{96,0},{1,33},{33,65},{65,97},{97,1},{2,34}... | collective-permute-start | bytes 1769480 | tf_op jit(solution)/shard_map/ppermute | solution.py:176
  80.2 15.4 %collective-permute-start.16 = (bf16[96,3072]{1,0:T(8,128)(2,1)S(1)}, bf16[96,3072]{1,0:T(8,128)(2,1)S(1)}, u32[]{:S(2)}, u32[]{:S(2)}) collective-permute-start(bf16[96,3072]{1,0:T(8,128)(2,1)S(1)} %collective-permute-done.14), channel_id=1, source_target_pairs={{0,96},{32,0},{64,32},{96,64},{1,97},{33,1},{65,33},{97,65},{2,98}... | collective-permute-start | bytes 1769480 | tf_op jit(solution)/shard_map/ppermute | solution.py:176
  95.2 54.1 %collective-permute-start.13 = (bf16[1920,768]{1,0:T(8,128)(2,1)}, bf16[1920,768]{1,0:T(8,128)(2,1)}, u32[]{:S(2)}, u32[]{:S(2)}) collective-permute-start(bf16[1920,768]{1,0:T(8,128)(2,1)} %pad_maximum_fusion.2), channel_id=1, source_target_pairs={{0,1},{1,0},{2,3},{3,2},{4,5},{5,4},{6,7},{7,6},{8,9},{9,8},{10,11... | collective-permute-start | bytes 8847368 | tf_op jit(solution)/shard_map/ppermute | solution.py:252
  110.0 57.3 %collective-permute-start.19 = (bf16[768,3072]{1,0:T(8,128)(2,1)}, bf16[768,3072]{1,0:T(8,128)(2,1)}, u32[]{:S(2)}, u32[]{:S(2)}) collective-permute-start(bf16[768,3072]{1,0:T(8,128)(2,1)} %pad_maximum_fusion), channel_id=1, source_target_pairs={{0,1},{1,0},{2,3},{3,2},{4,5},{5,4},{6,7},{7,6},{8,9},{9,8},{10,11... | collective-permute-start | bytes 14155784 | tf_op jit(solution)/shard_map/ppermute | solution.py:252
  238.5 45.6 %collective-permute-start.20 = (f32[512,1536]{1,0:T(8,128)}, f32[512,1536]{1,0:T(8,128)}, u32[]{:S(2)}, u32[]{:S(2)}) collective-permute-start(f32[512,1536]{1,0:T(8,128)} %slice.393), channel_id=1, source_target_pairs={{0,1},{1,0},{2,3},{3,2},{4,5},{5,4},{6,7},{7,6},{8,9},{9,8},{10,11... | collective-permute-start | bytes 9437192 | tf_op jit(solution)/shard_map/ppermute | solution.py:252
  347.9 29.4 %collective-permute-start.32 = (bf16[2,4,192,384]{3,2,1,0:T(8,128)(2,1)S(1)}, bf16[2,4,192,384]{3,2,1,0:T(8,128)(2,1)S(1)}, u32[]{:S(2)}, u32[]{:S(2)}) collective-permute-start(bf16[2,4,192,384]{3,2,1,0:T(8,128)(2,1)S(1)} %pad_maximum_fusion.8), channel_id=1, source_target_pairs={{0,8},{8,16},{16,24},{24,0},{1,9},{9,17},{17,25},{25,1},{2,10},{10... | collective-permute-start | bytes 3538952 | tf_op jit(solution)/shard_map/ppermute | solution.py:176
  355.4 29.0 %collective-permute-start.24 = (bf16[2,768,384]{2,1,0:T(8,128)(2,1)S(1)}, bf16[2,768,384]{2,1,0:T(8,128)(2,1)S(1)}, u32[]{:S(2)}, u32[]{:S(2)}) collective-permute-start(bf16[2,768,384]{2,1,0:T(8,128)(2,1)S(1)} %pad_maximum_fusion.6), channel_id=1, source_target_pairs={{0,32},{32,64},{64,96},{96,0},{1,33},{33,65},{65,97},{97,1},{2,34}... | collective-permute-start | bytes 3538952 | tf_op jit(solution)/shard_map/ppermute | solution.py:176
  355.8 28.9 %collective-permute-start.25 = (bf16[2,768,384]{2,1,0:T(8,128)(2,1)S(1)}, bf16[2,768,384]{2,1,0:T(8,128)(2,1)S(1)}, u32[]{:S(2)}, u32[]{:S(2)}) collective-permute-start(bf16[2,768,384]{2,1,0:T(8,128)(2,1)S(1)} %pad_maximum_fusion.7), channel_id=1, source_target_pairs={{0,96},{32,0},{64,32},{96,64},{1,97},{33,1},{65,33},{97,65},{2,98}... | collective-permute-start | bytes 3538952 | tf_op jit(solution)/shard_map/ppermute | solution.py:176
  360.1 28.0 %collective-permute-start.33 = (bf16[2,4,192,384]{3,2,1,0:T(8,128)(2,1)S(1)}, bf16[2,4,192,384]{3,2,1,0:T(8,128)(2,1)S(1)}, u32[]{:S(2)}, u32[]{:S(2)}) collective-permute-start(bf16[2,4,192,384]{3,2,1,0:T(8,128)(2,1)S(1)} %pad_maximum_fusion.9), channel_id=1, source_target_pairs={{0,24},{8,0},{16,8},{24,16},{1,25},{9,1},{17,9},{25,17},{2,26},{10... | collective-permute-start | bytes 3538952 | tf_op jit(solution)/shard_map/ppermute | solution.py:176
  377.4 15.9 %collective-permute-start.35 = (bf16[4,192,384]{2,1,0:T(8,128)(2,1)S(1)}, bf16[4,192,384]{2,1,0:T(8,128)(2,1)S(1)}, u32[]{:S(2)}, u32[]{:S(2)}) collective-permute-start(bf16[4,192,384]{2,1,0:T(8,128)(2,1)S(1)} %fusion.10), channel_id=1, source_target_pairs={{0,8},{8,16},{16,24},{24,0},{1,9},{9,17},{17,25},{25,1},{2,10},{10... | collective-permute-start | bytes 1769480 | tf_op jit(solution)/shard_map/ppermute | solution.py:176
  384.5 15.5 %collective-permute-start.27 = (bf16[768,384]{1,0:T(8,128)(2,1)S(1)}, bf16[768,384]{1,0:T(8,128)(2,1)S(1)}, u32[]{:S(2)}, u32[]{:S(2)}) collective-permute-start(bf16[768,384]{1,0:T(8,128)(2,1)S(1)} %fusion.14), channel_id=1, source_target_pairs={{0,32},{32,64},{64,96},{96,0},{1,33},{33,65},{65,97},{97,1},{2,34}... | collective-permute-start | bytes 1769480 | tf_op jit(solution)/shard_map/ppermute | solution.py:176
  393.7 16.5 %collective-permute-start.34 = (bf16[4,192,384]{2,1,0:T(8,128)(2,1)S(1)}, bf16[4,192,384]{2,1,0:T(8,128)(2,1)S(1)}, u32[]{:S(2)}, u32[]{:S(2)}) collective-permute-start(bf16[4,192,384]{2,1,0:T(8,128)(2,1)S(1)} %get-tuple-element.39), channel_id=1, source_target_pairs={{0,24},{8,0},{16,8},{24,16},{1,25},{9,1},{17,9},{25,17},{2,26},{10... | collective-permute-start | bytes 1769480 | tf_op jit(solution)/shard_map/ppermute | solution.py:176
  400.5 16.1 %collective-permute-start.30 = (bf16[192,768]{1,0:T(8,128)(2,1)S(1)}, bf16[192,768]{1,0:T(8,128)(2,1)S(1)}, u32[]{:S(2)}, u32[]{:S(2)}) collective-permute-start(bf16[192,768]{1,0:T(8,128)(2,1)S(1)} %get-tuple-element.69), channel_id=1, source_target_pairs={{0,24},{8,0},{16,8},{24,16},{1,25},{9,1},{17,9},{25,17},{2,26},{10... | collective-permute-start | bytes 884744 | tf_op jit(solution)/shard_map/ppermute | solution.py:176
  425.1 30.6 %collective-permute-start.39 = (bf16[192,768]{1,0:T(8,128)(2,1)S(1)}, bf16[192,768]{1,0:T(8,128)(2,1)S(1)}, u32[]{:S(2)}, u32[]{:S(2)}) collective-permute-start(bf16[192,768]{1,0:T(8,128)(2,1)S(1)} %fusion.55), channel_id=1, source_target_pairs={{0,6},{2,4},{4,2},{6,0},{1,7},{3,5},{5,3},{7,1},{8,14},{10,12},{12... | collective-permute-start | bytes 884744 | tf_op jit(solution)/shard_map/ppermute | solution.py:248
  426.6 51.9 %collective-permute-start.22 = (bf16[256,1536]{1,0:T(8,128)(2,1)S(1)}, bf16[256,1536]{1,0:T(8,128)(2,1)S(1)}, u32[]{:S(2)}, u32[]{:S(2)}) collective-permute-start(bf16[256,1536]{1,0:T(8,128)(2,1)S(1)} %get-tuple-element.91), channel_id=1, source_target_pairs={{2,0},{0,1},{3,2},{1,3},{6,4},{4,5},{7,6},{5,7},{10,8},{8,9},{11,1... | collective-permute-start | bytes 2359304 | tf_op jit(solution)/shard_map/ppermute | solution.py:343
  426.7 55.0 %collective-permute-start.21 = (bf16[256,1536]{1,0:T(8,128)(2,1)S(1)}, bf16[256,1536]{1,0:T(8,128)(2,1)S(1)}, u32[]{:S(2)}, u32[]{:S(2)}) collective-permute-start(bf16[256,1536]{1,0:T(8,128)(2,1)S(1)} %get-tuple-element.90), channel_id=1, source_target_pairs={{0,0},{1,2},{2,1},{3,3},{4,4},{5,6},{6,5},{7,7},{8,8},{9,10},{10,9... | collective-permute-start | bytes 2359304 | tf_op jit(solution)/shard_map/ppermute | solution.py:342
  474.9 16.8 %collective-permute-start.51 = (bf16[4,192,384]{2,1,0:T(8,128)(2,1)S(1)}, bf16[4,192,384]{2,1,0:T(8,128)(2,1)S(1)}, u32[]{:S(2)}, u32[]{:S(2)}) collective-permute-start(bf16[4,192,384]{2,1,0:T(8,128)(2,1)S(1)} %constant_dynamic-update-slice_fusion.7), channel_id=1, source_target_pairs={{0,8},{8,16},{16,24},{24,0},{1,9},{9,17},{17,25},{25,1},{2,10},{10... | collective-permute-start | bytes 1769480 | tf_op jit(solution)/shard_map/ppermute | solution.py:176
  478.4 16.8 %collective-permute-start.44 = (bf16[768,384]{1,0:T(8,128)(2,1)S(1)}, bf16[768,384]{1,0:T(8,128)(2,1)S(1)}, u32[]{:S(2)}, u32[]{:S(2)}) collective-permute-start(bf16[768,384]{1,0:T(8,128)(2,1)S(1)} %constant_dynamic-update-slice_fusion.14), channel_id=1, source_target_pairs={{0,32},{32,64},{64,96},{96,0},{1,33},{33,65},{65,97},{97,1},{2,34}... | collective-permute-start | bytes 1769480 | tf_op jit(solution)/shard_map/ppermute | solution.py:176
  (98 other events, 1047.9 us)

commit v5 on v3

--- a/solution.py
+++ b/solution.py
@@ -285,8 +285,9 @@
     g = lax.axis_index("xh") * 2 + lax.axis_index("c")
 
     def shard(w, j):
-        rows = w.shape[0] // 4
-        return lax.dynamic_slice_in_dim(w, jnp.bitwise_xor(g, j) * rows, rows, axis=0)
+        rows = w.shape[-2] // 4
+        part = lax.dynamic_slice_in_dim(w, jnp.bitwise_xor(g, j) * rows, rows, axis=w.ndim - 2)
+        return part.reshape(-1, w.shape[-1])
 
     send = jnp.concatenate([shard(w, 1) for w in grads] + [shard(w, 3) for w in grads])
     got = swap_core(send.astype(jnp.bfloat16))
@@ -314,7 +315,7 @@
     out = []
     start = 0
     for w in grads:
-        rows = w.shape[0] // 4
+        rows = w.size // (4 * w.shape[-1])
         out.append(full[start:start + rows].astype(jnp.float32))
         start += rows
     return out
@@ -426,8 +427,14 @@
     grad_gate, grad_upper = gate_back(grad_active)
     gate_low = grad_gate.astype(jnp.bfloat16)
     upper_low = grad_upper.astype(jnp.bfloat16)
-    grads[4] = contract_rows(normed_two_low, gate_low)
-    grads[5] = contract_rows(normed_two_low, upper_low)
+    def blocked_grad(left, right):
+        count = right.shape[1] // width
+        return jnp.stack(
+            [contract_rows(left, right[:, i * width:(i + 1) * width]) for i in range(count)]
+        )
+
+    grads[4] = blocked_grad(normed_two_low, gate_low)
+    grads[5] = blocked_grad(normed_two_low, upper_low)
     grad_normed_two = contract_cols(gate_low, gate_weight) + contract_cols(upper_low, up_weight)
     grad_after = grad_result.astype(jnp.float32) + norm_two_back(grad_normed_two)[0]
     after_low = grad_after.astype(jnp.bfloat16)
@@ -466,15 +473,13 @@
     both_out = from_sequence(jnp.concatenate([result_low, grad_hidden.astype(jnp.bfloat16)], axis=1))
     output = both_out[..., :width]
     input_grads = both_out[..., width:]
-    gate_rows = grads[4].shape[0]
+    blocks, gate_rows = grads[4].shape[0], grads[4].shape[1]
     low = [w.astype(jnp.bfloat16) for w in grads]
-    owned = reduce_group(
-        [low[0], low[1], low[2], low[3], low[4].reshape(-1, width), low[5].reshape(-1, width), low[6]],
-        sizes,
-        False,
-    )
-    owned[4] = owned[4].reshape(gate_rows // 4, -1)
-    owned[5] = owned[5].reshape(gate_rows // 4, -1)
+    owned = reduce_group(low, sizes, False)
+    for i in (4, 5):
+        owned[i] = owned[i].reshape(blocks, gate_rows // 4, width).transpose(1, 0, 2).reshape(
+            gate_rows // 4, blocks * width
+        )
 
     return (output, input_grads, *owned)
 

time: 520 us -> 514 us (0.988)
  the two profiles are of different devices: /device:TPU:0 before, /device:TPU:32 now
where the time goes in v5:
time: 514 us; the launch traced here: 504 us
  waiting for transfers between devices  144 us (28%)
  local copies, waits for them, and re-layouts  108 us (21%)
  starting transfers between devices  73.4 us (14%)
  matrix products  70.1 us (14%)
  Pallas kernels  54.2 us (11%)
  other arithmetic  51.6 us (10%)
    ppermute x32, waiting for transfers between devices, shift(): return lax.ppermute(x, axis, [(i, (i + step) % n) for i in range(n)])  95.6 us
    ppermute x32, starting transfers between devices, shift(): return lax.ppermute(x, axis, [(i, (i + step) % n) for i in range(n)])  52.7 us
    unnamed x183, local copies, waits for them, and re-layouts  36.3 us
    pallas_call x1, Pallas kernels, attention_backward(): pl.pallas_call(attention_backward_kernel, grid=(pairs,), in_specs=[pl.Blo...  30.8 us
    ppermute x4, waiting for transfers between devices, cross(): return lax.ppermute(x, ('xl', 'xh'), [(i, 3 - i) for i in range(4)])  29.8 us
    dot_general x7, matrix products, matmul(): return jnp.dot(left, right, preferred_element_type=jnp.float32)  26.4 us
    pallas_call x1, Pallas kernels, attention_forward(): pl.pallas_call(attention_forward_kernel, grid=(pairs,), in_specs=[pl.Bloc...  23.4 us
    dot_general x13, matrix products, contract_rows(): lax.dot_general(left, right, (((0,), (0,)), ((), ())), preferred_element_...  22.7 us
  transfers between devices with their start and end apart: 48, of which 29 were waited for; matrix products, arithmetic and copies ran while one was open for 21% of the time, Pallas kernels for 5%

profile of v5, /device:TPU:32, one launch (start us, length us, event | category | flops | bytes accessed | tf_op | source)
XLA Modules:
  0.0 504.1 jit_solution(17623744317731636222)
XLA Ops:
  11.2 16.8 %collective-permute-done.2 = bf16[144,768]{1,0:T(8,128)(2,1)S(1)} collective-permute-done((bf16[144,768]{1,0:T(8,128)(2,1)}, bf16[144,768]{1,0:T(8,128)(2,1)S(1)}, u32[]{:S(2)}, u32[]{:S(2)}) %collective-permute-start.2) | collective-permute-done | bytes 221216 | tf_op jit(solution)/shard_map/ppermute | solution.py:248
  36.5 5.0 collective-permute-done.4
  70.9 7.2 %collective-permute-done.14 = bf16[96,3072]{1,0:T(8,128)(2,1)S(1)} collective-permute-done((bf16[96,3072]{1,0:T(8,128)(2,1)}, bf16[96,3072]{1,0:T(8,128)(2,1)S(1)}, u32[]{:S(2)}, u32[]{:S(2)}) %collective-permute-start.14) | collective-permute-done | bytes 589856 | tf_op jit(solution)/shard_map/ppermute | solution.py:248
  97.4 4.4 collective-permute-done.18
  124.0 23.4 %shard_map.178 = (f32[512,768]{1,0:T(8,128)}, f32[6,512,2]{2,1,0:T(8,128)}) custom-call(bf16[512,768]{1,0:T(8,128)(2,1)} %copy.25.q_ref, bf16[1024,1536]{1,0:T(8,128)(2,1)} %pad_maximum_fusion.3.k_ref.v_ref, bf16[1024,1536]{1,0:T(8,128)(2,1)} %pad_maximum_fusion.3.k_ref.v_ref, s32[512,1]{1,0:T(8,128)} %iota_add_fusion.rq_ref, s32[512,1]{1,0:T(8,128)} %copy.26.sq_ref, ...), custom_call_target="tpu_custom_call" | custom-call | flops 1610612736 | bytes 5505024 | tf_op jit(solution)/shard_map/pallas_call | solution.py:118
  160.4 7.3 %fusion.64 = f32[512,3072]{1,0:T(8,128)} fusion(bf16[3072,768]{1,0:T(8,128)(2,1)} %slice_dynamic-update-slice_fusion, bf16[512,1536]{1,0:T(8,128)(2,1)S(1)} %maximum_select_fusion), kind=kOutput, calls=%fused_computation.203 | convolution fusion | flops 2415919104 | bytes 11796480 | tf_op jit(solution)/shard_map/dot_general | solution.py:45
  176.4 4.5 fusion.94
  180.9 9.3 %multiply_convert_fusion.1 = (bf16[512,3072]{1,0:T(8,128)(2,1)}, bf16[512,3072]{1,0:T(8,128)(2,1)S(1)}, bf16[512,3072]{1,0:T(8,128)(2,1)S(1)}) fusion(f32[512,3072]{1,0:T(8,128)S(1)} %fusion.94, f32[512,3072]{1,0:T(8,128)} %fusion.64, bf16[512,768]{1,0:T(8,128)(2,1)S(1)} %multiply_convert_fusion.2, bf16[768,3072]{1,0:T(8,128)(2,1)S(1)} %get-tuple-element.69), kind=kOutput, calls=%fused_computation.4 | convolution fusion | flops 2444230656 | bytes 27525120 | tf_op jit(solution)/shard_map/dot_general | solution.py:35
  198.8 5.1 %multiply_reduce_fusion = (f32[512]{0:T(512)S(1)}, f32[512,768]{1,0:T(8,128)S(1)}) fusion(f32[512,768]{1,0:T(8,128)S(1)} %get-tuple-element.124, f32[512]{0:T(512)S(1)} %broadcast_multiply_fusion, f32[512,768]{1,0:T(8,128)S(1)} %fusion.95, bf16[512,3072]{1,0:T(8,128)(2,1)S(1)} %get-tuple-element.38, bf16[768,3072]{1,0:T(8,128)(2,1)} %slice_dynamic-update-slice_fusion.6), kind=kOutput, calls=%fused_computation.60 | convolution fusion | flops 2417491456 | bytes 12587008 | tf_op jit(solution)/shard_map/dot_general | solution.py:45
  208.9 30.8 %shard_map.179 = (f32[512,768]{1,0:T(8,128)}, f32[1024,768]{1,0:T(8,128)}, f32[1024,768]{1,0:T(8,128)}) custom-call(bf16[512,768]{1,0:T(8,128)(2,1)} %copy.25.q_ref, bf16[1024,1536]{1,0:T(8,128)(2,1)} %pad_maximum_fusion.3.k_ref.v_ref, bf16[1024,1536]{1,0:T(8,128)(2,1)} %pad_maximum_fusion.3.k_ref.v_ref, bf16[512,768]{1,0:T(8,128)(2,1)} %convolution_convert_fusion.13.do_ref, ...), custom_call_target="tpu_custom_call" | custom-call | flops 4026531840 | bytes 12582912 | tf_op jit(solution)/shard_map/pallas_call | solution.py:147
  268.6 4.7 convolution_convert_fusion
  309.5 6.8 %add_convert_fusion.2 = bf16[512,768]{1,0:T(8,128)(2,1)} fusion(f32[512,768]{1,0:T(8,128)S(1)} %get-tuple-element.124, bf16[512,3072]{1,0:T(8,128)(2,1)} %get-tuple-element.37, bf16[3072,768]{1,0:T(8,128)(2,1)} %slice_dynamic-update-slice_fusion), kind=kOutput, calls=%fused_computation.61 | convolution fusion | flops 2416705536 | bytes 10223616 | tf_op jit(solution)/shard_map/dot_general | solution.py:35
  316.3 8.2 %collective-permute-done.23 = bf16[6144,768]{1,0:T(8,128)(2,1)} collective-permute-done((bf16[6144,768]{1,0:T(8,128)(2,1)}, bf16[6144,768]{1,0:T(8,128)(2,1)}, u32[]{:S(2)}, u32[]{:S(2)}) %collective-permute-start.23) | collective-permute-done | bytes 9437216 | tf_op jit(solution)/shard_map/ppermute | solution.py:252
  324.5 7.4 %convert_add_fusion = f32[2,3072,768]{2,1,0:T(8,128)S(1)} fusion(bf16[2,3072,768]{2,1,0:T(8,128)(2,1)} %bitcast.67, bf16[1,3072,768]{2,1,0:T(8,128)(2,1)} %bitcast.34, bf16[1,3072,768]{2,1,0:T(8,128)(2,1)} %bitcast.31), kind=kLoop, calls=%fused_computation | loop fusion | flops 18874368 | bytes 37748736 | tf_op jit(solution)/shard_map/add | solution.py:298
  332.0 7.3 %fusion.89 = (f32[1,3072,768]{2,1,0:T(8,128)}, f32[1,3072,768]{2,1,0:T(8,128)}) fusion(f32[2,3072,768]{2,1,0:T(8,128)S(1)} %convert_add_fusion), kind=kLoop, calls=%fused_computation.315 | loop fusion | bytes 37748736 | tf_op jit(solution)/shard_map/slice | solution.py:301
  355.8 14.4 %collective-permute-done.32 = bf16[2,4,192,384]{3,2,1,0:T(8,128)(2,1)S(1)} collective-permute-done((bf16[2,4,192,384]{3,2,1,0:T(8,128)(2,1)S(1)}, bf16[2,4,192,384]{3,2,1,0:T(8,128)(2,1)S(1)}, u32[]{:S(2)}, u32[]{:S(2)}) %collective-permute-start.32) | collective-permute-done | bytes 1179680 | tf_op jit(solution)/shard_map/ppermute | solution.py:176
  373.3 6.7 %collective-permute-done.24 = bf16[2,768,384]{2,1,0:T(8,128)(2,1)S(1)} collective-permute-done((bf16[2,768,384]{2,1,0:T(8,128)(2,1)S(1)}, bf16[2,768,384]{2,1,0:T(8,128)(2,1)S(1)}, u32[]{:S(2)}, u32[]{:S(2)}) %collective-permute-start.24) | collective-permute-done | bytes 1179680 | tf_op jit(solution)/shard_map/ppermute | solution.py:176
  390.3 5.3 %collective-permute-done.27 = bf16[768,384]{1,0:T(8,128)(2,1)S(1)} collective-permute-done((bf16[768,384]{1,0:T(8,128)(2,1)S(1)}, bf16[768,384]{1,0:T(8,128)(2,1)S(1)}, u32[]{:S(2)}, u32[]{:S(2)}) %collective-permute-start.27) | collective-permute-done | bytes 589856 | tf_op jit(solution)/shard_map/ppermute | solution.py:176
  427.0 5.8 %collective-permute-done.39 = bf16[192,768]{1,0:T(8,128)(2,1)S(1)} collective-permute-done((bf16[192,768]{1,0:T(8,128)(2,1)S(1)}, bf16[192,768]{1,0:T(8,128)(2,1)S(1)}, u32[]{:S(2)}, u32[]{:S(2)}) %collective-permute-start.39) | collective-permute-done | bytes 294944 | tf_op jit(solution)/shard_map/ppermute | solution.py:248
  444.9 4.6 collective-permute-done.43
  454.2 7.4 %collective-permute-start.21 = (bf16[256,1536]{1,0:T(8,128)(2,1)}, bf16[256,1536]{1,0:T(8,128)(2,1)}, u32[]{:S(2)}, u32[]{:S(2)}) collective-permute-start(bf16[256,1536]{1,0:T(8,128)(2,1)} %get-tuple-element.94), channel_id=1, source_target_pairs={{0,0},{1,2},{2,1},{3,3},{4,4},{5,6},{6,5},{7,7},{8,8},{9,10},{10,9... | collective-permute-start | bytes 2359304 | tf_op jit(solution)/shard_map/ppermute | solution.py:338
  461.6 6.4 %collective-permute-done.22 = bf16[256,1536]{1,0:T(8,128)(2,1)} collective-permute-done((bf16[256,1536]{1,0:T(8,128)(2,1)}, bf16[256,1536]{1,0:T(8,128)(2,1)}, u32[]{:S(2)}, u32[]{:S(2)}) %collective-permute-start.22) | collective-permute-done | bytes 786464 | tf_op jit(solution)/shard_map/ppermute | solution.py:339
  470.2 7.8 %collective-permute-done.45 = bf16[768,768]{1,0:T(8,128)(2,1)S(1)} collective-permute-done((bf16[768,768]{1,0:T(8,128)(2,1)S(1)}, bf16[768,768]{1,0:T(8,128)(2,1)S(1)}, u32[]{:S(2)}, u32[]{:S(2)}) %collective-permute-start.45) | collective-permute-done | bytes 1179680 | tf_op jit(solution)/shard_map/ppermute | solution.py:176
  483.8 10.0 %collective-permute-done.47 = bf16[384,768]{1,0:T(8,128)(2,1)S(1)} collective-permute-done((bf16[384,768]{1,0:T(8,128)(2,1)S(1)}, bf16[384,768]{1,0:T(8,128)(2,1)S(1)}, u32[]{:S(2)}, u32[]{:S(2)}) %collective-permute-start.47) | collective-permute-done | bytes 589856 | tf_op jit(solution)/shard_map/ppermute | solution.py:176
  (438 shorter events, 284.9 us)
Async XLA Ops:
  2.6 25.4 %collective-permute-start.2 = (bf16[144,768]{1,0:T(8,128)(2,1)}, bf16[144,768]{1,0:T(8,128)(2,1)S(1)}, u32[]{:S(2)}, u32[]{:S(2)}) collective-permute-start(bf16[144,768]{1,0:T(8,128)(2,1)} %fusion.72), channel_id=1, source_target_pairs={{0,6},{2,4},{4,2},{6,0},{1,7},{3,5},{5,3},{7,1},{8,14},{10,12},{12... | collective-permute-start | bytes 663560 | tf_op jit(solution)/shard_map/ppermute | solution.py:248
  5.6 38.3 %collective-permute-start.1 = (bf16[256,1536]{1,0:T(8,128)(2,1)S(1)}, bf16[256,1536]{1,0:T(8,128)(2,1)}, u32[]{:S(2)}, u32[]{:S(2)}) collective-permute-start(bf16[256,1536]{1,0:T(8,128)(2,1)S(1)} %get-tuple-element.97), channel_id=1, source_target_pairs={{0,2},{1,0},{2,3},{3,1},{4,6},{5,4},{6,7},{7,5},{8,10},{9,8},{10,1... | collective-permute-start | bytes 2359304 | tf_op jit(solution)/shard_map/ppermute | solution.py:328
  6.5 37.4 %collective-permute-start = (bf16[256,1536]{1,0:T(8,128)(2,1)S(1)}, bf16[256,1536]{1,0:T(8,128)(2,1)}, u32[]{:S(2)}, u32[]{:S(2)}) collective-permute-start(bf16[256,1536]{1,0:T(8,128)(2,1)S(1)} %get-tuple-element.96), channel_id=1, source_target_pairs={{0,0},{1,2},{2,1},{3,3},{4,4},{5,6},{6,5},{7,7},{8,8},{9,10},{10,9... | collective-permute-start | bytes 2359304 | tf_op jit(solution)/shard_map/ppermute | solution.py:327
  61.2 16.9 %collective-permute-start.14 = (bf16[96,3072]{1,0:T(8,128)(2,1)}, bf16[96,3072]{1,0:T(8,128)(2,1)S(1)}, u32[]{:S(2)}, u32[]{:S(2)}) collective-permute-start(bf16[96,3072]{1,0:T(8,128)(2,1)} %fusion.41), channel_id=1, source_target_pairs={{0,6},{2,4},{4,2},{6,0},{1,7},{3,5},{5,3},{7,1},{8,14},{10,12},{12... | collective-permute-start | bytes 1769480 | tf_op jit(solution)/shard_map/ppermute | solution.py:248
  64.1 56.0 %collective-permute-start.7 = (bf16[512,1536]{1,0:T(8,128)(2,1)}, bf16[512,1536]{1,0:T(8,128)(2,1)}, u32[]{:S(2)}, u32[]{:S(2)}) collective-permute-start(bf16[512,1536]{1,0:T(8,128)(2,1)} %pad_maximum_fusion.6), channel_id=1, source_target_pairs={{0,1},{1,0},{2,3},{3,2},{4,5},{5,4},{6,7},{7,6},{8,9},{9,8},{10,11... | collective-permute-start | bytes 4718600 | tf_op jit(solution)/shard_map/ppermute | solution.py:252
  64.3 17.5 %collective-permute-start.9 = (bf16[240,768]{1,0:T(8,128)(2,1)}, bf16[240,768]{1,0:T(8,128)(2,1)S(1)}, u32[]{:S(2)}, u32[]{:S(2)}) collective-permute-start(bf16[240,768]{1,0:T(8,128)(2,1)} %collective-permute-done.8), channel_id=1, source_target_pairs={{0,8},{8,16},{16,24},{24,0},{1,9},{9,17},{17,25},{25,1},{2,10},{10... | collective-permute-start | bytes 1105928 | tf_op jit(solution)/shard_map/ppermute | solution.py:176
  66.2 15.4 %collective-permute-start.10 = (bf16[240,768]{1,0:T(8,128)(2,1)}, bf16[240,768]{1,0:T(8,128)(2,1)S(1)}, u32[]{:S(2)}, u32[]{:S(2)}) collective-permute-start(bf16[240,768]{1,0:T(8,128)(2,1)} %collective-permute-done.8), channel_id=1, source_target_pairs={{0,24},{8,0},{16,8},{24,16},{1,25},{9,1},{17,9},{25,17},{2,26},{10... | collective-permute-start | bytes 1105928 | tf_op jit(solution)/shard_map/ppermute | solution.py:176
  78.1 19.1 %collective-permute-start.15 = (bf16[96,3072]{1,0:T(8,128)(2,1)S(1)}, bf16[96,3072]{1,0:T(8,128)(2,1)S(1)}, u32[]{:S(2)}, u32[]{:S(2)}) collective-permute-start(bf16[96,3072]{1,0:T(8,128)(2,1)S(1)} %collective-permute-done.14), channel_id=1, source_target_pairs={{0,32},{32,64},{64,96},{96,0},{1,33},{33,65},{65,97},{97,1},{2,34}... | collective-permute-start | bytes 1769480 | tf_op jit(solution)/shard_map/ppermute | solution.py:176
  91.4 56.1 %collective-permute-start.13 = (bf16[1920,768]{1,0:T(8,128)(2,1)}, bf16[1920,768]{1,0:T(8,128)(2,1)}, u32[]{:S(2)}, u32[]{:S(2)}) collective-permute-start(bf16[1920,768]{1,0:T(8,128)(2,1)} %pad_maximum_fusion.4), channel_id=1, source_target_pairs={{0,1},{1,0},{2,3},{3,2},{4,5},{5,4},{6,7},{7,6},{8,9},{9,8},{10,11... | collective-permute-start | bytes 8847368 | tf_op jit(solution)/shard_map/ppermute | solution.py:252
  108.3 59.4 %collective-permute-start.19 = (bf16[768,3072]{1,0:T(8,128)(2,1)}, bf16[768,3072]{1,0:T(8,128)(2,1)}, u32[]{:S(2)}, u32[]{:S(2)}) collective-permute-start(bf16[768,3072]{1,0:T(8,128)(2,1)} %pad_maximum_fusion), channel_id=1, source_target_pairs={{0,1},{1,0},{2,3},{3,2},{4,5},{5,4},{6,7},{7,6},{8,9},{9,8},{10,11... | collective-permute-start | bytes 14155784 | tf_op jit(solution)/shard_map/ppermute | solution.py:252
  246.6 26.7 %collective-permute-start.20 = (f32[512,1536]{1,0:T(8,128)}, f32[512,1536]{1,0:T(8,128)}, u32[]{:S(2)}, u32[]{:S(2)}) collective-permute-start(f32[512,1536]{1,0:T(8,128)} %slice.409), channel_id=1, source_target_pairs={{0,1},{1,0},{2,3},{3,2},{4,5},{5,4},{6,7},{7,6},{8,9},{9,8},{10,11... | collective-permute-start | bytes 9437192 | tf_op jit(solution)/shard_map/ppermute | solution.py:252
  342.2 28.1 %collective-permute-start.32 = (bf16[2,4,192,384]{3,2,1,0:T(8,128)(2,1)S(1)}, bf16[2,4,192,384]{3,2,1,0:T(8,128)(2,1)S(1)}, u32[]{:S(2)}, u32[]{:S(2)}) collective-permute-start(bf16[2,4,192,384]{3,2,1,0:T(8,128)(2,1)S(1)} %pad_maximum_fusion.9), channel_id=1, source_target_pairs={{0,8},{8,16},{16,24},{24,0},{1,9},{9,17},{17,25},{25,1},{2,10},{10... | collective-permute-start | bytes 3538952 | tf_op jit(solution)/shard_map/ppermute | solution.py:176
  350.8 29.2 %collective-permute-start.24 = (bf16[2,768,384]{2,1,0:T(8,128)(2,1)S(1)}, bf16[2,768,384]{2,1,0:T(8,128)(2,1)S(1)}, u32[]{:S(2)}, u32[]{:S(2)}) collective-permute-start(bf16[2,768,384]{2,1,0:T(8,128)(2,1)S(1)} %pad_maximum_fusion.7), channel_id=1, source_target_pairs={{0,32},{32,64},{64,96},{96,0},{1,33},{33,65},{65,97},{97,1},{2,34}... | collective-permute-start | bytes 3538952 | tf_op jit(solution)/shard_map/ppermute | solution.py:176
  351.4 28.8 %collective-permute-start.25 = (bf16[2,768,384]{2,1,0:T(8,128)(2,1)S(1)}, bf16[2,768,384]{2,1,0:T(8,128)(2,1)S(1)}, u32[]{:S(2)}, u32[]{:S(2)}) collective-permute-start(bf16[2,768,384]{2,1,0:T(8,128)(2,1)S(1)} %pad_maximum_fusion.8), channel_id=1, source_target_pairs={{0,96},{32,0},{64,32},{96,64},{1,97},{33,1},{65,33},{97,65},{2,98}... | collective-permute-start | bytes 3538952 | tf_op jit(solution)/shard_map/ppermute | solution.py:176
  354.8 28.9 %collective-permute-start.33 = (bf16[2,4,192,384]{3,2,1,0:T(8,128)(2,1)S(1)}, bf16[2,4,192,384]{3,2,1,0:T(8,128)(2,1)S(1)}, u32[]{:S(2)}, u32[]{:S(2)}) collective-permute-start(bf16[2,4,192,384]{3,2,1,0:T(8,128)(2,1)S(1)} %pad_maximum_fusion.10), channel_id=1, source_target_pairs={{0,24},{8,0},{16,8},{24,16},{1,25},{9,1},{17,9},{25,17},{2,26},{10... | collective-permute-start | bytes 3538952 | tf_op jit(solution)/shard_map/ppermute | solution.py:176
  370.4 15.5 %collective-permute-start.35 = (bf16[4,192,384]{2,1,0:T(8,128)(2,1)S(1)}, bf16[4,192,384]{2,1,0:T(8,128)(2,1)S(1)}, u32[]{:S(2)}, u32[]{:S(2)}) collective-permute-start(bf16[4,192,384]{2,1,0:T(8,128)(2,1)S(1)} %fusion.17), channel_id=1, source_target_pairs={{0,8},{8,16},{16,24},{24,0},{1,9},{9,17},{17,25},{25,1},{2,10},{10... | collective-permute-start | bytes 1769480 | tf_op jit(solution)/shard_map/ppermute | solution.py:176
  380.1 15.5 %collective-permute-start.27 = (bf16[768,384]{1,0:T(8,128)(2,1)S(1)}, bf16[768,384]{1,0:T(8,128)(2,1)S(1)}, u32[]{:S(2)}, u32[]{:S(2)}) collective-permute-start(bf16[768,384]{1,0:T(8,128)(2,1)S(1)} %fusion.21), channel_id=1, source_target_pairs={{0,32},{32,64},{64,96},{96,0},{1,33},{33,65},{65,97},{97,1},{2,34}... | collective-permute-start | bytes 1769480 | tf_op jit(solution)/shard_map/ppermute | solution.py:176
  380.4 15.2 %collective-permute-start.26 = (bf16[768,384]{1,0:T(8,128)(2,1)S(1)}, bf16[768,384]{1,0:T(8,128)(2,1)S(1)}, u32[]{:S(2)}, u32[]{:S(2)}) collective-permute-start(bf16[768,384]{1,0:T(8,128)(2,1)S(1)} %fusion.23), channel_id=1, source_target_pairs={{0,96},{32,0},{64,32},{96,64},{1,97},{33,1},{65,33},{97,65},{2,98}... | collective-permute-start | bytes 1769480 | tf_op jit(solution)/shard_map/ppermute | solution.py:176
  386.3 16.8 %collective-permute-start.34 = (bf16[4,192,384]{2,1,0:T(8,128)(2,1)S(1)}, bf16[4,192,384]{2,1,0:T(8,128)(2,1)S(1)}, u32[]{:S(2)}, u32[]{:S(2)}) collective-permute-start(bf16[4,192,384]{2,1,0:T(8,128)(2,1)S(1)} %get-tuple-element.41), channel_id=1, source_target_pairs={{0,24},{8,0},{16,8},{24,16},{1,25},{9,1},{17,9},{25,17},{2,26},{10... | collective-permute-start | bytes 1769480 | tf_op jit(solution)/shard_map/ppermute | solution.py:176
  396.2 17.0 %collective-permute-start.29 = (bf16[192,768]{1,0:T(8,128)(2,1)S(1)}, bf16[192,768]{1,0:T(8,128)(2,1)S(1)}, u32[]{:S(2)}, u32[]{:S(2)}) collective-permute-start(bf16[192,768]{1,0:T(8,128)(2,1)S(1)} %get-tuple-element.72), channel_id=1, source_target_pairs={{0,16},{8,24},{16,0},{24,8},{1,17},{9,25},{17,1},{25,9},{2,18},{10... | collective-permute-start | bytes 884744 | tf_op jit(solution)/shard_map/ppermute | solution.py:176
  449.5 32.2 %collective-permute-start.44 = (bf16[768,768]{1,0:T(8,128)(2,1)S(1)}, bf16[768,768]{1,0:T(8,128)(2,1)S(1)}, u32[]{:S(2)}, u32[]{:S(2)}) collective-permute-start(bf16[768,768]{1,0:T(8,128)(2,1)S(1)} %constant_dynamic-update-slice_fusion.15), channel_id=1, source_target_pairs={{0,32},{32,64},{64,96},{96,0},{1,33},{33,65},{65,97},{97,1},{2,34}... | collective-permute-start | bytes 3538952 | tf_op jit(solution)/shard_map/ppermute | solution.py:176
  449.6 28.4 %collective-permute-start.45 = (bf16[768,768]{1,0:T(8,128)(2,1)S(1)}, bf16[768,768]{1,0:T(8,128)(2,1)S(1)}, u32[]{:S(2)}, u32[]{:S(2)}) collective-permute-start(bf16[768,768]{1,0:T(8,128)(2,1)S(1)} %constant_dynamic-update-slice_fusion.15), channel_id=1, source_target_pairs={{0,96},{32,0},{64,32},{96,64},{1,97},{33,1},{65,33},{97,65},{2,98}... | collective-permute-start | bytes 3538952 | tf_op jit(solution)/shard_map/ppermute | solution.py:176
  478.0 15.8 %collective-permute-start.47 = (bf16[384,768]{1,0:T(8,128)(2,1)S(1)}, bf16[384,768]{1,0:T(8,128)(2,1)S(1)}, u32[]{:S(2)}, u32[]{:S(2)}) collective-permute-start(bf16[384,768]{1,0:T(8,128)(2,1)S(1)} %slice.445), channel_id=1, source_target_pairs={{0,96},{32,0},{64,32},{96,64},{1,97},{33,1},{65,33},{97,65},{2,98}... | collective-permute-start | bytes 1769480 | tf_op jit(solution)/shard_map/ppermute | solution.py:176
  481.8 15.1 %collective-permute-start.46 = (bf16[384,768]{1,0:T(8,128)(2,1)S(1)}, bf16[384,768]{1,0:T(8,128)(2,1)S(1)}, u32[]{:S(2)}, u32[]{:S(2)}) collective-permute-start(bf16[384,768]{1,0:T(8,128)(2,1)S(1)} %slice.444), channel_id=1, source_target_pairs={{0,32},{32,64},{64,96},{96,0},{1,33},{33,65},{65,97},{97,1},{2,34}... | collective-permute-start | bytes 1769480 | tf_op jit(solution)/shard_map/ppermute | solution.py:176
  (106 other events, 1144.9 us)
